TPU v7x, 256 devices: a whole 4x4x8 slice. The times are simulated.
256 devices in a mesh: section: 4 (over y), seq: 16 (over z_lo, x, core), head: 4 (over z_hi).
Axes of the slice: x: 4, y: 4, z: 8 (z_hi: 4, z_lo: 2; z = z_hi * 2 + z_lo), core: 2. Of those that a mesh axis runs over, the one named last changes fastest.
Arguments:
- encoder_states: bfloat16 [4, 2048, 4096], P(None, 'seq'), may hold values from -6 to 6
- w_kv: bfloat16 [4, 4096, 4096], P(None, None, ('section', 'head')), may hold values from -0.125 to 0.125
- queries: bfloat16 [4, 4, 256, 4, 512], P('section', None, None, None, 'head'), may hold values from -102 to 102
- cotangent: bfloat16 [4, 4, 256, 4, 512], P('section', None, None, None, 'head'), may hold values from -6 to 6
- src_len: int32 [4], replicated, may hold values from 512 to 2048, as said below
- tgt_len: int32 [4], replicated, may hold values from 64 to 256, as said below
Outputs:
- attn_out: bfloat16 [4, 4, 256, 4, 512], P('section', None, 'seq', None, 'head')
- query_grads: bfloat16 [4, 4, 256, 4, 512], P('section', None, 'seq', None, 'head')
- source_grads: bfloat16 [4, 2048, 4096], P(None, 'seq', ('section', 'head'))
Inputs may be any that keep to these rules, and one draw needn't show every extreme that they name: `src_len`: at least one sample has all 2048 source tokens. `tgt_len`: at least one sample has all 256 target tokens.
All inputs are finite; a program needn't handle non-finite values.
Results may differ from a plain program's by a relative error of at most 0.014.
The roundings to bfloat16 on the way count: a program that leaves them out, or rounds other values in their place, can miss the bound.
Values may be sent and summed in bfloat16 or wider, within the bound.
No kernel may reach another device: no remote copies, remote signals or barrier semaphores. Data moves between devices by JAX's collectives and lax.ppermute only.
A program may use at most 128 MiB of HBM per device.

v0:
```python
import jax
import jax.numpy as jnp
from jax import lax
from jax.sharding import PartitionSpec as P

masked_score = -1e30


def body(encoder_states, w_kv, queries, cotangent, src_len, tgt_len):
    sections = lax.axis_size("section")
    shards = lax.axis_size("seq")
    seat = lax.axis_index("seq")
    samples = encoder_states.shape[0]
    src_rows = encoder_states.shape[1]
    model_width = encoder_states.shape[2]
    layers = w_kv.shape[0]
    pair_cols = w_kv.shape[2]
    head_dim = pair_cols // 2
    piece_len = src_rows // shards
    groups = queries.shape[3]
    target_rows = queries.shape[2]
    out_rows = target_rows // shards
    key_count = shards * piece_len
    score_scale = head_dim ** (-0.5)
    local_source = encoder_states.reshape(samples, shards, piece_len, model_width)
    projected = jnp.einsum(
        "bqpd,ldc->lqbpc", local_source, w_kv, preferred_element_type=jnp.float32
    ).astype(jnp.bfloat16)
    moved = lax.all_to_all(
        projected.reshape(layers * shards, samples, piece_len, pair_cols),
        ("section", "seq"),
        split_axis=0,
        concat_axis=0,
        tiled=True,
    )
    moved = moved.reshape(sections, shards, samples, piece_len, pair_cols)
    key_rows = moved[..., :head_dim]
    value_rows = moved[..., head_dim:]
    query_now = queries[0]
    scores = jnp.einsum(
        "btgd,gqbpd->gbtqp", query_now, key_rows, preferred_element_type=jnp.float32
    )
    scores = scores.reshape(groups, samples, target_rows, key_count) * score_scale
    position = (
        jnp.arange(shards, dtype=jnp.int32)[:, None] * src_rows
        + seat * piece_len
        + jnp.arange(piece_len, dtype=jnp.int32)[None, :]
    )
    position = position.reshape(key_count)
    key_live = position[None, :] < src_len[:, None]
    scores = jnp.where(key_live[None, :, None, :], scores, masked_score)
    row_top = lax.pmax(jnp.max(scores, axis=-1), "seq")
    exponent = jnp.exp(scores - row_top[..., None])
    row_total = lax.psum(jnp.sum(exponent, axis=-1), "seq")
    probability = exponent / row_total[..., None]
    probability_low = probability.astype(jnp.bfloat16)
    blocks_low = probability_low.reshape(groups, samples, target_rows, shards, piece_len)
    part_out = jnp.einsum(
        "gbtqp,gqbpd->btgd", blocks_low, value_rows, preferred_element_type=jnp.float32
    )
    query_live = jnp.arange(target_rows, dtype=jnp.int32)[None, :] < tgt_len[:, None]
    grad_low = jnp.where(query_live[:, :, None, None], cotangent[0], jnp.zeros((), jnp.bfloat16))
    grad_probs = jnp.einsum(
        "btgd,gqbpd->gbtqp", grad_low, value_rows, preferred_element_type=jnp.float32
    )
    grad_probs = grad_probs.reshape(groups, samples, target_rows, key_count)
    full_out = lax.psum(part_out, "seq")
    row_delta = jnp.transpose(jnp.sum(grad_low.astype(jnp.float32) * full_out, axis=-1), (2, 0, 1))
    own_out = lax.dynamic_slice_in_dim(full_out, seat * out_rows, out_rows, 1)
    grad_scores = (probability * (grad_probs - row_delta[..., None])).astype(jnp.bfloat16)
    grad_scores = grad_scores.reshape(groups, samples, target_rows, shards, piece_len)
    part_query = score_scale * jnp.einsum(
        "gbtqp,gqbpd->btgd", grad_scores, key_rows, preferred_element_type=jnp.float32
    )
    own_query = lax.psum_scatter(part_query, "seq", scatter_dimension=1, tiled=True)
    grad_keys = score_scale * jnp.einsum(
        "gbtqp,btgd->gqbpd", grad_scores, query_now, preferred_element_type=jnp.float32
    )
    grad_values = jnp.einsum(
        "gbtqp,btgd->gqbpd", blocks_low, grad_low, preferred_element_type=jnp.float32
    )
    grad_pairs = jnp.concatenate([grad_keys, grad_values], axis=-1).astype(jnp.bfloat16)
    returned = lax.all_to_all(
        grad_pairs.reshape(sections * shards, samples, piece_len, pair_cols),
        ("section", "seq"),
        split_axis=0,
        concat_axis=0,
        tiled=True,
    )
    returned = returned.reshape(layers, shards, samples, piece_len, pair_cols)
    source_terms = jnp.einsum("lqbpc,ldc->bqpd", returned, w_kv, preferred_element_type=jnp.float32)
    source_terms = source_terms.reshape(samples, src_rows, model_width)
    source_part = lax.psum_scatter(
        source_terms, ("section", "head"), scatter_dimension=2, tiled=True
    )
    return (
        own_out.astype(jnp.bfloat16)[None],
        own_query.astype(jnp.bfloat16)[None],
        source_part.astype(jnp.bfloat16),
    )


def solution(mesh):
    placed = (
        P(None, "seq", None),
        P(None, None, ("section", "head")),
        P("section", None, None, None, "head"),
        P("section", None, None, None, "head"),
        P(),
        P(),
    )
    return jax.shard_map(
        body,
        mesh=mesh,
        in_specs=placed,
        out_specs=(
            P("section", None, "seq", None, "head"),
            P("section", None, "seq", None, "head"),
            P(None, "seq", ("section", "head")),
        ),
        check_vma=False,
    )
```

profile of v0, /device:TPU:56, one launch (start us, length us, event | category | flops | bytes accessed | tf_op | source)
XLA Modules:
  0.0 466.0 jit_solution(6176860153098522731)
XLA Ops:
  7.2 0.0 copy-start
  7.2 9.3 %fusion.15 = bf16[4,16,4,8,256]{4,1,3,2,0:T(8,128)(2,1)S(1)} fusion(bf16[4,16,8,4096]{3,2,1,0:T(8,128)(2,1)} %bitcast.99, bf16[4,4096,256]{2,1,0:T(8,128)(2,1)} %param.7), kind=kOutput, calls=%fused_computation.20 | convolution fusion | flops 4295491584 | bytes 13631488 | tf_op jit(solution)/shard_map/bqpd,ldc->lqbpc/dot_general | solution.py:26
  16.5 0.0 copy-start.8
  16.5 1.4 copy.46
  17.8 8.9 %all-to-all-start = ((bf16[64,4,8,256]{3,2,1,0:T(8,128)(2,1)}), bf16[64,4,8,256]{3,2,1,0:T(8,128)(2,1)S(1)}, u32[]{:S(2)}, u32[]{:S(2)}) async-start(bf16[64,4,8,256]{3,2,1,0:T(8,128)(2,1)} %bitcast.5), calls=%async_computation | async-start | bytes 2097152 | tf_op jit(solution)/shard_map/all_to_all | solution.py:29
  26.7 0.0 all-reduce.4.cloned.1.call-start
  26.8 0.1 iota_add_fusion
  26.9 0.1 broadcast_compare_fusion
  26.9 14.8 %all-to-all-done = bf16[64,4,8,256]{3,2,1,0:T(8,128)(2,1)S(1)} async-done(((bf16[64,4,8,256]{3,2,1,0:T(8,128)(2,1)}), bf16[64,4,8,256]{3,2,1,0:T(8,128)(2,1)S(1)}, u32[]{:S(2)}, u32[]{:S(2)}) %all-to-all-start) | async-done | bytes 1048608 | tf_op jit(solution)/shard_map/all_to_all | solution.py:29
  41.7 1.0 fusion.39
  42.7 0.0 copy-done
  42.7 0.8 copy-done.4
  43.5 0.6 bitcast_reduce_fusion
  44.1 54.0 %pmax.7 = f32[4,4,256]{2,1,0:T(4,128)S(1)} all-reduce(f32[4,4,256]{2,1,0:T(4,128)S(1)} %get-tuple-element.14), channel_id=1, replica_groups=mesh['section'=4,'seq'=16,'head'=4] {'seq'}, use_global_device_ids=true, to_apply=%region_1.2 | all-reduce | flops 4096 | bytes 32768 | tf_op jit(solution)/shard_map/pmax | solution.py:52
  98.1 0.6 fusion.9
  98.7 52.9 %psum.14 = f32[4,4,256]{2,1,0:T(4,128)S(1)} all-reduce(f32[4,4,256]{2,1,0:T(4,128)S(1)} %fusion.9), channel_id=1, replica_groups=mesh['section'=4,'seq'=16,'head'=4] {'seq'}, use_global_device_ids=true, to_apply=%region_3.4 | all-reduce | flops 4096 | bytes 32768 | tf_op jit(solution)/shard_map/psum | solution.py:54
  151.6 0.6 fusion.37
  152.2 0.0 copy-start.1
  152.2 1.0 copy-done.1
  153.2 1.9 convolution_bitcast_fusion
  155.1 0.0 all-reduce.4.cloned.1.call-update
  155.1 0.0 reduce-scatter.2.cloned.1.call-start
  155.2 2.3 copy.51
  157.5 0.1 iota_compare_fusion
  157.5 2.0 fusion.21
  159.5 0.9 copy.63
  160.5 122.0 %all-reduce.4.cloned.1.call-done = f32[4,256,4,128]{1,3,2,0:T(8,128)} async-done(((f32[4,256,4,128]{1,3,2,0:T(8,128)}), f32[4,256,4,128]{1,3,2,0:T(8,128)}) %all-reduce.4.cloned.1.call-update) | async-done | bytes 2097168 | tf_op jit(solution)/shard_map/psum | solution.py:67
  282.4 2.3 multiply_reduce_fusion
  284.7 0.0 copy-done.3
  284.8 0.9 multiply_convert_fusion
  285.7 0.5 fusion.22
  286.1 0.1 copy.60
  286.2 0.8 copy-done.7
  287.1 0.2 pad_maximum_fusion
  287.2 24.1 %all_to_all.10 = bf16[64,4,8,256]{3,2,1,0:T(8,128)(2,1)S(1)} all-to-all(bf16[64,4,8,256]{3,2,1,0:T(8,128)(2,1)S(1)} %pad_maximum_fusion), channel_id=1, replica_groups=mesh['section'=4,'seq'=16,'head'=4] {'section','seq'}, dimensions={0} | all-to-all | bytes 2097152 | tf_op jit(solution)/shard_map/all_to_all | solution.py:83
  311.4 7.0 %fusion = f32[16,4,8,4096,1]{3,2,1,0,4:T(8,128)S(1)} fusion(bf16[4,16,4,8,256]{4,3,2,1,0:T(8,128)(2,1)S(1)} %bitcast.97, bf16[4,4096,256]{2,1,0:T(8,128)(2,1)} %param.7), kind=kOutput, calls=%fused_computation | convolution fusion | flops 4294967296 | bytes 17825792 | tf_op jit(solution)/shard_map/lqbpc,ldc->bqpd/dot_general | solution.py:91
  318.4 3.8 copy.126
  322.1 0.0 reduce-scatter.2.cloned.1.call-update
  322.2 0.6 copy-done.10
  322.8 0.6 dynamic-slice
  324.0 1.4 fusion.32
  325.5 0.8 copy.65
  326.3 1.9 fusion.6
  328.2 2.0 copy.58
  330.2 113.9 %all-reduce.5 = bf16[4,256,4,128]{3,2,0,1:T(4,128)(2,1)S(1)} all-reduce(f32[4,256,4,128]{3,2,0,1:T(4,128)} %copy.58), channel_id=2, replica_groups=mesh['section'=4,'seq'=16,'head'=4] {'seq'}, use_global_device_ids=true, to_apply=%region_6.7.clone | all-reduce | flops 524288 | bytes 3145728
  444.1 0.7 copy.66
  444.8 12.6 %reduce-scatter.2.cloned.1.call-done = f32[4,128,256]{2,1,0:T(8,128)} async-done(((f32[4,128,4096]{2,1,0:T(8,128)}), f32[4,128,256]{2,1,0:T(8,128)}) %reduce-scatter.2.cloned.1.call-update) | async-done | bytes 524304 | tf_op jit(solution)/shard_map/reduce_scatter | solution.py:93
  457.4 1.8 convert_element_type.35
  (16 shorter events, 0.1 us)
Async XLA Ops:
  7.2 35.6 %copy-start = (bf16[1,4,256,4,128]{4,3,2,1,0:T(4,128)(2,1)S(1)}, bf16[1,4,256,4,128]{4,3,2,1,0:T(4,128)(2,1)}, u32[]{:S(2)}) copy-start(bf16[1,4,256,4,128]{4,3,2,1,0:T(4,128)(2,1)} %param.8) | copy-start | bytes 3145732
  16.5 10.4 %copy-start.8 = (s32[4]{0:T(128)S(1)}, s32[4]{0:T(128)}, u32[]{:S(2)}) copy-start(s32[4]{0:T(128)} %param.10) | copy-start | bytes 52
  17.8 23.9 %all-to-all-start = ((bf16[64,4,8,256]{3,2,1,0:T(8,128)(2,1)}), bf16[64,4,8,256]{3,2,1,0:T(8,128)(2,1)S(1)}, u32[]{:S(2)}, u32[]{:S(2)}) async-start(bf16[64,4,8,256]{3,2,1,0:T(8,128)(2,1)} %bitcast.5), calls=%async_computation | async-start | bytes 2097152 | tf_op jit(solution)/shard_map/all_to_all | solution.py:29
  26.7 255.7 %all-reduce.4.cloned.1.call-start = ((), (), s32[]{:S(2)}) async-start(), calls=%async_computation.3 | async-start | bytes 4194304 | tf_op jit(solution)/shard_map/psum | solution.py:67
  42.7 0.8 copy-start.4
  151.6 1.6 copy-start.5
  152.2 1.0 copy-start.1
  155.1 2.4 copy-start.9
  155.1 302.3 %reduce-scatter.2.cloned.1.call-start = ((), (), s32[]{:S(2)}) async-start(), calls=%async_computation.4 | async-start | bytes 8912896 | tf_op jit(solution)/shard_map/reduce_scatter | solution.py:93
  282.4 2.3 copy-start.3
  282.4 2.3 copy-start.6
  285.6 1.6 copy-start.2
  285.7 1.4 copy-start.7
  322.1 0.7 copy-start.10
Sparse Core Ops, SparseCore 0:
  155.2 127.1 all-reduce.3
  322.3 135.0 reduce-scatter.1
where the time goes:
time: 467 us; the launch traced here: 466 us
  blocking collectives  245 us (52%)
  waiting for transfers between devices  149 us (32%)
  matrix products  23.9 us (5%)
  local copies, waits for them, and re-layouts  18.3 us (4%)
  between operations  14.9 us (3%)
  starting transfers between devices  8.96 us (2%)
  other arithmetic  5.58 us (1%)
    psum x1, waiting for transfers between devices, body(): full_out = lax.psum(part_out, 'seq')  122 us
    unnamed x1, blocking collectives  114 us
    pmax x1, blocking collectives, body(): row_top = lax.pmax(jnp.max(scores, axis=-1), 'seq')  54 us
    psum x1, blocking collectives, body(): row_total = lax.psum(jnp.sum(exponent, axis=-1), 'seq')  52.9 us
    all_to_all x1, blocking collectives, body(): lax.all_to_all(grad_pairs.reshape(sections * shards, samples, piece_len,...  24.1 us
    all_to_all x1, waiting for transfers between devices, body(): lax.all_to_all(projected.reshape(layers * shards, samples, piece_len, pai...  14.8 us
    reduce_scatter x1, waiting for transfers between devices, body(): lax.psum_scatter(source_terms, ('section', 'head'), scatter_dimension=2,...  12.6 us
  transfers between devices with their start and end apart: 3, of which 3 were waited for; matrix products, arithmetic and copies ran while one was open for 3% of the time, Pallas kernels for 0%

commit v1 on v0

v1 whole, which is shorter than its diff:
```python
import functools

import jax
import jax.numpy as jnp
from jax import lax
from jax.experimental import pallas as pl
from jax.experimental.pallas import tpu as pltpu
from jax.sharding import PartitionSpec as P


masked_score = -1e30
NT = (((1,), (1,)), ((), ()))
NN = (((1,), (0,)), ((), ()))
TN = (((0,), (0,)), ((), ()))
CHUNKS = 2


def dot(a, b, dims):
    return lax.dot_general(a, b, dims, preferred_element_type=jnp.float32)


def low(a):
    return a.astype(jnp.bfloat16)


def wide(a):
    return a.astype(jnp.float32)


def bf(*shape):
    return jax.ShapeDtypeStruct(shape, jnp.bfloat16)


def kept_here(*shape, dtype=jnp.bfloat16):
    return pltpu.VMEM(shape, dtype)


def held(*arrays):
    return [pltpu.with_memory_space_constraint(a, pltpu.VMEM) for a in arrays]


def in_hbm(array):
    return pltpu.with_memory_space_constraint(array, pltpu.HBM)


ROOM = pltpu.CompilerParams(vmem_limit_bytes=16 * 1024 * 1024)
FAST = pl.BlockSpec(memory_space=pltpu.VMEM)
SLOW = pl.BlockSpec(memory_space=pl.ANY)
SCALAR = pl.BlockSpec(memory_space=pltpu.SMEM)


def project_kernel(x_ref, w_ref, out_ref):
    out_ref[pl.program_id(0)] = low(dot(x_ref[...], w_ref[0], NN))


def project(rows, w_kv):
    layers, width, cols = w_kv.shape
    count = rows.shape[0]
    return pl.pallas_call(
        project_kernel,
        out_shape=kept_here(layers, count, cols),
        grid=(layers,),
        in_specs=[
            pl.BlockSpec((count, width), lambda r: (0, 0)),
            pl.BlockSpec((1, width, cols), lambda r: (r, 0, 0)),
        ],
        out_specs=FAST,
        compiler_params=ROOM,
        name="project",
    )(in_hbm(rows), in_hbm(w_kv))


def forward_kernel(scalars, src_len, tgt_len, mine, mate, kv_ref, qc_ref, stat_ref):
    seat, core = scalars[0], scalars[1]
    layers, count, _ = kv_ref.shape
    _, _, samples, rows, head = qc_ref.shape
    shards = stat_ref.shape[0]
    keys = count // samples
    scale = head ** (-0.5)
    first = core == 0

    def one(b, carry):
        live = lax.broadcasted_iota(jnp.int32, (rows, head), 0) < tgt_len[b]
        key_live = seat * keys + lax.broadcasted_iota(jnp.int32, (keys, rows), 0) < src_len[b]
        tops, deltas = [], []
        for r in range(layers):
            whole = []
            for kind in range(2):
                a, c = wide(mine[r, kind, b]), wide(mate[r, kind, b])
                whole.append(jnp.concatenate([jnp.where(first, a, c), jnp.where(first, c, a)], axis=0))
            query, grad = low(whole[0]), low(jnp.where(live, whole[1], 0.0))
            qc_ref[0, r, b] = query
            qc_ref[1, r, b] = grad
            pair = kv_ref[r, pl.ds(pl.multiple_of(b * keys, keys), keys), :]
            scores = jnp.where(key_live, dot(pair[:, :head], query, NT) * scale, masked_score)
            top = jnp.max(scores, axis=0, keepdims=True)
            power = jnp.exp(scores - top)
            total = jnp.sum(power, axis=0, keepdims=True)
            part = jnp.sum(power * dot(pair[:, head:], grad, NT), axis=0, keepdims=True)
            tops.append(top + jnp.log(total))
            deltas.append(part / total)
        stats = jnp.concatenate(tops + deltas, axis=0)
        for peer in range(shards):
            stat_ref[peer, b] = stats
        return carry

    lax.fori_loop(0, samples, one, 0)


def forward(shards, scalars, src_len, tgt_len, mine, mate, kv):
    layers, _, samples, half, head = mine.shape
    rows = 2 * half
    return pl.pallas_call(
        forward_kernel,
        out_shape=(
            kept_here(2, layers, samples, rows, head),
            kept_here(shards, samples, 2 * layers, rows, dtype=jnp.float32),
        ),
        in_specs=[SCALAR] * 3 + [FAST] * 3,
        out_specs=(FAST, FAST),
        compiler_params=ROOM,
        name="forward",
    )(scalars, src_len, tgt_len, *held(mine, mate, kv))


def terms_of(grads, w_ref, place, part):
    terms = None
    at = pl.ds(pl.multiple_of(place * part, part), part)
    for r in range(grads.shape[0]):
        term = dot(grads[r], w_ref[r, at, :], NT)
        terms = term if terms is None else terms + term
    return terms


def backward_kernel(scalars, src_len, kv_ref, qc_ref, stat_ref, w_hbm, keep_ref, give_ref, grads, w_ref, *rest):
    far_refs, w_sem = rest[:-1], rest[-1]
    take = pltpu.make_async_copy(w_hbm, w_ref, w_sem)
    take.start()
    layers, count, _ = kv_ref.shape
    _, _, samples, rows, head = qc_ref.shape
    shards = stat_ref.shape[0]
    keys = count // samples
    scale = head ** (-0.5)
    seat = scalars[0]
    even = scalars[1] == 0

    def one(b, carry):
        stat = stat_ref[:, b]
        lse = stat[:, :layers]
        top = jnp.max(lse, axis=0)
        weight = jnp.exp(lse - top[None])
        inverse = 1.0 / jnp.sum(weight, axis=0)
        delta = jnp.sum(weight * stat[:, layers:], axis=0) * inverse
        down_live = seat * keys + lax.broadcasted_iota(jnp.int32, (keys, rows), 0) < src_len[b]
        at = pl.ds(pl.multiple_of(b * keys, keys), keys)
        for r in range(layers):
            pair = kv_ref[r, at, :]
            key, value = pair[:, :head], pair[:, head:]
            query, grad = qc_ref[0, r, b], qc_ref[1, r, b]
            scores = jnp.where(down_live, dot(key, query, NT) * scale, masked_score)
            prob = jnp.exp(scores - top[r:r + 1, :]) * inverse[r:r + 1, :]
            slope = low(prob * (dot(value, grad, NT) - delta[r:r + 1, :]))
            prob = low(prob)
            grads[r, at, :head] = low(dot(slope, query, NN) * scale)
            grads[r, at, head:] = low(dot(prob, grad, NN))
            for kind, out in enumerate((dot(prob, value, TN), dot(slope, key, TN) * scale)):
                out = out.reshape(shards // 2, 2, rows // shards, head)
                keep_ref[:, kind, r, b] = low(jnp.where(even, out[:, 0], out[:, 1]))
                give_ref[:, kind, r, b] = low(jnp.where(even, out[:, 1], out[:, 0]))
        return carry

    lax.fori_loop(0, samples, one, 0)
    take.wait()
    terms = low(terms_of(grads, w_ref, scalars[4], w_ref.shape[1] // 4))
    size = far_refs[0].shape[0]
    for k, ref in enumerate(far_refs):
        ref[...] = terms[k * size:(k + 1) * size]


def backward(scalars, src_len, kv, qc, stats, weights):
    _, layers, samples, rows, head = qc.shape
    shards = stats.shape[0]
    part = weights.shape[1] // 4
    half = kept_here(shards // 2, 2, layers, samples, rows // shards, head)
    far = kept_here(kv.shape[1] // (2 * CHUNKS), part)
    outs = (half, half, kept_here(*kv.shape), kept_here(*weights.shape)) + (far,) * (2 * CHUNKS)
    return pl.pallas_call(
        backward_kernel,
        out_shape=outs,
        in_specs=[SCALAR] * 2 + [FAST] * 3 + [SLOW],
        out_specs=(FAST,) * len(outs),
        scratch_shapes=[pltpu.SemaphoreType.DMA],
        compiler_params=ROOM,
        name="backward",
    )(scalars, src_len, *held(kv, qc, stats), in_hbm(weights))


def near_kernel(scalars, grads, w_ref, *outs):
    size = outs[0].shape[0]
    for side in range(2):
        terms = low(terms_of(grads, w_ref, scalars[5 + side], w_ref.shape[1] // 4))
        for k in range(CHUNKS):
            outs[side * CHUNKS + k][...] = terms[k * size:(k + 1) * size]


def near(scalars, grads, weights):
    outs = (kept_here(grads.shape[1] // CHUNKS, weights.shape[1] // 4),) * (2 * CHUNKS)
    return pl.pallas_call(
        near_kernel, out_shape=outs, in_specs=[SCALAR, FAST, FAST], out_specs=(FAST,) * len(outs), compiler_params=ROOM, name="near"
    )(scalars, *held(grads, weights))


def here_kernel(scalars, grads, w_ref, out_ref):
    out_ref[...] = low(terms_of(grads, w_ref, scalars[7], w_ref.shape[1] // 4))


def here(scalars, grads, weights):
    return pl.pallas_call(
        here_kernel,
        out_shape=kept_here(grads.shape[1], weights.shape[1] // 4),
        in_specs=[SCALAR, FAST, FAST],
        out_specs=FAST,
        compiler_params=ROOM,
        name="here",
    )(scalars, *held(grads, weights))


def halve_kernel(side, kept, came, keep_ref, give_ref):
    count = keep_ref.shape[0]
    mine = pl.ds(side[0] * count, count)
    other = pl.ds((1 - side[0]) * count, count)
    keep_ref[...] = low(wide(kept[mine]) + wide(came[mine]))
    give_ref[...] = low(wide(kept[other]) + wide(came[other]))


def halve(side, kept, came):
    out = kept_here(kept.shape[0] // 2, *kept.shape[1:])
    return pl.pallas_call(
        halve_kernel, out_shape=(out, out), in_specs=[SCALAR, FAST, FAST], out_specs=(FAST, FAST), compiler_params=ROOM
    )(side.reshape(1), *held(kept, came))


def deal_kernel(scalars, kept, came, *outs):
    for k, ref in enumerate(outs):
        layer = lax.rem(scalars[2] + k, len(outs))
        ref[...] = low(wide(kept[0, :, layer]) + wide(came[0, :, layer]))


def deal(scalars, kept, came):
    _, kinds, layers, samples, rows, head = kept.shape
    outs = (kept_here(kinds, samples, rows, head),) * layers
    return pl.pallas_call(
        deal_kernel, out_shape=outs, in_specs=[SCALAR, FAST, FAST], out_specs=(FAST,) * layers, compiler_params=ROOM, name="deal"
    )(scalars, *held(kept, came))


def pass_kernel(up_in, down_in, from_down, from_up, up_ref, down_ref):
    half = from_down.shape[0]
    up_ref[:half] = low(wide(up_in[:half]) + wide(from_down[...]))
    down_ref[half:] = low(wide(down_in[half:]) + wide(from_up[...]))
    up_ref[half:] = up_in[half:]
    down_ref[:half] = down_in[:half]


def pass_on(up_in, down_in, from_down, from_up):
    out = kept_here(*up_in.shape)
    return pl.pallas_call(
        pass_kernel, out_shape=(out, out), in_specs=[FAST] * 4, out_specs=(FAST, FAST), compiler_params=ROOM
    )(*held(up_in, down_in, from_down, from_up))


def gather_kernel(chunk, own, from_down, from_up, out_ref):
    heads, count, part = out_ref.shape
    for h in range(heads):
        at = slice(h * part, (h + 1) * part)
        mine = own[chunk * count:(chunk + 1) * count, at]
        out_ref[h] = low(wide(mine) + wide(from_down[:, at]) + wide(from_up[:, at]))


def gather(own, from_down, from_up, heads, chunk):
    count, width = from_down.shape
    return pl.pallas_call(
        functools.partial(gather_kernel, chunk),
        out_shape=kept_here(heads, count, width // heads),
        in_specs=[FAST] * 3,
        out_specs=FAST,
        compiler_params=ROOM,
    )(*held(own, from_down, from_up))


def finish_kernel(*refs):
    out_ref = refs[-1]
    count = out_ref.shape[0] // (len(refs) - 1)
    for c, ref in enumerate(refs[:-1]):
        total = wide(ref[0])
        for h in range(1, ref.shape[0]):
            total = total + wide(ref[h])
        out_ref[c * count:(c + 1) * count] = low(total)


def finish(pieces):
    _, count, part = pieces[0].shape
    return pl.pallas_call(
        finish_kernel,
        out_shape=bf(count * len(pieces), part),
        in_specs=[FAST] * len(pieces),
        out_specs=FAST,
        compiler_params=ROOM,
        name="finish",
    )(*held(*pieces))


def turn(count, by):
    return [(i, (i + by) % count) for i in range(count)]


def flip(count, bit):
    return [(i, i ^ bit) for i in range(count)]


def body(encoder_states, w_kv, queries, cotangent, src_len, tgt_len):
    sec = lax.axis_index("section")
    seat = lax.axis_index("seq")
    shards = lax.axis_size("seq")
    samples, src_rows, width = encoder_states.shape
    _, _, cols = w_kv.shape
    rows = queries.shape[2]
    half = rows // 2
    core = seat % 2
    places = [(sec + by) % 4 for by in (2, 1, 3, 0)]
    bits = [(seat // (1 << k)) % 2 for k in range(4)]
    scalars = jnp.stack([seat, core, sec, sec, *places, *bits]).astype(jnp.int32)

    def up(a):
        return lax.ppermute(a, "section", turn(4, 1))

    def down(a):
        return lax.ppermute(a, "section", turn(4, 3))

    def swap(a, axis):
        return lax.all_to_all(a, axis, 0, 0, tiled=True)

    halves = [
        jnp.transpose(lax.dynamic_slice_in_dim(a[0], core * half, half, 1), (2, 0, 1, 3)) for a in (queries, cotangent)
    ]
    mine = swap(jnp.stack(halves, 1), "section")
    kv = project(encoder_states.reshape(samples * src_rows, width), w_kv)
    mine, kv = lax.optimization_barrier((mine, kv))
    mate = lax.ppermute(mine, "seq", flip(shards, 1))
    qc, stats = forward(shards, scalars, src_len, tgt_len, mine, mate, kv)
    stats = swap(stats, "seq")

    heads = lax.axis_size("head")
    kept, give, grads, weights, *far = backward(scalars, src_len, kv, qc, stats, w_kv)
    passed = [(up(far[2 * c]), down(far[2 * c + 1])) for c in range(CHUNKS)]
    sides = near(scalars, grads, weights)
    own = here(scalars, grads, weights)
    pieces = []
    for c in range(CHUNKS):
        to_up, to_down = pass_on(sides[c], sides[CHUNKS + c], *passed[c])
        to_up, to_down = up(to_up), down(to_down)
        joined = gather(own, to_up, to_down, heads, c)
        pieces.append(swap(joined, "head"))
    source_grads = finish(pieces).reshape(samples, src_rows, cols)

    for stage, bit in enumerate((0, 3, 2, 1)):
        if stage:
            kept, give = halve(bits[bit].astype(jnp.int32), kept, came)
        came = lax.ppermute(give, "seq", flip(shards, 1 << bit))
    own, to_up, to_far, to_down = deal(scalars, kept, came)
    from_down, from_up = up(to_up), down(to_down)
    from_far = lax.ppermute(to_far, "section", turn(4, 2))
    ring = jnp.stack([own, from_down, from_far, from_up])
    groups = [lax.dynamic_index_in_dim(ring, (sec + 4 - g) % 4, 0, keepdims=False) for g in range(4)]
    od = jnp.stack(groups, axis=3)
    return od[0][None], od[1][None], source_grads


def solution(mesh):
    placed = (
        P(None, "seq", None),
        P(None, None, ("section", "head")),
        P("section", None, None, None, "head"),
        P("section", None, None, None, "head"),
        P(),
        P(),
    )

    return jax.shard_map(
        body,
        mesh=mesh,
        in_specs=placed,
        out_specs=(
            P("section", None, "seq", None, "head"),
            P("section", None, "seq", None, "head"),
            P(None, "seq", ("section", "head")),
        ),
        check_vma=False,
    )
```

time: 467 us -> 136 us (0.29)
  the two profiles are of different devices: /device:TPU:56 before, /device:TPU:64 now
where the time goes in v1:
time: 136 us
  waiting for transfers between devices  42.1 us (31%)
  starting transfers between devices  41.5 us (31%)
  Pallas kernels  29.5 us (22%)
  blocking collectives  16.4 us (12%)
  local copies, waits for them, and re-layouts  4.3 us (3%)
    all_to_all x3, starting transfers between devices, swap(): return lax.all_to_all(a, axis, 0, 0, tiled=True)  19 us
    ppermute x4, waiting for transfers between devices, body(): came = lax.ppermute(give, 'seq', flip(shards, 1 << bit))  16.9 us
    all_to_all x1, blocking collectives, swap(): return lax.all_to_all(a, axis, 0, 0, tiled=True)  16.4 us
    ppermute x5, waiting for transfers between devices, up(): return lax.ppermute(a, 'section', turn(4, 1))  13.7 us
    ppermute x5, starting transfers between devices, down(): return lax.ppermute(a, 'section', turn(4, 3))  12.3 us
    pallas_call x1, Pallas kernels, project(): pl.pallas_call(project_kernel, out_shape=kept_here(layers, count, cols),...  8.29 us
    pallas_call x1, Pallas kernels, backward(): pl.pallas_call(backward_kernel, out_shape=outs, in_specs=[SCALAR] * 2 + [...  7.34 us
    all_to_all x3, waiting for transfers between devices, swap(): return lax.all_to_all(a, axis, 0, 0, tiled=True)  6.81 us
  transfers between devices with their start and end apart: 19, of which 10 were waited for; matrix products, arithmetic and copies ran while one was open for 0% of the time, Pallas kernels for 15%

profile of v1, /device:TPU:64, one launch (start us, length us, event | category | flops | bytes accessed | tf_op | source)
XLA Modules:
  0.0 135.7 jit_solution(14064826764181197529)
XLA Ops:
  0.6 1.6 %constant_dynamic-slice_fusion = (bf16[1,4,128,4,128]{4,3,2,1,0:T(4,128)(2,1)S(1)}, bf16[1,4,128,4,128]{4,3,2,1,0:T(4,128)(2,1)S(1)}) fusion(bf16[1,4,256,4,128]{4,3,2,1,0:T(4,128)(2,1)} %param.9, s32[]{:T(128)S(6)} %select_n.86, bf16[1,4,256,4,128]{4,3,2,1,0:T(4,128)(2,1)} %param.8), kind=kLoop, calls=%fused_computation.9 | loop fusion | bytes 2097156 | tf_op jit(solution)/shard_map/dynamic_slice | solution.py:344
  2.2 0.1 copy.17
  2.3 0.1 copy.18
  2.4 1.1 pad_maximum_fusion
  3.5 4.6 %all-to-all-start = ((bf16[4,2,4,128,128]{4,3,2,1,0:T(8,128)(2,1)}), bf16[4,2,4,128,128]{4,3,2,1,0:T(8,128)(2,1)S(1)}, u32[]{:S(2)}, u32[]{:S(2)}) async-start(bf16[4,2,4,128,128]{4,3,2,1,0:T(8,128)(2,1)} %pad_maximum_fusion), calls=%async_computation | async-start | bytes 2097152 | tf_op jit(solution)/shard_map/all_to_all | solution.py:341
  8.1 8.3 %project.1.kv_ref = bf16[4,512,256]{2,1,0:T(8,128)(2,1)S(1)} custom-call(bf16[512,4096]{1,0:T(8,128)(2,1)} %bitcast.39, bf16[4,4096,256]{2,1,0:T(8,128)(2,1)} %w_hbm.1), custom_call_target="tpu_custom_call" | custom-call | tf_op jit(solution)/shard_map/project/pallas_call | solution.py:59
  16.4 6.8 %all-to-all-done.mine = bf16[4,2,4,128,128]{4,3,2,1,0:T(8,128)(2,1)S(1)} async-done(((bf16[4,2,4,128,128]{4,3,2,1,0:T(8,128)(2,1)}), bf16[4,2,4,128,128]{4,3,2,1,0:T(8,128)(2,1)S(1)}, u32[]{:S(2)}, u32[]{:S(2)}) %all-to-all-start) | async-done | bytes 1048608 | tf_op jit(solution)/shard_map/all_to_all | solution.py:341
  23.2 0.1 stack.84.scalars
  23.3 2.6 %collective-permute-done.mate = bf16[4,2,4,128,128]{4,3,2,1,0:T(8,128)(2,1)S(1)} collective-permute-done((bf16[4,2,4,128,128]{4,3,2,1,0:T(8,128)(2,1)S(1)}, bf16[4,2,4,128,128]{4,3,2,1,0:T(8,128)(2,1)S(1)}, u32[]{:S(2)}, u32[]{:S(2)}) %collective-permute-start) | collective-permute-done | bytes 1048608 | tf_op jit(solution)/shard_map/ppermute | solution.py:349
  25.9 2.2 %forward.1 = (bf16[2,4,4,256,128]{4,3,2,1,0:T(8,128)(2,1)S(1)}, f32[16,4,8,256]{3,2,1,0:T(8,128)S(1)}) custom-call(s32[12]{0:T(128)S(1)} %stack.84.scalars, s32[4]{0:T(128)S(1)} %copy-done.2, s32[4]{0:T(128)S(1)} %copy-done.3, bf16[4,2,4,128,128]{4,3,2,1,0:T(8,128)(2,1)S(1)} %all-to-all-done.mine, ...), custom_call_target="tpu_custom_call" | custom-call | tf_op jit(solution)/shard_map/forward/pallas_call | solution.py:113
  28.1 16.4 %all_to_all.20.stat_ref = f32[16,4,8,256]{3,2,1,0:T(8,128)S(1)} all-to-all(f32[16,4,8,256]{3,2,1,0:T(8,128)S(1)} %get-tuple-element.36), channel_id=1, replica_groups=mesh['section'=4,'seq'=16,'head'=4] {'seq'}, dimensions={0} | all-to-all | bytes 1048576 | tf_op jit(solution)/shard_map/all_to_all | solution.py:341
  44.4 7.3 %backward.1 = (bf16[8,2,4,4,16,128]{5,4,3,2,1,0:T(8,128)(2,1)S(1)}, bf16[8,2,4,4,16,128]{5,4,3,2,1,0:T(8,128)(2,1)}, bf16[4,512,256]{2,1,0:T(8,128)(2,1)S(1)}, b...) custom-call(s32[12]{0:T(128)S(1)} %stack.84.scalars, ...), custom_call_target="tpu_custom_call" | custom-call | tf_op jit(solution)/shard_map/backward/pallas_call | solution.py:187
  51.8 0.6 collective-permute-start.12
  52.4 2.7 %collective-permute-start.13 = (bf16[128,1024]{1,0:T(8,128)(2,1)S(1)}, bf16[128,1024]{1,0:T(8,128)(2,1)S(1)}, u32[]{:S(2)}, u32[]{:S(2)}) collective-permute-start(bf16[128,1024]{1,0:T(8,128)(2,1)S(1)} %get-tuple-element.60), channel_id=1, source_target_pairs={{0,192},{64,0},{128,64},{192,128},{1,193},{65,1},{129,65},{193,129... | collective-permute-start | bytes 786440 | tf_op jit(solution)/shard_map/ppermute | solution.py:338
  55.1 2.9 %near.1 = (bf16[256,1024]{1,0:T(8,128)(2,1)S(1)}, bf16[256,1024]{1,0:T(8,128)(2,1)S(1)}, bf16[256,1024]{1,0:T(8,128)(2,1)S(1)}, bf16[256,1024]{1,0:T(8,128)(2,1)S(1)}) custom-call(s32[12]{0:T(128)S(1)} %stack.84.scalars, bf16[4,512,256]{2,1,0:T(8,128)(2,1)S(1)} %get-tuple-element.49.grads, bf16[4,4096,256]{2,1,0:T(8,128)(2,1)S(1)} %get-tuple-element.50.w_ref), custom_call_target="tpu_custom_call" | custom-call | tf_op jit(solution)/shard_map/near/pallas_call | solution.py:208
  58.0 2.5 %collective-permute-done.12.from_down = bf16[128,1024]{1,0:T(8,128)(2,1)S(1)} collective-permute-done((bf16[128,1024]{1,0:T(8,128)(2,1)S(1)}, bf16[128,1024]{1,0:T(8,128)(2,1)S(1)}, u32[]{:S(2)}, u32[]{:S(2)}) %collective-permute-start.12) | collective-permute-done | bytes 262176 | tf_op jit(solution)/shard_map/ppermute | solution.py:335
  60.5 0.1 shard_map.90
  60.7 0.1 collective-permute-start.14
  60.8 3.2 %collective-permute-start.15 = (bf16[256,1024]{1,0:T(8,128)(2,1)S(1)}, bf16[256,1024]{1,0:T(8,128)(2,1)S(1)}, u32[]{:S(2)}, u32[]{:S(2)}) collective-permute-start(bf16[256,1024]{1,0:T(8,128)(2,1)S(1)} %get-tuple-element.62), channel_id=1, source_target_pairs={{0,192},{64,0},{128,64},{192,128},{1,193},{65,1},{129,65},{193,129... | collective-permute-start | bytes 1572872 | tf_op jit(solution)/shard_map/ppermute | solution.py:338
  64.0 3.2 %collective-permute-start.9 = (bf16[128,1024]{1,0:T(8,128)(2,1)}, bf16[128,1024]{1,0:T(8,128)(2,1)}, u32[]{:S(2)}, u32[]{:S(2)}) collective-permute-start(bf16[128,1024]{1,0:T(8,128)(2,1)} %get-tuple-element.54), channel_id=1, source_target_pairs={{0,192},{64,0},{128,64},{192,128},{1,193},{65,1},{129,65},{193,129... | collective-permute-start | bytes 786440 | tf_op jit(solution)/shard_map/ppermute | solution.py:338
  67.2 1.8 %here.1.own = bf16[512,1024]{1,0:T(8,128)(2,1)S(1)} custom-call(s32[12]{0:T(128)S(1)} %stack.84.scalars, bf16[4,512,256]{2,1,0:T(8,128)(2,1)S(1)} %get-tuple-element.49.grads, bf16[4,4096,256]{2,1,0:T(8,128)(2,1)S(1)} %get-tuple-element.50.w_ref), custom_call_target="tpu_custom_call" | custom-call | tf_op jit(solution)/shard_map/here/pallas_call | solution.py:218
  69.1 7.7 %collective-permute-done.14.from_down = bf16[256,1024]{1,0:T(8,128)(2,1)S(1)} collective-permute-done((bf16[256,1024]{1,0:T(8,128)(2,1)S(1)}, bf16[256,1024]{1,0:T(8,128)(2,1)S(1)}, u32[]{:S(2)}, u32[]{:S(2)}) %collective-permute-start.14) | collective-permute-done | bytes 524320 | tf_op jit(solution)/shard_map/ppermute | solution.py:335
  76.8 1.0 shard_map.91
  77.8 7.2 %all-to-all-start.3 = ((bf16[4,256,256]{2,1,0:T(8,128)(2,1)}), bf16[4,256,256]{2,1,0:T(8,128)(2,1)S(1)}, u32[]{:S(2)}, u32[]{:S(2)}) async-start(bf16[4,256,256]{2,1,0:T(8,128)(2,1)} %shard_map.91), calls=%async_computation.3 | async-start | bytes 1048576 | tf_op jit(solution)/shard_map/all_to_all | solution.py:341
  85.0 1.0 copy-done.1
  86.0 1.1 shard_map.88
  87.1 1.2 collective-permute-start.10
  88.3 2.2 %collective-permute-start.11 = (bf16[256,1024]{1,0:T(8,128)(2,1)S(1)}, bf16[256,1024]{1,0:T(8,128)(2,1)S(1)}, u32[]{:S(2)}, u32[]{:S(2)}) collective-permute-start(bf16[256,1024]{1,0:T(8,128)(2,1)S(1)} %get-tuple-element.56), channel_id=1, source_target_pairs={{0,192},{64,0},{128,64},{192,128},{1,193},{65,1},{129,65},{193,129... | collective-permute-start | bytes 1572872 | tf_op jit(solution)/shard_map/ppermute | solution.py:338
  90.5 2.2 %shard_map.85 = (bf16[4,2,4,4,16,128]{5,4,3,2,1,0:T(8,128)(2,1)S(1)}, bf16[4,2,4,4,16,128]{5,4,3,2,1,0:T(8,128)(2,1)}) custom-call(s32[1]{0:T(128)} %bitcast.9.side, bf16[8,2,4,4,16,128]{5,4,3,2,1,0:T(8,128)(2,1)S(1)} %get-tuple-element.37.kept, bf16[8,2,4,4,16,128]{5,4,3,2,1,0:T(8,128)(2,1)} %collective-permute-done.1.came), custom_call_target="tpu_custom_call" | custom-call | tf_op jit(solution)/shard_map/pallas_call | solution.py:238
  92.7 1.5 %collective-permute-start.2 = (bf16[4,2,4,4,16,128]{5,4,3,2,1,0:T(8,128)(2,1)}, bf16[4,2,4,4,16,128]{5,4,3,2,1,0:T(8,128)(2,1)S(1)}, u32[]{:S(2)}, u32[]{:S(2)}) collective-permute-start(bf16[4,2,4,4,16,128]{5,4,3,2,1,0:T(8,128)(2,1)} %get-tuple-element.40), channel_id=1, source_target_pairs={{0,32},{4,36},{8,40},{12,44},{16,48},{20,52},{24,56},{28,60},{32,0... | collective-permute-start | bytes 1572872 | tf_op jit(solution)/shard_map/ppermute | solution.py:369
  94.1 3.5 %collective-permute-done.10.from_down = bf16[256,1024]{1,0:T(8,128)(2,1)S(1)} collective-permute-done((bf16[256,1024]{1,0:T(8,128)(2,1)S(1)}, bf16[256,1024]{1,0:T(8,128)(2,1)S(1)}, u32[]{:S(2)}, u32[]{:S(2)}) %collective-permute-start.10) | collective-permute-done | bytes 524320 | tf_op jit(solution)/shard_map/ppermute | solution.py:335
  97.6 1.0 shard_map.89
  98.6 7.2 %all-to-all-start.2 = ((bf16[4,256,256]{2,1,0:T(8,128)(2,1)}), bf16[4,256,256]{2,1,0:T(8,128)(2,1)S(1)}, u32[]{:S(2)}, u32[]{:S(2)}) async-start(bf16[4,256,256]{2,1,0:T(8,128)(2,1)} %shard_map.89), calls=%async_computation.2 | async-start | bytes 1048576 | tf_op jit(solution)/shard_map/all_to_all | solution.py:341
  105.8 4.0 %collective-permute-done.2.came = bf16[4,2,4,4,16,128]{5,4,3,2,1,0:T(8,128)(2,1)S(1)} collective-permute-done((bf16[4,2,4,4,16,128]{5,4,3,2,1,0:T(8,128)(2,1)}, bf16[4,2,4,4,16,128]{5,4,3,2,1,0:T(8,128)(2,1)S(1)}, u32[]{:S(2)}, u32[]{:S(2)}) %collective-permute-start.2) | collective-permute-done | bytes 524320 | tf_op jit(solution)/shard_map/ppermute | solution.py:369
  109.8 0.1 shard_map.86
  109.9 0.9 collective-permute-start.3
  110.8 7.9 %collective-permute-done.3.came = bf16[2,2,4,4,16,128]{5,4,3,2,1,0:T(8,128)(2,1)S(1)} collective-permute-done((bf16[2,2,4,4,16,128]{5,4,3,2,1,0:T(8,128)(2,1)S(1)}, bf16[2,2,4,4,16,128]{5,4,3,2,1,0:T(8,128)(2,1)S(1)}, u32[]{:S(2)}, u32[]{:S(2)}) %collective-permute-start.3) | collective-permute-done | bytes 262176 | tf_op jit(solution)/shard_map/ppermute | solution.py:369
  118.8 0.1 collective-permute-start.4
  118.9 5.0 %collective-permute-done.4.came = bf16[1,2,4,4,16,128]{5,4,3,2,1,0:T(8,128)(2,1)S(1)} collective-permute-done((bf16[1,2,4,4,16,128]{5,4,3,2,1,0:T(8,128)(2,1)S(1)}, bf16[1,2,4,4,16,128]{5,4,3,2,1,0:T(8,128)(2,1)S(1)}, u32[]{:S(2)}, u32[]{:S(2)}) %collective-permute-start.4) | collective-permute-done | bytes 131104 | tf_op jit(solution)/shard_map/ppermute | solution.py:369
  123.8 0.6 deal.1
  124.4 2.3 %collective-permute-start.5 = (bf16[2,4,16,128]{3,2,1,0:T(8,128)(2,1)S(1)}, bf16[2,4,16,128]{3,2,1,0:T(8,128)(2,1)S(1)}, u32[]{:S(2)}, u32[]{:S(2)}) collective-permute-start(bf16[2,4,16,128]{3,2,1,0:T(8,128)(2,1)S(1)} %get-tuple-element.46), channel_id=1, source_target_pairs={{0,64},{64,128},{128,192},{192,0},{1,65},{65,129},{129,193},{193,1... | collective-permute-start | bytes 98312 | tf_op jit(solution)/shard_map/ppermute | solution.py:335
  126.7 3.6 %collective-permute-start.6 = (bf16[2,4,16,128]{3,2,1,0:T(8,128)(2,1)S(1)}, bf16[2,4,16,128]{3,2,1,0:T(8,128)(2,1)S(1)}, u32[]{:S(2)}, u32[]{:S(2)}) collective-permute-start(bf16[2,4,16,128]{3,2,1,0:T(8,128)(2,1)S(1)} %get-tuple-element.47), channel_id=1, source_target_pairs={{0,128},{64,192},{128,0},{192,64},{1,129},{65,193},{129,1},{193,65... | collective-permute-start | bytes 98312 | tf_op jit(solution)/shard_map/ppermute | solution.py:372
  130.3 0.9 collective-permute-start.7
  131.2 0.8 finish.1
  132.1 0.5 collective-permute-done.6
  132.5 1.7 %collective-permute-done.7 = bf16[2,4,16,128]{3,2,1,0:T(8,128)(2,1)S(1)} collective-permute-done((bf16[2,4,16,128]{3,2,1,0:T(8,128)(2,1)S(1)}, bf16[2,4,16,128]{3,2,1,0:T(8,128)(2,1)S(1)}, u32[]{:S(2)}, u32[]{:S(2)}) %collective-permute-start.7) | collective-permute-done | bytes 32800 | tf_op jit(solution)/shard_map/ppermute | solution.py:338
  134.3 0.7 copy.14
  135.0 0.7 copy.13
  (24 shorter events, 0.2 us)
Async XLA Ops:
  3.5 22.4 %copy-start.2 = (s32[4]{0:T(128)S(1)}, s32[4]{0:T(128)}, u32[]{:S(2)}) copy-start(s32[4]{0:T(128)} %src_len.3) | copy-start | bytes 52
  3.5 22.4 %copy-start.3 = (s32[4]{0:T(128)S(1)}, s32[4]{0:T(128)}, u32[]{:S(2)}) copy-start(s32[4]{0:T(128)} %tgt_len.1) | copy-start | bytes 52
  3.5 19.7 %all-to-all-start = ((bf16[4,2,4,128,128]{4,3,2,1,0:T(8,128)(2,1)}), bf16[4,2,4,128,128]{4,3,2,1,0:T(8,128)(2,1)S(1)}, u32[]{:S(2)}, u32[]{:S(2)}) async-start(bf16[4,2,4,128,128]{4,3,2,1,0:T(8,128)(2,1)} %pad_maximum_fusion), calls=%async_computation | async-start | bytes 2097152 | tf_op jit(solution)/shard_map/all_to_all | solution.py:341
  23.2 2.7 %collective-permute-start = (bf16[4,2,4,128,128]{4,3,2,1,0:T(8,128)(2,1)S(1)}, bf16[4,2,4,128,128]{4,3,2,1,0:T(8,128)(2,1)S(1)}, u32[]{:S(2)}, u32[]{:S(2)}) collective-permute-start(bf16[4,2,4,128,128]{4,3,2,1,0:T(8,128)(2,1)S(1)} %all-to-all-done.mine), channel_id=1, source_target_pairs={{0,4},{4,0},{8,12},{12,8},{16,20},{20,16},{24,28},{28,24},{32,36},... | collective-permute-start | bytes 3145736 | tf_op jit(solution)/shard_map/ppermute | solution.py:349
  51.8 8.7 %collective-permute-start.12 = (bf16[128,1024]{1,0:T(8,128)(2,1)S(1)}, bf16[128,1024]{1,0:T(8,128)(2,1)S(1)}, u32[]{:S(2)}, u32[]{:S(2)}) collective-permute-start(bf16[128,1024]{1,0:T(8,128)(2,1)S(1)} %get-tuple-element.59), channel_id=1, source_target_pairs={{0,64},{64,128},{128,192},{192,0},{1,65},{65,129},{129,193},{193,1... | collective-permute-start | bytes 786440 | tf_op jit(solution)/shard_map/ppermute | solution.py:335
  52.4 8.1 %collective-permute-start.13 = (bf16[128,1024]{1,0:T(8,128)(2,1)S(1)}, bf16[128,1024]{1,0:T(8,128)(2,1)S(1)}, u32[]{:S(2)}, u32[]{:S(2)}) collective-permute-start(bf16[128,1024]{1,0:T(8,128)(2,1)S(1)} %get-tuple-element.60), channel_id=1, source_target_pairs={{0,192},{64,0},{128,64},{192,128},{1,193},{65,1},{129,65},{193,129... | collective-permute-start | bytes 786440 | tf_op jit(solution)/shard_map/ppermute | solution.py:338
  58.0 11.1 %copy-start = (bf16[256,1024]{1,0:T(8,128)(2,1)}, bf16[256,1024]{1,0:T(8,128)(2,1)S(1)}, u32[]{:S(2)}) copy-start(bf16[256,1024]{1,0:T(8,128)(2,1)S(1)} %get-tuple-element.52.down_in) | copy-start | bytes 1572868
  60.7 16.1 %collective-permute-start.14 = (bf16[256,1024]{1,0:T(8,128)(2,1)S(1)}, bf16[256,1024]{1,0:T(8,128)(2,1)S(1)}, u32[]{:S(2)}, u32[]{:S(2)}) collective-permute-start(bf16[256,1024]{1,0:T(8,128)(2,1)S(1)} %get-tuple-element.61), channel_id=1, source_target_pairs={{0,64},{64,128},{128,192},{192,0},{1,65},{65,129},{129,193},{193,1... | collective-permute-start | bytes 1572872 | tf_op jit(solution)/shard_map/ppermute | solution.py:335
  60.8 16.0 %collective-permute-start.15 = (bf16[256,1024]{1,0:T(8,128)(2,1)S(1)}, bf16[256,1024]{1,0:T(8,128)(2,1)S(1)}, u32[]{:S(2)}, u32[]{:S(2)}) collective-permute-start(bf16[256,1024]{1,0:T(8,128)(2,1)S(1)} %get-tuple-element.62), channel_id=1, source_target_pairs={{0,192},{64,0},{128,64},{192,128},{1,193},{65,1},{129,65},{193,129... | collective-permute-start | bytes 1572872 | tf_op jit(solution)/shard_map/ppermute | solution.py:338
  64.0 26.5 %collective-permute-start.1 = (bf16[8,2,4,4,16,128]{5,4,3,2,1,0:T(8,128)(2,1)}, bf16[8,2,4,4,16,128]{5,4,3,2,1,0:T(8,128)(2,1)}, u32[]{:S(2)}, u32[]{:S(2)}) collective-permute-start(bf16[8,2,4,4,16,128]{5,4,3,2,1,0:T(8,128)(2,1)} %get-tuple-element.38), channel_id=1, source_target_pairs={{0,4},{4,0},{8,12},{12,8},{16,20},{20,16},{24,28},{28,24},{32,36},... | collective-permute-start | bytes 3145736 | tf_op jit(solution)/shard_map/ppermute | solution.py:369
  64.0 21.0 %collective-permute-start.8 = (bf16[128,1024]{1,0:T(8,128)(2,1)}, bf16[128,1024]{1,0:T(8,128)(2,1)S(1)}, u32[]{:S(2)}, u32[]{:S(2)}) collective-permute-start(bf16[128,1024]{1,0:T(8,128)(2,1)} %get-tuple-element.53), channel_id=1, source_target_pairs={{0,64},{64,128},{128,192},{192,0},{1,65},{65,129},{129,193},{193,1... | collective-permute-start | bytes 786440 | tf_op jit(solution)/shard_map/ppermute | solution.py:335
  64.0 21.0 %collective-permute-start.9 = (bf16[128,1024]{1,0:T(8,128)(2,1)}, bf16[128,1024]{1,0:T(8,128)(2,1)}, u32[]{:S(2)}, u32[]{:S(2)}) collective-permute-start(bf16[128,1024]{1,0:T(8,128)(2,1)} %get-tuple-element.54), channel_id=1, source_target_pairs={{0,192},{64,0},{128,64},{192,128},{1,193},{65,1},{129,65},{193,129... | collective-permute-start | bytes 786440 | tf_op jit(solution)/shard_map/ppermute | solution.py:338
  77.8 20.8 %all-to-all-start.3 = ((bf16[4,256,256]{2,1,0:T(8,128)(2,1)}), bf16[4,256,256]{2,1,0:T(8,128)(2,1)S(1)}, u32[]{:S(2)}, u32[]{:S(2)}) async-start(bf16[4,256,256]{2,1,0:T(8,128)(2,1)} %shard_map.91), calls=%async_computation.3 | async-start | bytes 1048576 | tf_op jit(solution)/shard_map/all_to_all | solution.py:341
  85.0 1.0 copy-start.1
  87.1 10.5 %collective-permute-start.10 = (bf16[256,1024]{1,0:T(8,128)(2,1)S(1)}, bf16[256,1024]{1,0:T(8,128)(2,1)S(1)}, u32[]{:S(2)}, u32[]{:S(2)}) collective-permute-start(bf16[256,1024]{1,0:T(8,128)(2,1)S(1)} %get-tuple-element.55), channel_id=1, source_target_pairs={{0,64},{64,128},{128,192},{192,0},{1,65},{65,129},{129,193},{193,1... | collective-permute-start | bytes 1572872 | tf_op jit(solution)/shard_map/ppermute | solution.py:335
  88.3 9.3 %collective-permute-start.11 = (bf16[256,1024]{1,0:T(8,128)(2,1)S(1)}, bf16[256,1024]{1,0:T(8,128)(2,1)S(1)}, u32[]{:S(2)}, u32[]{:S(2)}) collective-permute-start(bf16[256,1024]{1,0:T(8,128)(2,1)S(1)} %get-tuple-element.56), channel_id=1, source_target_pairs={{0,192},{64,0},{128,64},{192,128},{1,193},{65,1},{129,65},{193,129... | collective-permute-start | bytes 1572872 | tf_op jit(solution)/shard_map/ppermute | solution.py:338
  92.7 17.1 %collective-permute-start.2 = (bf16[4,2,4,4,16,128]{5,4,3,2,1,0:T(8,128)(2,1)}, bf16[4,2,4,4,16,128]{5,4,3,2,1,0:T(8,128)(2,1)S(1)}, u32[]{:S(2)}, u32[]{:S(2)}) collective-permute-start(bf16[4,2,4,4,16,128]{5,4,3,2,1,0:T(8,128)(2,1)} %get-tuple-element.40), channel_id=1, source_target_pairs={{0,32},{4,36},{8,40},{12,44},{16,48},{20,52},{24,56},{28,60},{32,0... | collective-permute-start | bytes 1572872 | tf_op jit(solution)/shard_map/ppermute | solution.py:369
  98.6 32.6 %all-to-all-start.2 = ((bf16[4,256,256]{2,1,0:T(8,128)(2,1)}), bf16[4,256,256]{2,1,0:T(8,128)(2,1)S(1)}, u32[]{:S(2)}, u32[]{:S(2)}) async-start(bf16[4,256,256]{2,1,0:T(8,128)(2,1)} %shard_map.89), calls=%async_computation.2 | async-start | bytes 1048576 | tf_op jit(solution)/shard_map/all_to_all | solution.py:341
  109.9 8.7 %collective-permute-start.3 = (bf16[2,2,4,4,16,128]{5,4,3,2,1,0:T(8,128)(2,1)S(1)}, bf16[2,2,4,4,16,128]{5,4,3,2,1,0:T(8,128)(2,1)S(1)}, u32[]{:S(2)}, u32[]{:S(2)}) collective-permute-start(bf16[2,2,4,4,16,128]{5,4,3,2,1,0:T(8,128)(2,1)S(1)} %get-tuple-element.42), channel_id=1, source_target_pairs={{0,16},{4,20},{8,24},{12,28},{16,0},{20,4},{24,8},{28,12},{32,48},... | collective-permute-start | bytes 786440 | tf_op jit(solution)/shard_map/ppermute | solution.py:369
  118.8 5.1 %collective-permute-start.4 = (bf16[1,2,4,4,16,128]{5,4,3,2,1,0:T(8,128)(2,1)S(1)}, bf16[1,2,4,4,16,128]{5,4,3,2,1,0:T(8,128)(2,1)S(1)}, u32[]{:S(2)}, u32[]{:S(2)}) collective-permute-start(bf16[1,2,4,4,16,128]{5,4,3,2,1,0:T(8,128)(2,1)S(1)} %get-tuple-element.44), channel_id=1, source_target_pairs={{0,8},{4,12},{8,0},{12,4},{16,24},{20,28},{24,16},{28,20},{32,40},... | collective-permute-start | bytes 393224 | tf_op jit(solution)/shard_map/ppermute | solution.py:369
  124.4 7.7 %collective-permute-start.5 = (bf16[2,4,16,128]{3,2,1,0:T(8,128)(2,1)S(1)}, bf16[2,4,16,128]{3,2,1,0:T(8,128)(2,1)S(1)}, u32[]{:S(2)}, u32[]{:S(2)}) collective-permute-start(bf16[2,4,16,128]{3,2,1,0:T(8,128)(2,1)S(1)} %get-tuple-element.46), channel_id=1, source_target_pairs={{0,64},{64,128},{128,192},{192,0},{1,65},{65,129},{129,193},{193,1... | collective-permute-start | bytes 98312 | tf_op jit(solution)/shard_map/ppermute | solution.py:335
  126.7 5.8 %collective-permute-start.6 = (bf16[2,4,16,128]{3,2,1,0:T(8,128)(2,1)S(1)}, bf16[2,4,16,128]{3,2,1,0:T(8,128)(2,1)S(1)}, u32[]{:S(2)}, u32[]{:S(2)}) collective-permute-start(bf16[2,4,16,128]{3,2,1,0:T(8,128)(2,1)S(1)} %get-tuple-element.47), channel_id=1, source_target_pairs={{0,128},{64,192},{128,0},{192,64},{1,129},{65,193},{129,1},{193,65... | collective-permute-start | bytes 98312 | tf_op jit(solution)/shard_map/ppermute | solution.py:372
  130.3 3.9 %collective-permute-start.7 = (bf16[2,4,16,128]{3,2,1,0:T(8,128)(2,1)S(1)}, bf16[2,4,16,128]{3,2,1,0:T(8,128)(2,1)S(1)}, u32[]{:S(2)}, u32[]{:S(2)}) collective-permute-start(bf16[2,4,16,128]{3,2,1,0:T(8,128)(2,1)S(1)} %get-tuple-element.48), channel_id=1, source_target_pairs={{0,192},{64,0},{128,64},{192,128},{1,193},{65,1},{129,65},{193,129... | collective-permute-start | bytes 98312 | tf_op jit(solution)/shard_map/ppermute | solution.py:338

commit v2 on v1

--- a/solution.py
+++ b/solution.py
@@ -70,16 +70,17 @@
     )(in_hbm(rows), in_hbm(w_kv))
 
 
-def forward_kernel(scalars, src_len, tgt_len, mine, mate, kv_ref, qc_ref, stat_ref):
+def forward_kernel(start, scalars, src_len, tgt_len, mine, mate, kv_ref, qc_ref, stat_ref):
     seat, core = scalars[0], scalars[1]
     layers, count, _ = kv_ref.shape
     _, _, samples, rows, head = qc_ref.shape
     shards = stat_ref.shape[0]
-    keys = count // samples
+    keys = count // mine.shape[2]
     scale = head ** (-0.5)
     first = core == 0
 
-    def one(b, carry):
+    def one(at, carry):
+        b = start + at
         live = lax.broadcasted_iota(jnp.int32, (rows, head), 0) < tgt_len[b]
         key_live = seat * keys + lax.broadcasted_iota(jnp.int32, (keys, rows), 0) < src_len[b]
         tops, deltas = [], []
@@ -89,8 +90,8 @@
                 a, c = wide(mine[r, kind, b]), wide(mate[r, kind, b])
                 whole.append(jnp.concatenate([jnp.where(first, a, c), jnp.where(first, c, a)], axis=0))
             query, grad = low(whole[0]), low(jnp.where(live, whole[1], 0.0))
-            qc_ref[0, r, b] = query
-            qc_ref[1, r, b] = grad
+            qc_ref[0, r, at] = query
+            qc_ref[1, r, at] = grad
             pair = kv_ref[r, pl.ds(pl.multiple_of(b * keys, keys), keys), :]
             scores = jnp.where(key_live, dot(pair[:, :head], query, NT) * scale, masked_score)
             top = jnp.max(scores, axis=0, keepdims=True)
@@ -101,17 +102,18 @@
             deltas.append(part / total)
         stats = jnp.concatenate(tops + deltas, axis=0)
         for peer in range(shards):
-            stat_ref[peer, b] = stats
+            stat_ref[peer, at] = stats
         return carry
 
     lax.fori_loop(0, samples, one, 0)
 
 
-def forward(shards, scalars, src_len, tgt_len, mine, mate, kv):
+def forward(chunk, shards, scalars, src_len, tgt_len, mine, mate, kv):
     layers, _, samples, half, head = mine.shape
+    samples = samples // CHUNKS
     rows = 2 * half
     return pl.pallas_call(
-        forward_kernel,
+        functools.partial(forward_kernel, chunk * samples),
         out_shape=(
             kept_here(2, layers, samples, rows, head),
             kept_here(shards, samples, 2 * layers, rows, dtype=jnp.float32),
@@ -119,44 +121,57 @@
         in_specs=[SCALAR] * 3 + [FAST] * 3,
         out_specs=(FAST, FAST),
         compiler_params=ROOM,
-        name="forward",
     )(scalars, src_len, tgt_len, *held(mine, mate, kv))
 
 
-def terms_of(grads, w_ref, place, part):
+def fetch(scalars, first, w_hbm, w_ref, w_sem):
+    part = w_ref.shape[2]
+    takes = []
+    for k in range(w_ref.shape[0]):
+        at = pl.ds(pl.multiple_of(scalars[4 + first + k] * part, part), part)
+        takes.append(pltpu.make_async_copy(w_hbm.at[:, at], w_ref.at[k], w_sem.at[k]))
+        takes[k].start()
+    return takes
+
+
+def fetched(count, weights):
+    layers, width, cols = weights.shape
+    return [pltpu.VMEM((count, layers, width // 4, cols), jnp.bfloat16), pltpu.SemaphoreType.DMA((count,))]
+
+
+def terms_of(grads, weights):
     terms = None
-    at = pl.ds(pl.multiple_of(place * part, part), part)
     for r in range(grads.shape[0]):
-        term = dot(grads[r], w_ref[r, at, :], NT)
+        term = dot(grads[r], weights[r], NT)
         terms = term if terms is None else terms + term
-    return terms
-
-
-def backward_kernel(scalars, src_len, kv_ref, qc_ref, stat_ref, w_hbm, keep_ref, give_ref, grads, w_ref, *rest):
-    far_refs, w_sem = rest[:-1], rest[-1]
-    take = pltpu.make_async_copy(w_hbm, w_ref, w_sem)
-    take.start()
-    layers, count, _ = kv_ref.shape
+    return low(terms)
+
+
+def backward_kernel(start, keys, scalars, src_len, kv_ref, qc_ref, stat_ref, w_hbm,
+                    keep_ref, give_ref, grads, up_ref, down_ref, w_ref, w_sem):
+    (take,) = fetch(scalars, 0, w_hbm, w_ref, w_sem)
+    layers, _, _ = kv_ref.shape
     _, _, samples, rows, head = qc_ref.shape
     shards = stat_ref.shape[0]
-    keys = count // samples
     scale = head ** (-0.5)
     seat = scalars[0]
     even = scalars[1] == 0
 
-    def one(b, carry):
-        stat = stat_ref[:, b]
+    def one(k, carry):
+        b = start + k
+        stat = stat_ref[:, k]
         lse = stat[:, :layers]
         top = jnp.max(lse, axis=0)
         weight = jnp.exp(lse - top[None])
         inverse = 1.0 / jnp.sum(weight, axis=0)
         delta = jnp.sum(weight * stat[:, layers:], axis=0) * inverse
         down_live = seat * keys + lax.broadcasted_iota(jnp.int32, (keys, rows), 0) < src_len[b]
-        at = pl.ds(pl.multiple_of(b * keys, keys), keys)
+        taken = pl.ds(pl.multiple_of(b * keys, keys), keys)
+        at = pl.ds(pl.multiple_of(k * keys, keys), keys)
         for r in range(layers):
-            pair = kv_ref[r, at, :]
+            pair = kv_ref[r, taken, :]
             key, value = pair[:, :head], pair[:, head:]
-            query, grad = qc_ref[0, r, b], qc_ref[1, r, b]
+            query, grad = qc_ref[0, r, k], qc_ref[1, r, k]
             scores = jnp.where(down_live, dot(key, query, NT) * scale, masked_score)
             prob = jnp.exp(scores - top[r:r + 1, :]) * inverse[r:r + 1, :]
             slope = low(prob * (dot(value, grad, NT) - delta[r:r + 1, :]))
@@ -165,79 +180,95 @@
             grads[r, at, head:] = low(dot(prob, grad, NN))
             for kind, out in enumerate((dot(prob, value, TN), dot(slope, key, TN) * scale)):
                 out = out.reshape(shards // 2, 2, rows // shards, head)
-                keep_ref[:, kind, r, b] = low(jnp.where(even, out[:, 0], out[:, 1]))
-                give_ref[:, kind, r, b] = low(jnp.where(even, out[:, 1], out[:, 0]))
+                keep_ref[:, kind, r, k] = low(jnp.where(even, out[:, 0], out[:, 1]))
+                give_ref[:, kind, r, k] = low(jnp.where(even, out[:, 1], out[:, 0]))
         return carry
 
     lax.fori_loop(0, samples, one, 0)
     take.wait()
-    terms = low(terms_of(grads, w_ref, scalars[4], w_ref.shape[1] // 4))
-    size = far_refs[0].shape[0]
-    for k, ref in enumerate(far_refs):
-        ref[...] = terms[k * size:(k + 1) * size]
-
-
-def backward(scalars, src_len, kv, qc, stats, weights):
+    terms = terms_of(grads, w_ref.at[0])
+    half = up_ref.shape[0]
+    up_ref[...] = terms[:half]
+    down_ref[...] = terms[half:]
+
+
+def backward(chunk, scalars, src_len, kv, qc, stats, weights):
     _, layers, samples, rows, head = qc.shape
     shards = stats.shape[0]
-    part = weights.shape[1] // 4
     half = kept_here(shards // 2, 2, layers, samples, rows // shards, head)
-    far = kept_here(kv.shape[1] // (2 * CHUNKS), part)
-    outs = (half, half, kept_here(*kv.shape), kept_here(*weights.shape)) + (far,) * (2 * CHUNKS)
-    return pl.pallas_call(
-        backward_kernel,
+    count = kv.shape[1] // CHUNKS
+    far = kept_here(count // 2, weights.shape[1] // 4)
+    outs = (half, half, kept_here(layers, count, kv.shape[2]), far, far)
+    return pl.pallas_call(
+        functools.partial(backward_kernel, chunk * samples, count // samples),
         out_shape=outs,
         in_specs=[SCALAR] * 2 + [FAST] * 3 + [SLOW],
         out_specs=(FAST,) * len(outs),
-        scratch_shapes=[pltpu.SemaphoreType.DMA],
-        compiler_params=ROOM,
-        name="backward",
+        scratch_shapes=fetched(1, weights),
+        compiler_params=ROOM,
     )(scalars, src_len, *held(kv, qc, stats), in_hbm(weights))
 
 
-def near_kernel(scalars, grads, w_ref, *outs):
-    size = outs[0].shape[0]
-    for side in range(2):
-        terms = low(terms_of(grads, w_ref, scalars[5 + side], w_ref.shape[1] // 4))
-        for k in range(CHUNKS):
-            outs[side * CHUNKS + k][...] = terms[k * size:(k + 1) * size]
+def near_kernel(scalars, grads, w_hbm, up_ref, down_ref, w_ref, w_sem):
+    takes = fetch(scalars, 1, w_hbm, w_ref, w_sem)
+    for side, ref in enumerate((up_ref, down_ref)):
+        takes[side].wait()
+        ref[...] = terms_of(grads, w_ref.at[side])
 
 
 def near(scalars, grads, weights):
-    outs = (kept_here(grads.shape[1] // CHUNKS, weights.shape[1] // 4),) * (2 * CHUNKS)
-    return pl.pallas_call(
-        near_kernel, out_shape=outs, in_specs=[SCALAR, FAST, FAST], out_specs=(FAST,) * len(outs), compiler_params=ROOM, name="near"
-    )(scalars, *held(grads, weights))
-
-
-def here_kernel(scalars, grads, w_ref, out_ref):
-    out_ref[...] = low(terms_of(grads, w_ref, scalars[7], w_ref.shape[1] // 4))
+    outs = (kept_here(grads.shape[1], weights.shape[1] // 4),) * 2
+    return pl.pallas_call(
+        near_kernel,
+        out_shape=outs,
+        in_specs=[SCALAR, FAST, SLOW],
+        out_specs=(FAST,) * len(outs),
+        scratch_shapes=fetched(2, weights),
+        compiler_params=ROOM,
+    )(scalars, *held(grads), in_hbm(weights))
+
+
+def here_kernel(scalars, grads, w_hbm, out_ref, w_ref, w_sem):
+    (take,) = fetch(scalars, 3, w_hbm, w_ref, w_sem)
+    take.wait()
+    out_ref[...] = terms_of(grads, w_ref.at[0])
 
 
 def here(scalars, grads, weights):
     return pl.pallas_call(
         here_kernel,
         out_shape=kept_here(grads.shape[1], weights.shape[1] // 4),
-        in_specs=[SCALAR, FAST, FAST],
+        in_specs=[SCALAR, FAST, SLOW],
         out_specs=FAST,
-        compiler_params=ROOM,
-        name="here",
-    )(scalars, *held(grads, weights))
-
-
-def halve_kernel(side, kept, came, keep_ref, give_ref):
+        scratch_shapes=fetched(1, weights),
+        compiler_params=ROOM,
+    )(scalars, *held(grads), in_hbm(weights))
+
+
+def halve_kernel(parts, side, *refs):
+    kept, came = refs[:parts], refs[parts:2 * parts]
+    keep_ref, give_ref = refs[2 * parts:]
     count = keep_ref.shape[0]
     mine = pl.ds(side[0] * count, count)
     other = pl.ds((1 - side[0]) * count, count)
-    keep_ref[...] = low(wide(kept[mine]) + wide(came[mine]))
-    give_ref[...] = low(wide(kept[other]) + wide(came[other]))
+    size = keep_ref.shape[3] // parts
+    for k in range(parts):
+        at = slice(k * size, (k + 1) * size)
+        keep_ref[:, :, :, at] = low(wide(kept[k][mine]) + wide(came[k][mine]))
+        give_ref[:, :, :, at] = low(wide(kept[k][other]) + wide(came[k][other]))
 
 
 def halve(side, kept, came):
-    out = kept_here(kept.shape[0] // 2, *kept.shape[1:])
-    return pl.pallas_call(
-        halve_kernel, out_shape=(out, out), in_specs=[SCALAR, FAST, FAST], out_specs=(FAST, FAST), compiler_params=ROOM
-    )(side.reshape(1), *held(kept, came))
+    parts = len(kept)
+    count, kinds, layers, samples, rows, head = kept[0].shape
+    out = kept_here(count // 2, kinds, layers, samples * parts, rows, head)
+    return pl.pallas_call(
+        functools.partial(halve_kernel, parts),
+        out_shape=(out, out),
+        in_specs=[SCALAR] + [FAST] * (2 * parts),
+        out_specs=(FAST, FAST),
+        compiler_params=ROOM,
+    )(side.reshape(1), *held(*kept, *came))
 
 
 def deal_kernel(scalars, kept, came, *outs):
@@ -269,18 +300,17 @@
     )(*held(up_in, down_in, from_down, from_up))
 
 
-def gather_kernel(chunk, own, from_down, from_up, out_ref):
-    heads, count, part = out_ref.shape
+def gather_kernel(own, from_down, from_up, out_ref):
+    heads, _, part = out_ref.shape
     for h in range(heads):
         at = slice(h * part, (h + 1) * part)
-        mine = own[chunk * count:(chunk + 1) * count, at]
-        out_ref[h] = low(wide(mine) + wide(from_down[:, at]) + wide(from_up[:, at]))
-
-
-def gather(own, from_down, from_up, heads, chunk):
+        out_ref[h] = low(wide(own[:, at]) + wide(from_down[:, at]) + wide(from_up[:, at]))
+
+
+def gather(own, from_down, from_up, heads):
     count, width = from_down.shape
     return pl.pallas_call(
-        functools.partial(gather_kernel, chunk),
+        gather_kernel,
         out_shape=kept_here(heads, count, width // heads),
         in_specs=[FAST] * 3,
         out_specs=FAST,
@@ -347,27 +377,29 @@
     kv = project(encoder_states.reshape(samples * src_rows, width), w_kv)
     mine, kv = lax.optimization_barrier((mine, kv))
     mate = lax.ppermute(mine, "seq", flip(shards, 1))
-    qc, stats = forward(shards, scalars, src_len, tgt_len, mine, mate, kv)
-    stats = swap(stats, "seq")
-
     heads = lax.axis_size("head")
-    kept, give, grads, weights, *far = backward(scalars, src_len, kv, qc, stats, w_kv)
-    passed = [(up(far[2 * c]), down(far[2 * c + 1])) for c in range(CHUNKS)]
-    sides = near(scalars, grads, weights)
-    own = here(scalars, grads, weights)
-    pieces = []
+    ready = []
     for c in range(CHUNKS):
-        to_up, to_down = pass_on(sides[c], sides[CHUNKS + c], *passed[c])
+        qc, stats = forward(c, shards, scalars, src_len, tgt_len, mine, mate, kv)
+        ready.append((qc, swap(stats, "seq")))
+    pieces, kept, came = [], [], []
+    for c in range(CHUNKS):
+        keep, give, grads, far_up, far_down = backward(c, scalars, src_len, kv, *ready[c], w_kv)
+        came.append(lax.ppermute(give, "seq", flip(shards, 1)))
+        kept.append(keep)
+        far_up, far_down = up(far_up), down(far_down)
+        to_up, to_down = near(scalars, grads, w_kv)
+        own = here(scalars, grads, w_kv)
+        to_up, to_down = pass_on(to_up, to_down, far_up, far_down)
         to_up, to_down = up(to_up), down(to_down)
-        joined = gather(own, to_up, to_down, heads, c)
+        joined = gather(own, to_up, to_down, heads)
         pieces.append(swap(joined, "head"))
     source_grads = finish(pieces).reshape(samples, src_rows, cols)
 
-    for stage, bit in enumerate((0, 3, 2, 1)):
-        if stage:
-            kept, give = halve(bits[bit].astype(jnp.int32), kept, came)
-        came = lax.ppermute(give, "seq", flip(shards, 1 << bit))
-    own, to_up, to_far, to_down = deal(scalars, kept, came)
+    for bit in (3, 2, 1):
+        keep, give = halve(bits[bit].astype(jnp.int32), kept, came)
+        kept, came = [keep], [lax.ppermute(give, "seq", flip(shards, 1 << bit))]
+    own, to_up, to_far, to_down = deal(scalars, kept[0], came[0])
     from_down, from_up = up(to_up), down(to_down)
     from_far = lax.ppermute(to_far, "section", turn(4, 2))
     ring = jnp.stack([own, from_down, from_far, from_up])

time: 136 us -> 143 us (1.051)
  blocking collectives: 16.4 us -> 0 us
  Pallas kernels: 29.5 us -> 39.5 us
  starting transfers between devices: 41.5 us -> 48 us
  local copies, waits for them, and re-layouts: 4.3 us -> 8.89 us
  waiting for transfers between devices: 42.1 us -> 44 us
    all_to_all x1 -> x0, blocking collectives: 16.4 us -> none  [swap(): return lax.all_to_all(a, axis, 0, 0, tiled=True)]
    all_to_all x3 -> x5, starting transfers between devices: 19 us -> 27.3 us  [swap(): return lax.all_to_all(a, axis, 0, 0, tiled=True)]
    pallas_call x8 -> x11, Pallas kernels: 16.8 us -> 22.9 us  [the longest x2 8.21 us: backward(): pl.pallas_call(functools.partial(backward_kernel, chunk * samples, count...]
    all_to_all x3 -> x5, waiting for transfers between devices: 6.81 us -> 11.7 us  [swap(): return lax.all_to_all(a, axis, 0, 0, tiled=True)]
    unnamed x10 -> x26, local copies, waits for them, and re-layouts: 2.42 us -> 7.01 us
    pallas_call x1 -> x2, Pallas kernels: 1.82 us -> 5.77 us  [here(): pl.pallas_call(here_kernel, out_shape=kept_here(grads.shape[1], weights.s...]
    ppermute x4 -> x5, starting transfers between devices: 2.43 us -> 6.16 us  [the longest x3 5.57 us: body(): kept, came = ([keep], [lax.ppermute(give, 'seq', flip(shards, 1 << bit))])]
    ppermute x5, starting transfers between devices: 4.22 us -> 1.02 us  [up(): return lax.ppermute(a, 'section', turn(4, 1))]
  transfers between devices with their start and end apart: 19 -> 22, of which waited for: 10 -> 10; matrix products, arithmetic and copies ran while one was open for 0% -> 1% of each run, Pallas kernels for 15% -> 26%
where the time goes in v2:
time: 143 us; the launch traced here: 142 us
  starting transfers between devices  48 us (34%)
  waiting for transfers between devices  44 us (31%)
  Pallas kernels  39.5 us (28%)
  local copies, waits for them, and re-layouts  8.89 us (6%)
    all_to_all x5, starting transfers between devices, swap(): return lax.all_to_all(a, axis, 0, 0, tiled=True)  27.3 us
    ppermute x3, waiting for transfers between devices, body(): kept, came = ([keep], [lax.ppermute(give, 'seq', flip(shards, 1 << bit))])  13.7 us
    ppermute x5, waiting for transfers between devices, up(): return lax.ppermute(a, 'section', turn(4, 1))  13.2 us
    all_to_all x5, waiting for transfers between devices, swap(): return lax.all_to_all(a, axis, 0, 0, tiled=True)  11.7 us
    ppermute x5, starting transfers between devices, down(): return lax.ppermute(a, 'section', turn(4, 3))  11 us
    pallas_call x1, Pallas kernels, project(): pl.pallas_call(project_kernel, out_shape=kept_here(layers, count, cols),...  8.29 us
    pallas_call x2, Pallas kernels, backward(): pl.pallas_call(functools.partial(backward_kernel, chunk * samples, count...  8.21 us
    pallas_call x2, Pallas kernels, near(): pl.pallas_call(near_kernel, out_shape=outs, in_specs=[SCALAR, FAST, SLOW]...  7.26 us
  transfers between devices with their start and end apart: 22, of which 10 were waited for; matrix products, arithmetic and copies ran while one was open for 1% of the time, Pallas kernels for 26%

profile of v2, /device:TPU:64, one launch (start us, length us, event | category | flops | bytes accessed | tf_op | source)
XLA Modules:
  0.0 142.5 jit_solution(39589484215925072)
XLA Ops:
  0.6 1.6 %constant_dynamic-slice_fusion = (bf16[1,4,128,4,128]{4,3,2,1,0:T(4,128)(2,1)S(1)}, bf16[1,4,128,4,128]{4,3,2,1,0:T(4,128)(2,1)S(1)}) fusion(bf16[1,4,256,4,128]{4,3,2,1,0:T(4,128)(2,1)} %param.9, s32[]{:T(128)S(6)} %select_n.86, bf16[1,4,256,4,128]{4,3,2,1,0:T(4,128)(2,1)} %param.8), kind=kLoop, calls=%fused_computation.9 | loop fusion | bytes 2097156 | tf_op jit(solution)/shard_map/dynamic_slice | solution.py:374
  2.4 1.1 pad_maximum_fusion
  3.5 4.6 %all-to-all-start = ((bf16[4,2,4,128,128]{4,3,2,1,0:T(8,128)(2,1)}), bf16[4,2,4,128,128]{4,3,2,1,0:T(8,128)(2,1)S(1)}, u32[]{:S(2)}, u32[]{:S(2)}) async-start(bf16[4,2,4,128,128]{4,3,2,1,0:T(8,128)(2,1)} %pad_maximum_fusion), calls=%async_computation | async-start | bytes 2097152 | tf_op jit(solution)/shard_map/all_to_all | solution.py:371
  8.1 8.3 %project.1.kv_ref = bf16[4,512,256]{2,1,0:T(8,128)(2,1)S(1)} custom-call(bf16[512,4096]{1,0:T(8,128)(2,1)} %bitcast.39, bf16[4,4096,256]{2,1,0:T(8,128)(2,1)} %w_hbm.11), custom_call_target="tpu_custom_call" | custom-call | tf_op jit(solution)/shard_map/project/pallas_call | solution.py:59
  16.4 6.8 %all-to-all-done.mine = bf16[4,2,4,128,128]{4,3,2,1,0:T(8,128)(2,1)S(1)} async-done(((bf16[4,2,4,128,128]{4,3,2,1,0:T(8,128)(2,1)}), bf16[4,2,4,128,128]{4,3,2,1,0:T(8,128)(2,1)S(1)}, u32[]{:S(2)}, u32[]{:S(2)}) %all-to-all-start) | async-done | bytes 1048608 | tf_op jit(solution)/shard_map/all_to_all | solution.py:371
  23.3 2.6 %collective-permute-done.mate = bf16[4,2,4,128,128]{4,3,2,1,0:T(8,128)(2,1)S(1)} collective-permute-done((bf16[4,2,4,128,128]{4,3,2,1,0:T(8,128)(2,1)S(1)}, bf16[4,2,4,128,128]{4,3,2,1,0:T(8,128)(2,1)S(1)}, u32[]{:S(2)}, u32[]{:S(2)}) %collective-permute-start) | collective-permute-done | bytes 1048608 | tf_op jit(solution)/shard_map/ppermute | solution.py:379
  25.9 1.4 shard_map.85
  27.3 1.0 copy-done.2
  28.2 0.7 copy-done.9
  28.9 5.8 %all-to-all-start.1 = ((f32[16,2,8,256]{3,2,1,0:T(8,128)}), f32[16,2,8,256]{3,2,1,0:T(8,128)S(1)}, u32[]{:S(2)}, u32[]{:S(2)}) async-start(f32[16,2,8,256]{3,2,1,0:T(8,128)} %copy-done.9), calls=%async_computation.1 | async-start | bytes 524288 | tf_op jit(solution)/shard_map/all_to_all | solution.py:371
  34.7 1.4 shard_map.87
  36.1 1.0 copy-done
  37.1 0.7 copy-done.8
  37.8 4.9 %all-to-all-done.1.stat_ref = f32[16,2,8,256]{3,2,1,0:T(8,128)S(1)} async-done(((f32[16,2,8,256]{3,2,1,0:T(8,128)}), f32[16,2,8,256]{3,2,1,0:T(8,128)S(1)}, u32[]{:S(2)}, u32[]{:S(2)}) %all-to-all-start.1) | async-done | bytes 262176 | tf_op jit(solution)/shard_map/all_to_all | solution.py:371
  42.7 3.5 %all-to-all-start.2 = ((f32[16,2,8,256]{3,2,1,0:T(8,128)}), f32[16,2,8,256]{3,2,1,0:T(8,128)S(1)}, u32[]{:S(2)}, u32[]{:S(2)}) async-start(f32[16,2,8,256]{3,2,1,0:T(8,128)} %copy-done.8), calls=%async_computation.2 | async-start | bytes 524288 | tf_op jit(solution)/shard_map/all_to_all | solution.py:371
  46.3 1.2 copy-done.3
  47.5 3.8 %shard_map.86 = (bf16[8,2,4,2,16,128]{5,4,3,2,1,0:T(8,128)(2,1)S(1)}, bf16[8,2,4,2,16,128]{5,4,3,2,1,0:T(8,128)(2,1)}, bf16[4,256,256]{2,1,0:T(8,128)(2,1)S(1)},...) custom-call(s32[12]{0:T(128)S(1)} %stack.84.scalars, s32[4]{0:T(128)S(1)} %copy-done.10, ...), custom_call_target="tpu_custom_call" | custom-call | tf_op jit(solution)/shard_map/pallas_call | solution.py:202
  51.3 0.7 collective-permute-start.9
  51.9 2.7 %collective-permute-start.10 = (bf16[128,1024]{1,0:T(8,128)(2,1)S(1)}, bf16[128,1024]{1,0:T(8,128)(2,1)S(1)}, u32[]{:S(2)}, u32[]{:S(2)}) collective-permute-start(bf16[128,1024]{1,0:T(8,128)(2,1)S(1)} %get-tuple-element.61), channel_id=1, source_target_pairs={{0,192},{64,0},{128,64},{192,128},{1,193},{65,1},{129,65},{193,129... | collective-permute-start | bytes 786440 | tf_op jit(solution)/shard_map/ppermute | solution.py:368
  54.6 3.6 %shard_map.93 = (bf16[256,1024]{1,0:T(8,128)(2,1)S(1)}, bf16[256,1024]{1,0:T(8,128)(2,1)S(1)}) custom-call(s32[12]{0:T(128)S(1)} %stack.84.scalars, bf16[4,256,256]{2,1,0:T(8,128)(2,1)S(1)} %get-tuple-element.57.grads, bf16[4,4096,256]{2,1,0:T(8,128)(2,1)} %w_hbm.11), custom_call_target="tpu_custom_call" | custom-call | tf_op jit(solution)/shard_map/pallas_call | solution.py:221
  58.2 2.8 %collective-permute-done.9.from_down = bf16[128,1024]{1,0:T(8,128)(2,1)S(1)} collective-permute-done((bf16[128,1024]{1,0:T(8,128)(2,1)S(1)}, bf16[128,1024]{1,0:T(8,128)(2,1)S(1)}, u32[]{:S(2)}, u32[]{:S(2)}) %collective-permute-start.9) | collective-permute-done | bytes 262176 | tf_op jit(solution)/shard_map/ppermute | solution.py:365
  61.1 1.1 shard_map.94
  62.1 3.2 %collective-permute-start.12 = (bf16[256,1024]{1,0:T(8,128)(2,1)}, bf16[256,1024]{1,0:T(8,128)(2,1)}, u32[]{:S(2)}, u32[]{:S(2)}) collective-permute-start(bf16[256,1024]{1,0:T(8,128)(2,1)} %get-tuple-element.63), channel_id=1, source_target_pairs={{0,192},{64,0},{128,64},{192,128},{1,193},{65,1},{129,65},{193,129... | collective-permute-start | bytes 1572872 | tf_op jit(solution)/shard_map/ppermute | solution.py:368
  65.4 4.5 %shard_map.88 = (bf16[8,2,4,2,16,128]{5,4,3,2,1,0:T(8,128)(2,1)S(1)}, bf16[8,2,4,2,16,128]{5,4,3,2,1,0:T(8,128)(2,1)}, bf16[4,256,256]{2,1,0:T(8,128)(2,1)S(1)},...) custom-call(s32[12]{0:T(128)S(1)} %stack.84.scalars, s32[4]{0:T(128)S(1)} %copy-done.10, ...), custom_call_target="tpu_custom_call" | custom-call | tf_op jit(solution)/shard_map/pallas_call | solution.py:202
  70.5 8.0 %collective-permute-done.11.from_down = bf16[256,1024]{1,0:T(8,128)(2,1)} collective-permute-done((bf16[256,1024]{1,0:T(8,128)(2,1)}, bf16[256,1024]{1,0:T(8,128)(2,1)}, u32[]{:S(2)}, u32[]{:S(2)}) %collective-permute-start.11) | collective-permute-done | bytes 524320 | tf_op jit(solution)/shard_map/ppermute | solution.py:365
  78.5 1.7 %collective-permute-start.14 = (bf16[128,1024]{1,0:T(8,128)(2,1)}, bf16[128,1024]{1,0:T(8,128)(2,1)S(1)}, u32[]{:S(2)}, u32[]{:S(2)}) collective-permute-start(bf16[128,1024]{1,0:T(8,128)(2,1)} %get-tuple-element.68), channel_id=1, source_target_pairs={{0,192},{64,0},{128,64},{192,128},{1,193},{65,1},{129,65},{193,129... | collective-permute-start | bytes 786440 | tf_op jit(solution)/shard_map/ppermute | solution.py:368
  80.2 2.9 %shard_map.92.own = bf16[256,1024]{1,0:T(8,128)(2,1)S(1)} custom-call(s32[12]{0:T(128)S(1)} %stack.84.scalars, bf16[4,256,256]{2,1,0:T(8,128)(2,1)S(1)} %get-tuple-element.57.grads, bf16[4,4096,256]{2,1,0:T(8,128)(2,1)} %w_hbm.11), custom_call_target="tpu_custom_call" | custom-call | tf_op jit(solution)/shard_map/pallas_call | solution.py:238
  83.1 2.2 %shard_map.95 = bf16[4,256,256]{2,1,0:T(8,128)(2,1)} custom-call(bf16[256,1024]{1,0:T(8,128)(2,1)S(1)} %shard_map.92.own, bf16[256,1024]{1,0:T(8,128)(2,1)} %collective-permute-done.11.from_down, bf16[256,1024]{1,0:T(8,128)(2,1)} %collective-permute-done.12.from_up), custom_call_target="tpu_custom_call" | custom-call | tf_op jit(solution)/shard_map/pallas_call | solution.py:312
  85.3 7.2 %all-to-all-start.3 = ((bf16[4,256,256]{2,1,0:T(8,128)(2,1)}), bf16[4,256,256]{2,1,0:T(8,128)(2,1)S(1)}, u32[]{:S(2)}, u32[]{:S(2)}) async-start(bf16[4,256,256]{2,1,0:T(8,128)(2,1)} %shard_map.95), calls=%async_computation.3 | async-start | bytes 1048576 | tf_op jit(solution)/shard_map/all_to_all | solution.py:371
  92.5 1.0 copy-done.7
  93.6 1.3 shard_map.89
  94.8 1.8 %collective-permute-start.3 = (bf16[4,2,4,4,16,128]{5,4,3,2,1,0:T(8,128)(2,1)S(1)}, bf16[4,2,4,4,16,128]{5,4,3,2,1,0:T(8,128)(2,1)S(1)}, u32[]{:S(2)}, u32[]{:S(2)}) collective-permute-start(bf16[4,2,4,4,16,128]{5,4,3,2,1,0:T(8,128)(2,1)S(1)} %get-tuple-element.48), channel_id=1, source_target_pairs={{0,32},{4,36},{8,40},{12,44},{16,48},{20,52},{24,56},{28,60},{32,0... | collective-permute-start | bytes 1572872 | tf_op jit(solution)/shard_map/ppermute | solution.py:401
  96.6 3.6 %shard_map.97 = (bf16[256,1024]{1,0:T(8,128)(2,1)S(1)}, bf16[256,1024]{1,0:T(8,128)(2,1)S(1)}) custom-call(s32[12]{0:T(128)S(1)} %stack.84.scalars, bf16[4,256,256]{2,1,0:T(8,128)(2,1)S(1)} %get-tuple-element.64.grads, bf16[4,4096,256]{2,1,0:T(8,128)(2,1)} %w_hbm.11), custom_call_target="tpu_custom_call" | custom-call | tf_op jit(solution)/shard_map/pallas_call | solution.py:221
  100.8 3.0 %collective-permute-start.16 = (bf16[256,1024]{1,0:T(8,128)(2,1)S(1)}, bf16[256,1024]{1,0:T(8,128)(2,1)S(1)}, u32[]{:S(2)}, u32[]{:S(2)}) collective-permute-start(bf16[256,1024]{1,0:T(8,128)(2,1)S(1)} %get-tuple-element.70), channel_id=1, source_target_pairs={{0,192},{64,0},{128,64},{192,128},{1,193},{65,1},{129,65},{193,129... | collective-permute-start | bytes 1572872 | tf_op jit(solution)/shard_map/ppermute | solution.py:368
  103.7 9.3 %collective-permute-done.3.refs_1_ = bf16[4,2,4,4,16,128]{5,4,3,2,1,0:T(8,128)(2,1)S(1)} collective-permute-done((bf16[4,2,4,4,16,128]{5,4,3,2,1,0:T(8,128)(2,1)S(1)}, bf16[4,2,4,4,16,128]{5,4,3,2,1,0:T(8,128)(2,1)S(1)}, u32[]{:S(2)}, u32[]{:S(2)}) %collective-permute-start.3) | collective-permute-done | bytes 524320 | tf_op jit(solution)/shard_map/ppermute | solution.py:401
  113.2 3.1 %collective-permute-start.4 = (bf16[2,2,4,4,16,128]{5,4,3,2,1,0:T(8,128)(2,1)S(1)}, bf16[2,2,4,4,16,128]{5,4,3,2,1,0:T(8,128)(2,1)S(1)}, u32[]{:S(2)}, u32[]{:S(2)}) collective-permute-start(bf16[2,2,4,4,16,128]{5,4,3,2,1,0:T(8,128)(2,1)S(1)} %get-tuple-element.50), channel_id=1, source_target_pairs={{0,16},{4,20},{8,24},{12,28},{16,0},{20,4},{24,8},{28,12},{32,48},... | collective-permute-start | bytes 786440 | tf_op jit(solution)/shard_map/ppermute | solution.py:401
  116.3 2.9 %shard_map.96.own = bf16[256,1024]{1,0:T(8,128)(2,1)S(1)} custom-call(s32[12]{0:T(128)S(1)} %stack.84.scalars, bf16[4,256,256]{2,1,0:T(8,128)(2,1)S(1)} %get-tuple-element.64.grads, bf16[4,4096,256]{2,1,0:T(8,128)(2,1)} %w_hbm.11), custom_call_target="tpu_custom_call" | custom-call | tf_op jit(solution)/shard_map/pallas_call | solution.py:238
  119.2 1.0 shard_map.99
  120.2 6.2 %all-to-all-start.4 = ((bf16[4,256,256]{2,1,0:T(8,128)(2,1)}), bf16[4,256,256]{2,1,0:T(8,128)(2,1)S(1)}, u32[]{:S(2)}, u32[]{:S(2)}) async-start(bf16[4,256,256]{2,1,0:T(8,128)(2,1)} %shard_map.99), calls=%async_computation.4 | async-start | bytes 1048576 | tf_op jit(solution)/shard_map/all_to_all | solution.py:371
  126.4 0.7 collective-permute-start.5
  127.1 4.3 %collective-permute-done.5.came = bf16[1,2,4,4,16,128]{5,4,3,2,1,0:T(8,128)(2,1)S(1)} collective-permute-done((bf16[1,2,4,4,16,128]{5,4,3,2,1,0:T(8,128)(2,1)S(1)}, bf16[1,2,4,4,16,128]{5,4,3,2,1,0:T(8,128)(2,1)S(1)}, u32[]{:S(2)}, u32[]{:S(2)}) %collective-permute-start.5) | collective-permute-done | bytes 131104 | tf_op jit(solution)/shard_map/ppermute | solution.py:401
  132.4 2.6 %collective-permute-start.7 = (bf16[2,4,16,128]{3,2,1,0:T(8,128)(2,1)S(1)}, bf16[2,4,16,128]{3,2,1,0:T(8,128)(2,1)S(1)}, u32[]{:S(2)}, u32[]{:S(2)}) collective-permute-start(bf16[2,4,16,128]{3,2,1,0:T(8,128)(2,1)S(1)} %get-tuple-element.55), channel_id=1, source_target_pairs={{0,128},{64,192},{128,0},{192,64},{1,129},{65,193},{129,1},{193,65... | collective-permute-start | bytes 98312 | tf_op jit(solution)/shard_map/ppermute | solution.py:404
  135.1 1.0 collective-permute-done.8
  136.1 1.8 %collective-permute-done.7 = bf16[2,4,16,128]{3,2,1,0:T(8,128)(2,1)S(1)} collective-permute-done((bf16[2,4,16,128]{3,2,1,0:T(8,128)(2,1)S(1)}, bf16[2,4,16,128]{3,2,1,0:T(8,128)(2,1)S(1)}, u32[]{:S(2)}, u32[]{:S(2)}) %collective-permute-start.7) | collective-permute-done | bytes 32800 | tf_op jit(solution)/shard_map/ppermute | solution.py:404
  137.9 2.3 %collective-permute-done.6 = bf16[2,4,16,128]{3,2,1,0:T(8,128)(2,1)S(1)} collective-permute-done((bf16[2,4,16,128]{3,2,1,0:T(8,128)(2,1)S(1)}, bf16[2,4,16,128]{3,2,1,0:T(8,128)(2,1)S(1)}, u32[]{:S(2)}, u32[]{:S(2)}) %collective-permute-start.6) | collective-permute-done | bytes 32800 | tf_op jit(solution)/shard_map/ppermute | solution.py:365
  140.3 0.7 copy.13
  141.0 0.7 copy.14
  141.7 0.8 finish.1
  (49 shorter events, 2.6 us)
Async XLA Ops:
  3.5 22.4 %copy-start.10 = (s32[4]{0:T(128)S(1)}, s32[4]{0:T(128)}, u32[]{:S(2)}) copy-start(s32[4]{0:T(128)} %src_len.7) | copy-start | bytes 52
  3.5 22.4 %copy-start.11 = (s32[4]{0:T(128)S(1)}, s32[4]{0:T(128)}, u32[]{:S(2)}) copy-start(s32[4]{0:T(128)} %tgt_len.3) | copy-start | bytes 52
  3.5 19.7 %all-to-all-start = ((bf16[4,2,4,128,128]{4,3,2,1,0:T(8,128)(2,1)}), bf16[4,2,4,128,128]{4,3,2,1,0:T(8,128)(2,1)S(1)}, u32[]{:S(2)}, u32[]{:S(2)}) async-start(bf16[4,2,4,128,128]{4,3,2,1,0:T(8,128)(2,1)} %pad_maximum_fusion), calls=%async_computation | async-start | bytes 2097152 | tf_op jit(solution)/shard_map/all_to_all | solution.py:371
  23.2 2.7 %collective-permute-start = (bf16[4,2,4,128,128]{4,3,2,1,0:T(8,128)(2,1)S(1)}, bf16[4,2,4,128,128]{4,3,2,1,0:T(8,128)(2,1)S(1)}, u32[]{:S(2)}, u32[]{:S(2)}) collective-permute-start(bf16[4,2,4,128,128]{4,3,2,1,0:T(8,128)(2,1)S(1)} %all-to-all-done.mine), channel_id=1, source_target_pairs={{0,4},{4,0},{8,12},{12,8},{16,20},{20,16},{24,28},{28,24},{32,36},... | collective-permute-start | bytes 3145736 | tf_op jit(solution)/shard_map/ppermute | solution.py:379
  27.3 1.0 copy-start.2
  28.2 0.7 copy-start.9
  28.9 13.8 %all-to-all-start.1 = ((f32[16,2,8,256]{3,2,1,0:T(8,128)}), f32[16,2,8,256]{3,2,1,0:T(8,128)S(1)}, u32[]{:S(2)}, u32[]{:S(2)}) async-start(f32[16,2,8,256]{3,2,1,0:T(8,128)} %copy-done.9), calls=%async_computation.1 | async-start | bytes 524288 | tf_op jit(solution)/shard_map/all_to_all | solution.py:371
  36.1 1.0 copy-start
  37.1 0.7 copy-start.8
  42.7 22.7 %all-to-all-start.2 = ((f32[16,2,8,256]{3,2,1,0:T(8,128)}), f32[16,2,8,256]{3,2,1,0:T(8,128)S(1)}, u32[]{:S(2)}, u32[]{:S(2)}) async-start(f32[16,2,8,256]{3,2,1,0:T(8,128)} %copy-done.8), calls=%async_computation.2 | async-start | bytes 524288 | tf_op jit(solution)/shard_map/all_to_all | solution.py:371
  46.3 1.2 copy-start.3
  51.3 14.1 %copy-start.4 = (bf16[8,2,4,2,16,128]{5,4,3,2,1,0:T(8,128)(2,1)}, bf16[8,2,4,2,16,128]{5,4,3,2,1,0:T(8,128)(2,1)S(1)}, u32[]{:S(2)}) copy-start(bf16[8,2,4,2,16,128]{5,4,3,2,1,0:T(8,128)(2,1)S(1)} %get-tuple-element.41.refs_0_) | copy-start | bytes 1572868
  51.3 14.1 %copy-start.1 = (bf16[2,4,2,256,128]{4,3,2,1,0:T(8,128)(2,1)S(1)}, bf16[2,4,2,256,128]{4,3,2,1,0:T(8,128)(2,1)}, u32[]{:S(2)}) copy-start(bf16[2,4,2,256,128]{4,3,2,1,0:T(8,128)(2,1)} %copy-done) | copy-start | bytes 3145732
  51.3 9.8 %collective-permute-start.9 = (bf16[128,1024]{1,0:T(8,128)(2,1)S(1)}, bf16[128,1024]{1,0:T(8,128)(2,1)S(1)}, u32[]{:S(2)}, u32[]{:S(2)}) collective-permute-start(bf16[128,1024]{1,0:T(8,128)(2,1)S(1)} %get-tuple-element.60), channel_id=1, source_target_pairs={{0,64},{64,128},{128,192},{192,0},{1,65},{65,129},{129,193},{193,1... | collective-permute-start | bytes 786440 | tf_op jit(solution)/shard_map/ppermute | solution.py:365
  51.9 9.1 %collective-permute-start.10 = (bf16[128,1024]{1,0:T(8,128)(2,1)S(1)}, bf16[128,1024]{1,0:T(8,128)(2,1)S(1)}, u32[]{:S(2)}, u32[]{:S(2)}) collective-permute-start(bf16[128,1024]{1,0:T(8,128)(2,1)S(1)} %get-tuple-element.61), channel_id=1, source_target_pairs={{0,192},{64,0},{128,64},{192,128},{1,193},{65,1},{129,65},{193,129... | collective-permute-start | bytes 786440 | tf_op jit(solution)/shard_map/ppermute | solution.py:368
  62.1 16.3 %collective-permute-start.11 = (bf16[256,1024]{1,0:T(8,128)(2,1)}, bf16[256,1024]{1,0:T(8,128)(2,1)}, u32[]{:S(2)}, u32[]{:S(2)}) collective-permute-start(bf16[256,1024]{1,0:T(8,128)(2,1)} %get-tuple-element.62), channel_id=1, source_target_pairs={{0,64},{64,128},{128,192},{192,0},{1,65},{65,129},{129,193},{193,1... | collective-permute-start | bytes 1572872 | tf_op jit(solution)/shard_map/ppermute | solution.py:365
  62.1 21.0 %collective-permute-start.12 = (bf16[256,1024]{1,0:T(8,128)(2,1)}, bf16[256,1024]{1,0:T(8,128)(2,1)}, u32[]{:S(2)}, u32[]{:S(2)}) collective-permute-start(bf16[256,1024]{1,0:T(8,128)(2,1)} %get-tuple-element.63), channel_id=1, source_target_pairs={{0,192},{64,0},{128,64},{192,128},{1,193},{65,1},{129,65},{193,129... | collective-permute-start | bytes 1572872 | tf_op jit(solution)/shard_map/ppermute | solution.py:368
  65.4 27.1 %collective-permute-start.1 = (bf16[8,2,4,2,16,128]{5,4,3,2,1,0:T(8,128)(2,1)}, bf16[8,2,4,2,16,128]{5,4,3,2,1,0:T(8,128)(2,1)}, u32[]{:S(2)}, u32[]{:S(2)}) collective-permute-start(bf16[8,2,4,2,16,128]{5,4,3,2,1,0:T(8,128)(2,1)} %get-tuple-element.45), channel_id=1, source_target_pairs={{0,4},{4,0},{8,12},{12,8},{16,20},{20,16},{24,28},{28,24},{32,36},... | collective-permute-start | bytes 1572872 | tf_op jit(solution)/shard_map/ppermute | solution.py:388
  69.9 13.2 %copy-start.6 = (bf16[8,2,4,2,16,128]{5,4,3,2,1,0:T(8,128)(2,1)}, bf16[8,2,4,2,16,128]{5,4,3,2,1,0:T(8,128)(2,1)S(1)}, u32[]{:S(2)}) copy-start(bf16[8,2,4,2,16,128]{5,4,3,2,1,0:T(8,128)(2,1)S(1)} %get-tuple-element.44.refs_1_) | copy-start | bytes 1572868
  69.9 22.6 %copy-start.5 = (bf16[8,2,4,2,16,128]{5,4,3,2,1,0:T(8,128)(2,1)S(1)}, bf16[8,2,4,2,16,128]{5,4,3,2,1,0:T(8,128)(2,1)}, u32[]{:S(2)}) copy-start(bf16[8,2,4,2,16,128]{5,4,3,2,1,0:T(8,128)(2,1)} %copy-done.4) | copy-start | bytes 1572868
  69.9 22.6 %collective-permute-start.2 = (bf16[8,2,4,2,16,128]{5,4,3,2,1,0:T(8,128)(2,1)}, bf16[8,2,4,2,16,128]{5,4,3,2,1,0:T(8,128)(2,1)S(1)}, u32[]{:S(2)}, u32[]{:S(2)}) collective-permute-start(bf16[8,2,4,2,16,128]{5,4,3,2,1,0:T(8,128)(2,1)} %get-tuple-element.46), channel_id=1, source_target_pairs={{0,4},{4,0},{8,12},{12,8},{16,20},{20,16},{24,28},{28,24},{32,36},... | collective-permute-start | bytes 1572872 | tf_op jit(solution)/shard_map/ppermute | solution.py:388
  70.5 29.8 %collective-permute-start.13 = (bf16[128,1024]{1,0:T(8,128)(2,1)}, bf16[128,1024]{1,0:T(8,128)(2,1)S(1)}, u32[]{:S(2)}, u32[]{:S(2)}) collective-permute-start(bf16[128,1024]{1,0:T(8,128)(2,1)} %get-tuple-element.67), channel_id=1, source_target_pairs={{0,64},{64,128},{128,192},{192,0},{1,65},{65,129},{129,193},{193,1... | collective-permute-start | bytes 786440 | tf_op jit(solution)/shard_map/ppermute | solution.py:365
  78.5 21.8 %collective-permute-start.14 = (bf16[128,1024]{1,0:T(8,128)(2,1)}, bf16[128,1024]{1,0:T(8,128)(2,1)S(1)}, u32[]{:S(2)}, u32[]{:S(2)}) collective-permute-start(bf16[128,1024]{1,0:T(8,128)(2,1)} %get-tuple-element.68), channel_id=1, source_target_pairs={{0,192},{64,0},{128,64},{192,128},{1,193},{65,1},{129,65},{193,129... | collective-permute-start | bytes 786440 | tf_op jit(solution)/shard_map/ppermute | solution.py:368
  85.3 34.9 %all-to-all-start.3 = ((bf16[4,256,256]{2,1,0:T(8,128)(2,1)}), bf16[4,256,256]{2,1,0:T(8,128)(2,1)S(1)}, u32[]{:S(2)}, u32[]{:S(2)}) async-start(bf16[4,256,256]{2,1,0:T(8,128)(2,1)} %shard_map.95), calls=%async_computation.3 | async-start | bytes 1048576 | tf_op jit(solution)/shard_map/all_to_all | solution.py:371
  92.5 1.0 copy-start.7
  94.8 18.2 %collective-permute-start.3 = (bf16[4,2,4,4,16,128]{5,4,3,2,1,0:T(8,128)(2,1)S(1)}, bf16[4,2,4,4,16,128]{5,4,3,2,1,0:T(8,128)(2,1)S(1)}, u32[]{:S(2)}, u32[]{:S(2)}) collective-permute-start(bf16[4,2,4,4,16,128]{5,4,3,2,1,0:T(8,128)(2,1)S(1)} %get-tuple-element.48), channel_id=1, source_target_pairs={{0,32},{4,36},{8,40},{12,44},{16,48},{20,52},{24,56},{28,60},{32,0... | collective-permute-start | bytes 1572872 | tf_op jit(solution)/shard_map/ppermute | solution.py:401
  100.4 18.8 %collective-permute-start.15 = (bf16[256,1024]{1,0:T(8,128)(2,1)S(1)}, bf16[256,1024]{1,0:T(8,128)(2,1)S(1)}, u32[]{:S(2)}, u32[]{:S(2)}) collective-permute-start(bf16[256,1024]{1,0:T(8,128)(2,1)S(1)} %get-tuple-element.69), channel_id=1, source_target_pairs={{0,64},{64,128},{128,192},{192,0},{1,65},{65,129},{129,193},{193,1... | collective-permute-start | bytes 1572872 | tf_op jit(solution)/shard_map/ppermute | solution.py:365
  100.8 18.4 %collective-permute-start.16 = (bf16[256,1024]{1,0:T(8,128)(2,1)S(1)}, bf16[256,1024]{1,0:T(8,128)(2,1)S(1)}, u32[]{:S(2)}, u32[]{:S(2)}) collective-permute-start(bf16[256,1024]{1,0:T(8,128)(2,1)S(1)} %get-tuple-element.70), channel_id=1, source_target_pairs={{0,192},{64,0},{128,64},{192,128},{1,193},{65,1},{129,65},{193,129... | collective-permute-start | bytes 1572872 | tf_op jit(solution)/shard_map/ppermute | solution.py:368
  113.2 13.2 %collective-permute-start.4 = (bf16[2,2,4,4,16,128]{5,4,3,2,1,0:T(8,128)(2,1)S(1)}, bf16[2,2,4,4,16,128]{5,4,3,2,1,0:T(8,128)(2,1)S(1)}, u32[]{:S(2)}, u32[]{:S(2)}) collective-permute-start(bf16[2,2,4,4,16,128]{5,4,3,2,1,0:T(8,128)(2,1)S(1)} %get-tuple-element.50), channel_id=1, source_target_pairs={{0,16},{4,20},{8,24},{12,28},{16,0},{20,4},{24,8},{28,12},{32,48},... | collective-permute-start | bytes 786440 | tf_op jit(solution)/shard_map/ppermute | solution.py:401
  120.2 21.5 %all-to-all-start.4 = ((bf16[4,256,256]{2,1,0:T(8,128)(2,1)}), bf16[4,256,256]{2,1,0:T(8,128)(2,1)S(1)}, u32[]{:S(2)}, u32[]{:S(2)}) async-start(bf16[4,256,256]{2,1,0:T(8,128)(2,1)} %shard_map.99), calls=%async_computation.4 | async-start | bytes 1048576 | tf_op jit(solution)/shard_map/all_to_all | solution.py:371
  126.4 5.1 %collective-permute-start.5 = (bf16[1,2,4,4,16,128]{5,4,3,2,1,0:T(8,128)(2,1)S(1)}, bf16[1,2,4,4,16,128]{5,4,3,2,1,0:T(8,128)(2,1)S(1)}, u32[]{:S(2)}, u32[]{:S(2)}) collective-permute-start(bf16[1,2,4,4,16,128]{5,4,3,2,1,0:T(8,128)(2,1)S(1)} %get-tuple-element.52), channel_id=1, source_target_pairs={{0,8},{4,12},{8,0},{12,4},{16,24},{20,28},{24,16},{28,20},{32,40},... | collective-permute-start | bytes 393224 | tf_op jit(solution)/shard_map/ppermute | solution.py:401
  132.1 4.0 %collective-permute-start.8 = (bf16[2,4,16,128]{3,2,1,0:T(8,128)(2,1)S(1)}, bf16[2,4,16,128]{3,2,1,0:T(8,128)(2,1)S(1)}, u32[]{:S(2)}, u32[]{:S(2)}) collective-permute-start(bf16[2,4,16,128]{3,2,1,0:T(8,128)(2,1)S(1)} %get-tuple-element.56), channel_id=1, source_target_pairs={{0,192},{64,0},{128,64},{192,128},{1,193},{65,1},{129,65},{193,129... | collective-permute-start | bytes 98312 | tf_op jit(solution)/shard_map/ppermute | solution.py:368
  132.4 5.4 %collective-permute-start.7 = (bf16[2,4,16,128]{3,2,1,0:T(8,128)(2,1)S(1)}, bf16[2,4,16,128]{3,2,1,0:T(8,128)(2,1)S(1)}, u32[]{:S(2)}, u32[]{:S(2)}) collective-permute-start(bf16[2,4,16,128]{3,2,1,0:T(8,128)(2,1)S(1)} %get-tuple-element.55), channel_id=1, source_target_pairs={{0,128},{64,192},{128,0},{192,64},{1,129},{65,193},{129,1},{193,65... | collective-permute-start | bytes 98312 | tf_op jit(solution)/shard_map/ppermute | solution.py:404
  135.1 5.1 %collective-permute-start.6 = (bf16[2,4,16,128]{3,2,1,0:T(8,128)(2,1)S(1)}, bf16[2,4,16,128]{3,2,1,0:T(8,128)(2,1)S(1)}, u32[]{:S(2)}, u32[]{:S(2)}) collective-permute-start(bf16[2,4,16,128]{3,2,1,0:T(8,128)(2,1)S(1)} %get-tuple-element.54), channel_id=1, source_target_pairs={{0,64},{64,128},{128,192},{192,0},{1,65},{65,129},{129,193},{193,1... | collective-permute-start | bytes 98312 | tf_op jit(solution)/shard_map/ppermute | solution.py:365

commit v3 on v1

--- a/solution.py
+++ b/solution.py
@@ -13,6 +13,7 @@
 NN = (((1,), (0,)), ((), ()))
 TN = (((0,), (0,)), ((), ()))
 CHUNKS = 2
+GROUPED = (1, 3)
 
 
 def dot(a, b, dims):
@@ -123,28 +124,38 @@
     )(scalars, src_len, tgt_len, *held(mine, mate, kv))
 
 
-def terms_of(grads, w_ref, place, part):
+def terms_of(grads, w_ref, place):
     terms = None
+    part = w_ref.shape[1] // 4
     at = pl.ds(pl.multiple_of(place * part, part), part)
     for r in range(grads.shape[0]):
         term = dot(grads[r], w_ref[r, at, :], NT)
         terms = term if terms is None else terms + term
-    return terms
-
-
-def backward_kernel(scalars, src_len, kv_ref, qc_ref, stat_ref, w_hbm, keep_ref, give_ref, grads, w_ref, *rest):
-    far_refs, w_sem = rest[:-1], rest[-1]
-    take = pltpu.make_async_copy(w_hbm, w_ref, w_sem)
-    take.start()
-    layers, count, _ = kv_ref.shape
-    _, _, samples, rows, head = qc_ref.shape
+    return low(terms)
+
+
+def backward_kernel(start, keys, scalars, src_len, kv_ref, qc_ref, stat_ref, w_in,
+                    keep_ref, give_ref, grads, up_ref, down_ref, *rest):
+    layers, _, _ = kv_ref.shape
+    rows, head = qc_ref.shape[3:]
     shards = stat_ref.shape[0]
-    keys = count // samples
+    samples = keep_ref.shape[3]
     scale = head ** (-0.5)
     seat = scalars[0]
     even = scalars[1] == 0
-
-    def one(b, carry):
+    takes = []
+    if rest:
+        w_ref, w_sem = rest
+        part = w_ref.shape[1] // 4
+        for k in range(4):
+            at = pl.ds(pl.multiple_of(scalars[4 + k] * part, part), part)
+            takes.append(pltpu.make_async_copy(w_in.at[:, at], w_ref.at[:, at], w_sem.at[k]))
+            takes[k].start()
+    else:
+        w_ref = w_in
+
+    def one(k, carry):
+        b = start + k
         stat = stat_ref[:, b]
         lse = stat[:, :layers]
         top = jnp.max(lse, axis=0)
@@ -152,9 +163,10 @@
         inverse = 1.0 / jnp.sum(weight, axis=0)
         delta = jnp.sum(weight * stat[:, layers:], axis=0) * inverse
         down_live = seat * keys + lax.broadcasted_iota(jnp.int32, (keys, rows), 0) < src_len[b]
-        at = pl.ds(pl.multiple_of(b * keys, keys), keys)
+        taken = pl.ds(pl.multiple_of(b * keys, keys), keys)
+        at = pl.ds(pl.multiple_of(k * keys, keys), keys)
         for r in range(layers):
-            pair = kv_ref[r, at, :]
+            pair = kv_ref[r, taken, :]
             key, value = pair[:, :head], pair[:, head:]
             query, grad = qc_ref[0, r, b], qc_ref[1, r, b]
             scores = jnp.where(down_live, dot(key, query, NT) * scale, masked_score)
@@ -165,79 +177,121 @@
             grads[r, at, head:] = low(dot(prob, grad, NN))
             for kind, out in enumerate((dot(prob, value, TN), dot(slope, key, TN) * scale)):
                 out = out.reshape(shards // 2, 2, rows // shards, head)
-                keep_ref[:, kind, r, b] = low(jnp.where(even, out[:, 0], out[:, 1]))
-                give_ref[:, kind, r, b] = low(jnp.where(even, out[:, 1], out[:, 0]))
+                keep_ref[:, kind, r, k] = low(jnp.where(even, out[:, 0], out[:, 1]))
+                give_ref[:, kind, r, k] = low(jnp.where(even, out[:, 1], out[:, 0]))
         return carry
 
     lax.fori_loop(0, samples, one, 0)
-    take.wait()
-    terms = low(terms_of(grads, w_ref, scalars[4], w_ref.shape[1] // 4))
-    size = far_refs[0].shape[0]
-    for k, ref in enumerate(far_refs):
-        ref[...] = terms[k * size:(k + 1) * size]
-
-
-def backward(scalars, src_len, kv, qc, stats, weights):
+    for take in takes[:1]:
+        take.wait()
+    terms = terms_of(grads, w_ref, scalars[4])
+    half = keys // 2
+    for k in range(samples):
+        up_ref[k * half:(k + 1) * half] = terms[k * keys:k * keys + half]
+        down_ref[k * half:(k + 1) * half] = terms[k * keys + half:(k + 1) * keys]
+    for take in takes[1:]:
+        take.wait()
+
+
+def backward(chunk, scalars, src_len, kv, qc, stats, weights):
     _, layers, samples, rows, head = qc.shape
     shards = stats.shape[0]
-    part = weights.shape[1] // 4
+    keys = kv.shape[1] // samples
+    samples = samples // CHUNKS
     half = kept_here(shards // 2, 2, layers, samples, rows // shards, head)
-    far = kept_here(kv.shape[1] // (2 * CHUNKS), part)
-    outs = (half, half, kept_here(*kv.shape), kept_here(*weights.shape)) + (far,) * (2 * CHUNKS)
-    return pl.pallas_call(
-        backward_kernel,
+    far = kept_here(samples * keys // 2, weights.shape[1] // 4)
+    outs = (half, half, kept_here(layers, samples * keys, kv.shape[2]), far, far)
+    scratch = []
+    if chunk == 0:
+        outs += (kept_here(*weights.shape),)
+        scratch = [pltpu.SemaphoreType.DMA((4,))]
+        weights = in_hbm(weights)
+    else:
+        (weights,) = held(weights)
+    return pl.pallas_call(
+        functools.partial(backward_kernel, chunk * samples, keys),
         out_shape=outs,
-        in_specs=[SCALAR] * 2 + [FAST] * 3 + [SLOW],
+        in_specs=[SCALAR] * 2 + [FAST] * 3 + [FAST if chunk else SLOW],
         out_specs=(FAST,) * len(outs),
-        scratch_shapes=[pltpu.SemaphoreType.DMA],
-        compiler_params=ROOM,
-        name="backward",
-    )(scalars, src_len, *held(kv, qc, stats), in_hbm(weights))
-
-
-def near_kernel(scalars, grads, w_ref, *outs):
-    size = outs[0].shape[0]
+        scratch_shapes=scratch,
+        compiler_params=ROOM,
+    )(scalars, src_len, *held(kv, qc, stats), weights)
+
+
+def near_kernel(scalars, *refs):
+    grads, w_ref, outs = refs[:CHUNKS], refs[CHUNKS], refs[CHUNKS + 1:]
+    groups = len(outs) // 2
     for side in range(2):
-        terms = low(terms_of(grads, w_ref, scalars[5 + side], w_ref.shape[1] // 4))
-        for k in range(CHUNKS):
-            outs[side * CHUNKS + k][...] = terms[k * size:(k + 1) * size]
-
-
-def near(scalars, grads, weights):
-    outs = (kept_here(grads.shape[1] // CHUNKS, weights.shape[1] // 4),) * (2 * CHUNKS)
-    return pl.pallas_call(
-        near_kernel, out_shape=outs, in_specs=[SCALAR, FAST, FAST], out_specs=(FAST,) * len(outs), compiler_params=ROOM, name="near"
-    )(scalars, *held(grads, weights))
-
-
-def here_kernel(scalars, grads, w_ref, out_ref):
-    out_ref[...] = low(terms_of(grads, w_ref, scalars[7], w_ref.shape[1] // 4))
+        done = 0
+        terms = [terms_of(g, w_ref, scalars[5 + side]) for g in grads]
+        size = terms[0].shape[0]
+        for k in range(groups):
+            ref = outs[side * groups + k]
+            filled = 0
+            while filled < ref.shape[0]:
+                chunk, at = divmod(done + filled, size)
+                count = min(ref.shape[0] - filled, size - at)
+                ref[filled:filled + count] = terms[chunk][at:at + count]
+                filled += count
+            done += filled
+
+
+def near(scalars, grads, weights, keys):
+    outs = tuple(kept_here(g * keys, weights.shape[1] // 4) for g in GROUPED) * 2
+    return pl.pallas_call(
+        near_kernel,
+        out_shape=outs,
+        in_specs=[SCALAR] + [FAST] * (len(grads) + 1),
+        out_specs=(FAST,) * len(outs),
+        compiler_params=ROOM,
+        name="near",
+    )(scalars, *held(*grads, weights))
+
+
+def here_kernel(scalars, *refs):
+    grads, w_ref, out_ref = refs[:-2], refs[-2], refs[-1]
+    size = grads[0].shape[1]
+    for k, part in enumerate(grads):
+        out_ref[k * size:(k + 1) * size] = terms_of(part, w_ref, scalars[7])
 
 
 def here(scalars, grads, weights):
+    count = sum(g.shape[1] for g in grads)
     return pl.pallas_call(
         here_kernel,
-        out_shape=kept_here(grads.shape[1], weights.shape[1] // 4),
-        in_specs=[SCALAR, FAST, FAST],
+        out_shape=kept_here(count, weights.shape[1] // 4),
+        in_specs=[SCALAR] + [FAST] * (len(grads) + 1),
         out_specs=FAST,
         compiler_params=ROOM,
         name="here",
-    )(scalars, *held(grads, weights))
-
-
-def halve_kernel(side, kept, came, keep_ref, give_ref):
-    count = keep_ref.shape[0]
-    mine = pl.ds(side[0] * count, count)
-    other = pl.ds((1 - side[0]) * count, count)
-    keep_ref[...] = low(wide(kept[mine]) + wide(came[mine]))
-    give_ref[...] = low(wide(kept[other]) + wide(came[other]))
-
-
-def halve(side, kept, came):
-    out = kept_here(kept.shape[0] // 2, *kept.shape[1:])
-    return pl.pallas_call(
-        halve_kernel, out_shape=(out, out), in_specs=[SCALAR, FAST, FAST], out_specs=(FAST, FAST), compiler_params=ROOM
-    )(side.reshape(1), *held(kept, came))
+    )(scalars, *held(*grads, weights))
+
+
+def halve_kernel(parts, run, side, *refs):
+    kept, came = refs[:parts], refs[parts:2 * parts]
+    keep_ref, give_ref = refs[2 * parts:]
+    size = keep_ref.shape[3] // parts
+    for start in range(0, keep_ref.shape[0], run):
+        mine = pl.ds(2 * start + side[0] * run, run)
+        other = pl.ds(2 * start + (1 - side[0]) * run, run)
+        to = slice(start, start + run)
+        for k in range(parts):
+            at = slice(k * size, (k + 1) * size)
+            keep_ref[to, :, :, at] = low(wide(kept[k][mine]) + wide(came[k][mine]))
+            give_ref[to, :, :, at] = low(wide(kept[k][other]) + wide(came[k][other]))
+
+
+def halve(side, kept, came, run):
+    parts = len(kept)
+    count, kinds, layers, samples, rows, head = kept[0].shape
+    out = kept_here(count // 2, kinds, layers, samples * parts, rows, head)
+    return pl.pallas_call(
+        functools.partial(halve_kernel, parts, run),
+        out_shape=(out, out),
+        in_specs=[SCALAR] + [FAST] * (2 * parts),
+        out_specs=(FAST, FAST),
+        compiler_params=ROOM,
+    )(side.reshape(1), *held(*kept, *came))
 
 
 def deal_kernel(scalars, kept, came, *outs):
@@ -254,33 +308,47 @@
     )(scalars, *held(kept, came))
 
 
-def pass_kernel(up_in, down_in, from_down, from_up, up_ref, down_ref):
-    half = from_down.shape[0]
-    up_ref[:half] = low(wide(up_in[:half]) + wide(from_down[...]))
-    down_ref[half:] = low(wide(down_in[half:]) + wide(from_up[...]))
-    up_ref[half:] = up_in[half:]
-    down_ref[:half] = down_in[:half]
-
-
-def pass_on(up_in, down_in, from_down, from_up):
+def pass_kernel(keys, start, up_in, down_in, *refs):
+    ups, downs = refs[:(len(refs) - 2) // 2], refs[(len(refs) - 2) // 2:-2]
+    up_ref, down_ref = refs[-2:]
+    half = keys // 2
+    per = ups[0].shape[0] // half
+    first = start // per
+    for k in range(up_in.shape[0] // keys):
+        chunk, place = divmod(start + k, per)
+        came = slice(place * half, (place + 1) * half)
+        top, bottom = slice(k * keys, k * keys + half), slice(k * keys + half, (k + 1) * keys)
+        up_ref[top] = low(wide(up_in[top]) + wide(ups[chunk - first][came]))
+        down_ref[bottom] = low(wide(down_in[bottom]) + wide(downs[chunk - first][came]))
+        up_ref[bottom] = up_in[bottom]
+        down_ref[top] = down_in[top]
+
+
+def pass_on(keys, start, up_in, down_in, ups, downs):
+    per = ups[0].shape[0] // (keys // 2)
+    last = (start + up_in.shape[0] // keys - 1) // per
+    ups, downs = ups[start // per:last + 1], downs[start // per:last + 1]
     out = kept_here(*up_in.shape)
     return pl.pallas_call(
-        pass_kernel, out_shape=(out, out), in_specs=[FAST] * 4, out_specs=(FAST, FAST), compiler_params=ROOM
-    )(*held(up_in, down_in, from_down, from_up))
-
-
-def gather_kernel(chunk, own, from_down, from_up, out_ref):
+        functools.partial(pass_kernel, keys, start),
+        out_shape=(out, out),
+        in_specs=[FAST] * (2 + 2 * len(ups)),
+        out_specs=(FAST, FAST),
+        compiler_params=ROOM,
+    )(*held(up_in, down_in, *ups, *downs))
+
+
+def gather_kernel(start, own, from_down, from_up, out_ref):
     heads, count, part = out_ref.shape
     for h in range(heads):
         at = slice(h * part, (h + 1) * part)
-        mine = own[chunk * count:(chunk + 1) * count, at]
-        out_ref[h] = low(wide(mine) + wide(from_down[:, at]) + wide(from_up[:, at]))
-
-
-def gather(own, from_down, from_up, heads, chunk):
+        out_ref[h] = low(wide(own[start:start + count, at]) + wide(from_down[:, at]) + wide(from_up[:, at]))
+
+
+def gather(start, own, from_down, from_up, heads):
     count, width = from_down.shape
     return pl.pallas_call(
-        functools.partial(gather_kernel, chunk),
+        functools.partial(gather_kernel, start),
         out_shape=kept_here(heads, count, width // heads),
         in_specs=[FAST] * 3,
         out_specs=FAST,
@@ -290,19 +358,19 @@
 
 def finish_kernel(*refs):
     out_ref = refs[-1]
-    count = out_ref.shape[0] // (len(refs) - 1)
-    for c, ref in enumerate(refs[:-1]):
+    start = 0
+    for ref in refs[:-1]:
         total = wide(ref[0])
         for h in range(1, ref.shape[0]):
             total = total + wide(ref[h])
-        out_ref[c * count:(c + 1) * count] = low(total)
+        out_ref[start:start + ref.shape[1]] = low(total)
+        start += ref.shape[1]
 
 
 def finish(pieces):
-    _, count, part = pieces[0].shape
     return pl.pallas_call(
         finish_kernel,
-        out_shape=bf(count * len(pieces), part),
+        out_shape=bf(sum(p.shape[1] for p in pieces), pieces[0].shape[2]),
         in_specs=[FAST] * len(pieces),
         out_specs=FAST,
         compiler_params=ROOM,
@@ -351,23 +419,32 @@
     stats = swap(stats, "seq")
 
     heads = lax.axis_size("head")
-    kept, give, grads, weights, *far = backward(scalars, src_len, kv, qc, stats, w_kv)
-    passed = [(up(far[2 * c]), down(far[2 * c + 1])) for c in range(CHUNKS)]
-    sides = near(scalars, grads, weights)
+    weights = w_kv
+    kept, came, grads, ups, downs = [], [], [], [], []
+    for c in range(CHUNKS):
+        keep, give, part, far_up, far_down, *copied = backward(c, scalars, src_len, kv, qc, stats, weights)
+        weights = copied[0] if copied else weights
+        ups.append(up(far_up))
+        downs.append(down(far_down))
+        came.append(lax.ppermute(give, "seq", flip(shards, 1)))
+        kept.append(keep)
+        grads.append(part)
+    sides = near(scalars, grads, weights, src_rows)
     own = here(scalars, grads, weights)
     pieces = []
-    for c in range(CHUNKS):
-        to_up, to_down = pass_on(sides[c], sides[CHUNKS + c], *passed[c])
+    start = 0
+    for c, group in enumerate(GROUPED):
+        to_up, to_down = pass_on(src_rows, start, sides[c], sides[len(GROUPED) + c], ups, downs)
         to_up, to_down = up(to_up), down(to_down)
-        joined = gather(own, to_up, to_down, heads, c)
+        joined = gather(start * src_rows, own, to_up, to_down, heads)
         pieces.append(swap(joined, "head"))
+        start += group
     source_grads = finish(pieces).reshape(samples, src_rows, cols)
 
-    for stage, bit in enumerate((0, 3, 2, 1)):
-        if stage:
-            kept, give = halve(bits[bit].astype(jnp.int32), kept, came)
-        came = lax.ppermute(give, "seq", flip(shards, 1 << bit))
-    own, to_up, to_far, to_down = deal(scalars, kept, came)
+    for bit, run in ((1, 1), (3, 2), (2, 1)):
+        keep, give = halve(bits[bit].astype(jnp.int32), kept, came, run)
+        kept, came = [keep], [lax.ppermute(give, "seq", flip(shards, 1 << bit))]
+    own, to_up, to_far, to_down = deal(scalars, kept[0], came[0])
     from_down, from_up = up(to_up), down(to_down)
     from_far = lax.ppermute(to_far, "section", turn(4, 2))
     ring = jnp.stack([own, from_down, from_far, from_up])

time: 136 us -> 152 us (1.12)
  the two profiles are of different devices: /device:TPU:64 before, /device:TPU:56 now
where the time goes in v3:
time: 152 us; the launch traced here: 151 us
  waiting for transfers between devices  63.5 us (42%)
  starting transfers between devices  33.1 us (22%)
  Pallas kernels  31 us (20%)
  blocking collectives  15 us (10%)
  local copies, waits for them, and re-layouts  6.14 us (4%)
    ppermute x5, waiting for transfers between devices, down(): return lax.ppermute(a, 'section', turn(4, 3))  24.2 us
    ppermute x3, waiting for transfers between devices, body(): kept, came = ([keep], [lax.ppermute(give, 'seq', flip(shards, 1 << bit))])  23.8 us
    all_to_all x3, starting transfers between devices, swap(): return lax.all_to_all(a, axis, 0, 0, tiled=True)  15.9 us
    all_to_all x1, blocking collectives, swap(): return lax.all_to_all(a, axis, 0, 0, tiled=True)  15 us
    ppermute x5, starting transfers between devices, up(): return lax.ppermute(a, 'section', turn(4, 1))  9.08 us
    all_to_all x3, waiting for transfers between devices, swap(): return lax.all_to_all(a, axis, 0, 0, tiled=True)  8.83 us
    pallas_call x2, Pallas kernels, backward(): pl.pallas_call(functools.partial(backward_kernel, chunk * samples, keys),...  8.6 us
    pallas_call x1, Pallas kernels, project(): pl.pallas_call(project_kernel, out_shape=kept_here(layers, count, cols),...  8.29 us
  transfers between devices with their start and end apart: 20, of which 12 were waited for; matrix products, arithmetic and copies ran while one was open for 1% of the time, Pallas kernels for 15%

profile of v3, /device:TPU:56, one launch (start us, length us, event | category | flops | bytes accessed | tf_op | source)
XLA Modules:
  0.0 150.7 jit_solution(3809167598211883309)
XLA Ops:
  0.6 1.6 %constant_dynamic-slice_fusion = (bf16[1,4,128,4,128]{4,3,2,1,0:T(4,128)(2,1)S(1)}, bf16[1,4,128,4,128]{4,3,2,1,0:T(4,128)(2,1)S(1)}) fusion(bf16[1,4,256,4,128]{4,3,2,1,0:T(4,128)(2,1)} %param.9, s32[]{:T(128)S(6)} %select_n.86, bf16[1,4,256,4,128]{4,3,2,1,0:T(4,128)(2,1)} %param.8), kind=kLoop, calls=%fused_computation.9 | loop fusion | bytes 2097156 | tf_op jit(solution)/shard_map/dynamic_slice | solution.py:412
  2.2 0.1 copy.17
  2.3 0.1 copy.18
  2.4 1.1 pad_maximum_fusion
  3.5 4.8 %all-to-all-start = ((bf16[4,2,4,128,128]{4,3,2,1,0:T(8,128)(2,1)}), bf16[4,2,4,128,128]{4,3,2,1,0:T(8,128)(2,1)S(1)}, u32[]{:S(2)}, u32[]{:S(2)}) async-start(bf16[4,2,4,128,128]{4,3,2,1,0:T(8,128)(2,1)} %pad_maximum_fusion), calls=%async_computation | async-start | bytes 2097152 | tf_op jit(solution)/shard_map/all_to_all | solution.py:409
  8.3 8.3 %project.1.kv_ref = bf16[4,512,256]{2,1,0:T(8,128)(2,1)S(1)} custom-call(bf16[512,4096]{1,0:T(8,128)(2,1)} %bitcast.39, bf16[4,4096,256]{2,1,0:T(8,128)(2,1)} %w_in.1), custom_call_target="tpu_custom_call" | custom-call | tf_op jit(solution)/shard_map/project/pallas_call | solution.py:60
  16.6 4.7 %all-to-all-done.mine = bf16[4,2,4,128,128]{4,3,2,1,0:T(8,128)(2,1)S(1)} async-done(((bf16[4,2,4,128,128]{4,3,2,1,0:T(8,128)(2,1)}), bf16[4,2,4,128,128]{4,3,2,1,0:T(8,128)(2,1)S(1)}, u32[]{:S(2)}, u32[]{:S(2)}) %all-to-all-start) | async-done | bytes 1048608 | tf_op jit(solution)/shard_map/all_to_all | solution.py:409
  21.5 2.6 %collective-permute-done.mate = bf16[4,2,4,128,128]{4,3,2,1,0:T(8,128)(2,1)S(1)} collective-permute-done((bf16[4,2,4,128,128]{4,3,2,1,0:T(8,128)(2,1)S(1)}, bf16[4,2,4,128,128]{4,3,2,1,0:T(8,128)(2,1)S(1)}, u32[]{:S(2)}, u32[]{:S(2)}) %collective-permute-start) | collective-permute-done | bytes 1048608 | tf_op jit(solution)/shard_map/ppermute | solution.py:417
  24.0 2.2 %forward.1 = (bf16[2,4,4,256,128]{4,3,2,1,0:T(8,128)(2,1)S(1)}, f32[16,4,8,256]{3,2,1,0:T(8,128)S(1)}) custom-call(s32[12]{0:T(128)S(1)} %stack.84.scalars, s32[4]{0:T(128)S(1)} %copy-done.4, s32[4]{0:T(128)S(1)} %copy-done.5, bf16[4,2,4,128,128]{4,3,2,1,0:T(8,128)(2,1)S(1)} %all-to-all-done.mine, ...), custom_call_target="tpu_custom_call" | custom-call | tf_op jit(solution)/shard_map/forward/pallas_call | solution.py:114
  26.2 15.0 %all_to_all.20.stat_ref = f32[16,4,8,256]{3,2,1,0:T(8,128)S(1)} all-to-all(f32[16,4,8,256]{3,2,1,0:T(8,128)S(1)} %get-tuple-element.39), channel_id=1, replica_groups=mesh['section'=4,'seq'=16,'head'=4] {'seq'}, dimensions={0} | all-to-all | bytes 1048576 | tf_op jit(solution)/shard_map/all_to_all | solution.py:409
  41.3 4.8 %shard_map.85 = (bf16[8,2,4,2,16,128]{5,4,3,2,1,0:T(8,128)(2,1)S(1)}, bf16[8,2,4,2,16,128]{5,4,3,2,1,0:T(8,128)(2,1)}, bf16[4,256,256]{2,1,0:T(8,128)(2,1)S(1)},...) custom-call(s32[12]{0:T(128)S(1)} %stack.84.scalars, ...), custom_call_target="tpu_custom_call" | custom-call | tf_op jit(solution)/shard_map/pallas_call | solution.py:211
  46.1 2.1 %collective-permute-start.9 = (bf16[128,1024]{1,0:T(8,128)(2,1)S(1)}, bf16[128,1024]{1,0:T(8,128)(2,1)S(1)}, u32[]{:S(2)}, u32[]{:S(2)}) collective-permute-start(bf16[128,1024]{1,0:T(8,128)(2,1)S(1)} %get-tuple-element.59), channel_id=1, source_target_pairs={{0,64},{64,128},{128,192},{192,0},{1,65},{65,129},{129,193},{193,1... | collective-permute-start | bytes 786440 | tf_op jit(solution)/shard_map/ppermute | solution.py:403
  48.3 3.8 %shard_map.86 = (bf16[8,2,4,2,16,128]{5,4,3,2,1,0:T(8,128)(2,1)S(1)}, bf16[8,2,4,2,16,128]{5,4,3,2,1,0:T(8,128)(2,1)}, bf16[4,256,256]{2,1,0:T(8,128)(2,1)S(1)},...) custom-call(s32[12]{0:T(128)S(1)} %stack.84.scalars, s32[4]{0:T(128)S(1)} %copy-done.4, ...), custom_call_target="tpu_custom_call" | custom-call | tf_op jit(solution)/shard_map/pallas_call | solution.py:211
  52.0 3.3 %collective-permute-start.13 = (bf16[128,1024]{1,0:T(8,128)(2,1)S(1)}, bf16[128,1024]{1,0:T(8,128)(2,1)S(1)}, u32[]{:S(2)}, u32[]{:S(2)}) collective-permute-start(bf16[128,1024]{1,0:T(8,128)(2,1)S(1)} %get-tuple-element.65), channel_id=1, source_target_pairs={{0,64},{64,128},{128,192},{192,0},{1,65},{65,129},{129,193},{193,1... | collective-permute-start | bytes 786440 | tf_op jit(solution)/shard_map/ppermute | solution.py:403
  55.3 2.9 %near.1 = (bf16[128,1024]{1,0:T(8,128)(2,1)S(1)}, bf16[384,1024]{1,0:T(8,128)(2,1)S(1)}, bf16[128,1024]{1,0:T(8,128)(2,1)S(1)}, bf16[384,1024]{1,0:T(8,128)(2,1)S(1)}) custom-call(s32[12]{0:T(128)S(1)} %stack.84.scalars, bf16[4,256,256]{2,1,0:T(8,128)(2,1)S(1)} %get-tuple-element.55.refs_0_, bf16[4,256,256]{2,1,0:T(8,128)(2,1)S(1)} %get-tuple-element.56.refs_1_, ...), custom_call_target="tpu_custom_call" | custom-call | tf_op jit(solution)/shard_map/near/pallas_call | solution.py:241
  58.3 3.3 %collective-permute-start.11 = (bf16[128,1024]{1,0:T(8,128)(2,1)S(1)}, bf16[128,1024]{1,0:T(8,128)(2,1)S(1)}, u32[]{:S(2)}, u32[]{:S(2)}) collective-permute-start(bf16[128,1024]{1,0:T(8,128)(2,1)S(1)} %get-tuple-element.61), channel_id=1, source_target_pairs={{0,64},{64,128},{128,192},{192,0},{1,65},{65,129},{129,193},{193,1... | collective-permute-start | bytes 786440 | tf_op jit(solution)/shard_map/ppermute | solution.py:403
  61.6 0.5 collective-permute-start.2
  62.1 1.8 %collective-permute-done.14.refs_3_ = bf16[128,1024]{1,0:T(8,128)(2,1)S(1)} collective-permute-done((bf16[128,1024]{1,0:T(8,128)(2,1)S(1)}, bf16[128,1024]{1,0:T(8,128)(2,1)S(1)}, u32[]{:S(2)}, u32[]{:S(2)}) %collective-permute-start.14) | collective-permute-done | bytes 262176 | tf_op jit(solution)/shard_map/ppermute | solution.py:406
  64.0 1.4 shard_map.92
  65.3 0.3 collective-permute-start.15
  65.6 1.7 %collective-permute-start.16 = (bf16[384,1024]{1,0:T(8,128)(2,1)}, bf16[384,1024]{1,0:T(8,128)(2,1)S(1)}, u32[]{:S(2)}, u32[]{:S(2)}) collective-permute-start(bf16[384,1024]{1,0:T(8,128)(2,1)} %get-tuple-element.68), channel_id=1, source_target_pairs={{0,192},{64,0},{128,64},{192,128},{1,193},{65,1},{129,65},{193,129... | collective-permute-start | bytes 2359304 | tf_op jit(solution)/shard_map/ppermute | solution.py:406
  67.4 0.6 collective-permute-done.11.from_down
  68.0 1.8 %here.1.own = bf16[512,1024]{1,0:T(8,128)(2,1)S(1)} custom-call(s32[12]{0:T(128)S(1)} %stack.84.scalars, bf16[4,256,256]{2,1,0:T(8,128)(2,1)S(1)} %get-tuple-element.55.refs_0_, bf16[4,256,256]{2,1,0:T(8,128)(2,1)S(1)} %get-tuple-element.56.refs_1_, bf16[4,4096,256]{2,1,0:T(8,128)(2,1)S(1)} %get-tuple-element.41.w_in.refs_2_), custom_call_target="tpu_custom_call" | custom-call | tf_op jit(solution)/shard_map/here/pallas_call | solution.py:260
  69.9 20.7 %collective-permute-done.12.from_up = bf16[128,1024]{1,0:T(8,128)(2,1)S(1)} collective-permute-done((bf16[128,1024]{1,0:T(8,128)(2,1)S(1)}, bf16[128,1024]{1,0:T(8,128)(2,1)S(1)}, u32[]{:S(2)}, u32[]{:S(2)}) %collective-permute-start.12) | collective-permute-done | bytes 262176 | tf_op jit(solution)/shard_map/ppermute | solution.py:406
  90.5 0.8 shard_map.91
  91.3 7.6 %all-to-all-start.2 = ((bf16[4,128,256]{2,1,0:T(8,128)(2,1)}), bf16[4,128,256]{2,1,0:T(8,128)(2,1)S(1)}, u32[]{:S(2)}, u32[]{:S(2)}) async-start(bf16[4,128,256]{2,1,0:T(8,128)(2,1)} %shard_map.91), calls=%async_computation.2 | async-start | bytes 524288 | tf_op jit(solution)/shard_map/all_to_all | solution.py:409
  98.9 1.0 copy-done.1
  99.9 2.2 %shard_map.87 = (bf16[4,2,4,4,16,128]{5,4,3,2,1,0:T(8,128)(2,1)S(1)}, bf16[4,2,4,4,16,128]{5,4,3,2,1,0:T(8,128)(2,1)}) custom-call(s32[1]{0:T(128)} %bitcast.7.side, bf16[8,2,4,2,16,128]{5,4,3,2,1,0:T(8,128)(2,1)S(1)} %get-tuple-element.40.refs_0_, bf16[8,2,4,2,16,128]{5,4,3,2,1,0:T(8,128)(2,1)S(1)} %copy-done.1, ...), custom_call_target="tpu_custom_call" | custom-call | tf_op jit(solution)/shard_map/pallas_call | solution.py:288
  102.1 0.8 copy-done.2
  102.9 0.1 collective-permute-start.3
  103.0 1.2 shard_map.93
  104.2 4.1 %all-to-all-done.2.refs_0_ = bf16[4,128,256]{2,1,0:T(8,128)(2,1)S(1)} async-done(((bf16[4,128,256]{2,1,0:T(8,128)(2,1)}), bf16[4,128,256]{2,1,0:T(8,128)(2,1)S(1)}, u32[]{:S(2)}, u32[]{:S(2)}) %all-to-all-start.2) | async-done | bytes 262176 | tf_op jit(solution)/shard_map/all_to_all | solution.py:409
  108.3 3.5 %all-to-all-start.3 = ((bf16[4,384,256]{2,1,0:T(8,128)(2,1)}), bf16[4,384,256]{2,1,0:T(8,128)(2,1)S(1)}, u32[]{:S(2)}, u32[]{:S(2)}) async-start(bf16[4,384,256]{2,1,0:T(8,128)(2,1)} %shard_map.93), calls=%async_computation.3 | async-start | bytes 1572864 | tf_op jit(solution)/shard_map/all_to_all | solution.py:409
  111.8 2.4 %collective-permute-done.3.refs_1_ = bf16[4,2,4,4,16,128]{5,4,3,2,1,0:T(8,128)(2,1)S(1)} collective-permute-done((bf16[4,2,4,4,16,128]{5,4,3,2,1,0:T(8,128)(2,1)}, bf16[4,2,4,4,16,128]{5,4,3,2,1,0:T(8,128)(2,1)S(1)}, u32[]{:S(2)}, u32[]{:S(2)}) %collective-permute-start.3) | collective-permute-done | bytes 524320 | tf_op jit(solution)/shard_map/ppermute | solution.py:446
  114.2 1.0 copy-done.3
  115.3 0.1 shard_map.88
  115.4 1.5 %collective-permute-start.4 = (bf16[2,2,4,4,16,128]{5,4,3,2,1,0:T(8,128)(2,1)S(1)}, bf16[2,2,4,4,16,128]{5,4,3,2,1,0:T(8,128)(2,1)S(1)}, u32[]{:S(2)}, u32[]{:S(2)}) collective-permute-start(bf16[2,2,4,4,16,128]{5,4,3,2,1,0:T(8,128)(2,1)S(1)} %get-tuple-element.48), channel_id=1, source_target_pairs={{0,32},{4,36},{8,40},{12,44},{16,48},{20,52},{24,56},{28,60},{32,0... | collective-permute-start | bytes 786440 | tf_op jit(solution)/shard_map/ppermute | solution.py:446
  116.9 17.0 %collective-permute-done.4.refs_1_ = bf16[2,2,4,4,16,128]{5,4,3,2,1,0:T(8,128)(2,1)S(1)} collective-permute-done((bf16[2,2,4,4,16,128]{5,4,3,2,1,0:T(8,128)(2,1)S(1)}, bf16[2,2,4,4,16,128]{5,4,3,2,1,0:T(8,128)(2,1)S(1)}, u32[]{:S(2)}, u32[]{:S(2)}) %collective-permute-start.4) | collective-permute-done | bytes 262176 | tf_op jit(solution)/shard_map/ppermute | solution.py:446
  134.0 2.2 %collective-permute-start.5 = (bf16[1,2,4,4,16,128]{5,4,3,2,1,0:T(8,128)(2,1)S(1)}, bf16[1,2,4,4,16,128]{5,4,3,2,1,0:T(8,128)(2,1)S(1)}, u32[]{:S(2)}, u32[]{:S(2)}) collective-permute-start(bf16[1,2,4,4,16,128]{5,4,3,2,1,0:T(8,128)(2,1)S(1)} %get-tuple-element.50), channel_id=1, source_target_pairs={{0,16},{4,20},{8,24},{12,28},{16,0},{20,4},{24,8},{28,12},{32,48},... | collective-permute-start | bytes 393224 | tf_op jit(solution)/shard_map/ppermute | solution.py:446
  136.1 4.4 %collective-permute-done.5.came = bf16[1,2,4,4,16,128]{5,4,3,2,1,0:T(8,128)(2,1)S(1)} collective-permute-done((bf16[1,2,4,4,16,128]{5,4,3,2,1,0:T(8,128)(2,1)S(1)}, bf16[1,2,4,4,16,128]{5,4,3,2,1,0:T(8,128)(2,1)S(1)}, u32[]{:S(2)}, u32[]{:S(2)}) %collective-permute-start.5) | collective-permute-done | bytes 131104 | tf_op jit(solution)/shard_map/ppermute | solution.py:446
  140.5 0.6 deal.1
  141.2 2.1 %collective-permute-start.7 = (bf16[2,4,16,128]{3,2,1,0:T(8,128)(2,1)S(1)}, bf16[2,4,16,128]{3,2,1,0:T(8,128)(2,1)S(1)}, u32[]{:S(2)}, u32[]{:S(2)}) collective-permute-start(bf16[2,4,16,128]{3,2,1,0:T(8,128)(2,1)S(1)} %get-tuple-element.53), channel_id=1, source_target_pairs={{0,128},{64,192},{128,0},{192,64},{1,129},{65,193},{129,1},{193,65... | collective-permute-start | bytes 98312 | tf_op jit(solution)/shard_map/ppermute | solution.py:449
  143.3 1.8 %collective-permute-done.6 = bf16[2,4,16,128]{3,2,1,0:T(8,128)(2,1)S(1)} collective-permute-done((bf16[2,4,16,128]{3,2,1,0:T(8,128)(2,1)S(1)}, bf16[2,4,16,128]{3,2,1,0:T(8,128)(2,1)S(1)}, u32[]{:S(2)}, u32[]{:S(2)}) %collective-permute-start.6) | collective-permute-done | bytes 32800 | tf_op jit(solution)/shard_map/ppermute | solution.py:403
  145.1 1.6 %collective-permute-done.7 = bf16[2,4,16,128]{3,2,1,0:T(8,128)(2,1)S(1)} collective-permute-done((bf16[2,4,16,128]{3,2,1,0:T(8,128)(2,1)S(1)}, bf16[2,4,16,128]{3,2,1,0:T(8,128)(2,1)S(1)}, u32[]{:S(2)}, u32[]{:S(2)}) %collective-permute-start.7) | collective-permute-done | bytes 32800 | tf_op jit(solution)/shard_map/ppermute | solution.py:449
  146.7 1.7 %collective-permute-done.8 = bf16[2,4,16,128]{3,2,1,0:T(8,128)(2,1)S(1)} collective-permute-done((bf16[2,4,16,128]{3,2,1,0:T(8,128)(2,1)S(1)}, bf16[2,4,16,128]{3,2,1,0:T(8,128)(2,1)S(1)}, u32[]{:S(2)}, u32[]{:S(2)}) %collective-permute-start.8) | collective-permute-done | bytes 32800 | tf_op jit(solution)/shard_map/ppermute | solution.py:406
  148.5 0.7 copy.14
  149.2 0.7 copy.13
  149.9 0.8 finish.1
  (31 shorter events, 0.4 us)
Async XLA Ops:
  3.5 20.5 %copy-start.4 = (s32[4]{0:T(128)S(1)}, s32[4]{0:T(128)}, u32[]{:S(2)}) copy-start(s32[4]{0:T(128)} %src_len.5) | copy-start | bytes 52
  3.5 20.5 %copy-start.5 = (s32[4]{0:T(128)S(1)}, s32[4]{0:T(128)}, u32[]{:S(2)}) copy-start(s32[4]{0:T(128)} %tgt_len.1) | copy-start | bytes 52
  3.5 17.8 %all-to-all-start = ((bf16[4,2,4,128,128]{4,3,2,1,0:T(8,128)(2,1)}), bf16[4,2,4,128,128]{4,3,2,1,0:T(8,128)(2,1)S(1)}, u32[]{:S(2)}, u32[]{:S(2)}) async-start(bf16[4,2,4,128,128]{4,3,2,1,0:T(8,128)(2,1)} %pad_maximum_fusion), calls=%async_computation | async-start | bytes 2097152 | tf_op jit(solution)/shard_map/all_to_all | solution.py:409
  21.4 2.7 %collective-permute-start = (bf16[4,2,4,128,128]{4,3,2,1,0:T(8,128)(2,1)S(1)}, bf16[4,2,4,128,128]{4,3,2,1,0:T(8,128)(2,1)S(1)}, u32[]{:S(2)}, u32[]{:S(2)}) collective-permute-start(bf16[4,2,4,128,128]{4,3,2,1,0:T(8,128)(2,1)S(1)} %all-to-all-done.mine), channel_id=1, source_target_pairs={{0,4},{4,0},{8,12},{12,8},{16,20},{20,16},{24,28},{28,24},{32,36},... | collective-permute-start | bytes 3145736 | tf_op jit(solution)/shard_map/ppermute | solution.py:417
  46.1 12.1 %collective-permute-start.9 = (bf16[128,1024]{1,0:T(8,128)(2,1)S(1)}, bf16[128,1024]{1,0:T(8,128)(2,1)S(1)}, u32[]{:S(2)}, u32[]{:S(2)}) collective-permute-start(bf16[128,1024]{1,0:T(8,128)(2,1)S(1)} %get-tuple-element.59), channel_id=1, source_target_pairs={{0,64},{64,128},{128,192},{192,0},{1,65},{65,129},{129,193},{193,1... | collective-permute-start | bytes 786440 | tf_op jit(solution)/shard_map/ppermute | solution.py:403
  48.3 10.0 %collective-permute-start.10 = (bf16[128,1024]{1,0:T(8,128)(2,1)S(1)}, bf16[128,1024]{1,0:T(8,128)(2,1)S(1)}, u32[]{:S(2)}, u32[]{:S(2)}) collective-permute-start(bf16[128,1024]{1,0:T(8,128)(2,1)S(1)} %get-tuple-element.60), channel_id=1, source_target_pairs={{0,192},{64,0},{128,64},{192,128},{1,193},{65,1},{129,65},{193,129... | collective-permute-start | bytes 786440 | tf_op jit(solution)/shard_map/ppermute | solution.py:406
  52.0 17.8 %copy-start = (bf16[8,2,4,2,16,128]{5,4,3,2,1,0:T(8,128)(2,1)}, bf16[8,2,4,2,16,128]{5,4,3,2,1,0:T(8,128)(2,1)S(1)}, u32[]{:S(2)}) copy-start(bf16[8,2,4,2,16,128]{5,4,3,2,1,0:T(8,128)(2,1)S(1)} %get-tuple-element.42.refs_1_) | copy-start | bytes 1572868
  52.0 10.1 %collective-permute-start.13 = (bf16[128,1024]{1,0:T(8,128)(2,1)S(1)}, bf16[128,1024]{1,0:T(8,128)(2,1)S(1)}, u32[]{:S(2)}, u32[]{:S(2)}) collective-permute-start(bf16[128,1024]{1,0:T(8,128)(2,1)S(1)} %get-tuple-element.65), channel_id=1, source_target_pairs={{0,64},{64,128},{128,192},{192,0},{1,65},{65,129},{129,193},{193,1... | collective-permute-start | bytes 786440 | tf_op jit(solution)/shard_map/ppermute | solution.py:403
  55.3 8.7 %collective-permute-start.14 = (bf16[128,1024]{1,0:T(8,128)(2,1)S(1)}, bf16[128,1024]{1,0:T(8,128)(2,1)S(1)}, u32[]{:S(2)}, u32[]{:S(2)}) collective-permute-start(bf16[128,1024]{1,0:T(8,128)(2,1)S(1)} %get-tuple-element.66), channel_id=1, source_target_pairs={{0,192},{64,0},{128,64},{192,128},{1,193},{65,1},{129,65},{193,129... | collective-permute-start | bytes 786440 | tf_op jit(solution)/shard_map/ppermute | solution.py:406
  58.3 9.7 %collective-permute-start.11 = (bf16[128,1024]{1,0:T(8,128)(2,1)S(1)}, bf16[128,1024]{1,0:T(8,128)(2,1)S(1)}, u32[]{:S(2)}, u32[]{:S(2)}) collective-permute-start(bf16[128,1024]{1,0:T(8,128)(2,1)S(1)} %get-tuple-element.61), channel_id=1, source_target_pairs={{0,64},{64,128},{128,192},{192,0},{1,65},{65,129},{129,193},{193,1... | collective-permute-start | bytes 786440 | tf_op jit(solution)/shard_map/ppermute | solution.py:403
  61.6 37.3 %collective-permute-start.1 = (bf16[8,2,4,2,16,128]{5,4,3,2,1,0:T(8,128)(2,1)}, bf16[8,2,4,2,16,128]{5,4,3,2,1,0:T(8,128)(2,1)}, u32[]{:S(2)}, u32[]{:S(2)}) collective-permute-start(bf16[8,2,4,2,16,128]{5,4,3,2,1,0:T(8,128)(2,1)} %get-tuple-element.43), channel_id=1, source_target_pairs={{0,4},{4,0},{8,12},{12,8},{16,20},{20,16},{24,28},{28,24},{32,36},... | collective-permute-start | bytes 1572872 | tf_op jit(solution)/shard_map/ppermute | solution.py:429
  61.6 37.3 %collective-permute-start.2 = (bf16[8,2,4,2,16,128]{5,4,3,2,1,0:T(8,128)(2,1)}, bf16[8,2,4,2,16,128]{5,4,3,2,1,0:T(8,128)(2,1)}, u32[]{:S(2)}, u32[]{:S(2)}) collective-permute-start(bf16[8,2,4,2,16,128]{5,4,3,2,1,0:T(8,128)(2,1)} %get-tuple-element.44), channel_id=1, source_target_pairs={{0,4},{4,0},{8,12},{12,8},{16,20},{20,16},{24,28},{28,24},{32,36},... | collective-permute-start | bytes 1572872 | tf_op jit(solution)/shard_map/ppermute | solution.py:429
  65.3 37.7 %collective-permute-start.15 = (bf16[384,1024]{1,0:T(8,128)(2,1)}, bf16[384,1024]{1,0:T(8,128)(2,1)S(1)}, u32[]{:S(2)}, u32[]{:S(2)}) collective-permute-start(bf16[384,1024]{1,0:T(8,128)(2,1)} %get-tuple-element.67), channel_id=1, source_target_pairs={{0,64},{64,128},{128,192},{192,0},{1,65},{65,129},{129,193},{193,1... | collective-permute-start | bytes 2359304 | tf_op jit(solution)/shard_map/ppermute | solution.py:403
  65.6 37.4 %collective-permute-start.16 = (bf16[384,1024]{1,0:T(8,128)(2,1)}, bf16[384,1024]{1,0:T(8,128)(2,1)S(1)}, u32[]{:S(2)}, u32[]{:S(2)}) collective-permute-start(bf16[384,1024]{1,0:T(8,128)(2,1)} %get-tuple-element.68), channel_id=1, source_target_pairs={{0,192},{64,0},{128,64},{192,128},{1,193},{65,1},{129,65},{193,129... | collective-permute-start | bytes 2359304 | tf_op jit(solution)/shard_map/ppermute | solution.py:406
  68.0 22.5 %collective-permute-start.12 = (bf16[128,1024]{1,0:T(8,128)(2,1)S(1)}, bf16[128,1024]{1,0:T(8,128)(2,1)S(1)}, u32[]{:S(2)}, u32[]{:S(2)}) collective-permute-start(bf16[128,1024]{1,0:T(8,128)(2,1)S(1)} %get-tuple-element.62), channel_id=1, source_target_pairs={{0,192},{64,0},{128,64},{192,128},{1,193},{65,1},{129,65},{193,129... | collective-permute-start | bytes 786440 | tf_op jit(solution)/shard_map/ppermute | solution.py:406
  91.3 17.0 %all-to-all-start.2 = ((bf16[4,128,256]{2,1,0:T(8,128)(2,1)}), bf16[4,128,256]{2,1,0:T(8,128)(2,1)S(1)}, u32[]{:S(2)}, u32[]{:S(2)}) async-start(bf16[4,128,256]{2,1,0:T(8,128)(2,1)} %shard_map.91), calls=%async_computation.2 | async-start | bytes 524288 | tf_op jit(solution)/shard_map/all_to_all | solution.py:409
  98.9 1.0 copy-start.1
  102.1 0.8 copy-start.2
  102.9 11.3 %collective-permute-start.3 = (bf16[4,2,4,4,16,128]{5,4,3,2,1,0:T(8,128)(2,1)}, bf16[4,2,4,4,16,128]{5,4,3,2,1,0:T(8,128)(2,1)S(1)}, u32[]{:S(2)}, u32[]{:S(2)}) collective-permute-start(bf16[4,2,4,4,16,128]{5,4,3,2,1,0:T(8,128)(2,1)} %get-tuple-element.46), channel_id=1, source_target_pairs={{0,8},{4,12},{8,0},{12,4},{16,24},{20,28},{24,16},{28,20},{32,40},... | collective-permute-start | bytes 1572872 | tf_op jit(solution)/shard_map/ppermute | solution.py:446
  108.3 41.6 %all-to-all-start.3 = ((bf16[4,384,256]{2,1,0:T(8,128)(2,1)}), bf16[4,384,256]{2,1,0:T(8,128)(2,1)S(1)}, u32[]{:S(2)}, u32[]{:S(2)}) async-start(bf16[4,384,256]{2,1,0:T(8,128)(2,1)} %shard_map.93), calls=%async_computation.3 | async-start | bytes 1572864 | tf_op jit(solution)/shard_map/all_to_all | solution.py:409
  114.2 1.0 copy-start.3
  115.4 18.5 %collective-permute-start.4 = (bf16[2,2,4,4,16,128]{5,4,3,2,1,0:T(8,128)(2,1)S(1)}, bf16[2,2,4,4,16,128]{5,4,3,2,1,0:T(8,128)(2,1)S(1)}, u32[]{:S(2)}, u32[]{:S(2)}) collective-permute-start(bf16[2,2,4,4,16,128]{5,4,3,2,1,0:T(8,128)(2,1)S(1)} %get-tuple-element.48), channel_id=1, source_target_pairs={{0,32},{4,36},{8,40},{12,44},{16,48},{20,52},{24,56},{28,60},{32,0... | collective-permute-start | bytes 786440 | tf_op jit(solution)/shard_map/ppermute | solution.py:446
  134.0 6.6 %collective-permute-start.5 = (bf16[1,2,4,4,16,128]{5,4,3,2,1,0:T(8,128)(2,1)S(1)}, bf16[1,2,4,4,16,128]{5,4,3,2,1,0:T(8,128)(2,1)S(1)}, u32[]{:S(2)}, u32[]{:S(2)}) collective-permute-start(bf16[1,2,4,4,16,128]{5,4,3,2,1,0:T(8,128)(2,1)S(1)} %get-tuple-element.50), channel_id=1, source_target_pairs={{0,16},{4,20},{8,24},{12,28},{16,0},{20,4},{24,8},{28,12},{32,48},... | collective-permute-start | bytes 393224 | tf_op jit(solution)/shard_map/ppermute | solution.py:446
  141.1 4.0 %collective-permute-start.6 = (bf16[2,4,16,128]{3,2,1,0:T(8,128)(2,1)S(1)}, bf16[2,4,16,128]{3,2,1,0:T(8,128)(2,1)S(1)}, u32[]{:S(2)}, u32[]{:S(2)}) collective-permute-start(bf16[2,4,16,128]{3,2,1,0:T(8,128)(2,1)S(1)} %get-tuple-element.52), channel_id=1, source_target_pairs={{0,64},{64,128},{128,192},{192,0},{1,65},{65,129},{129,193},{193,1... | collective-permute-start | bytes 98312 | tf_op jit(solution)/shard_map/ppermute | solution.py:403
  141.2 5.5 %collective-permute-start.7 = (bf16[2,4,16,128]{3,2,1,0:T(8,128)(2,1)S(1)}, bf16[2,4,16,128]{3,2,1,0:T(8,128)(2,1)S(1)}, u32[]{:S(2)}, u32[]{:S(2)}) collective-permute-start(bf16[2,4,16,128]{3,2,1,0:T(8,128)(2,1)S(1)} %get-tuple-element.53), channel_id=1, source_target_pairs={{0,128},{64,192},{128,0},{192,64},{1,129},{65,193},{129,1},{193,65... | collective-permute-start | bytes 98312 | tf_op jit(solution)/shard_map/ppermute | solution.py:449
  143.3 5.1 %collective-permute-start.8 = (bf16[2,4,16,128]{3,2,1,0:T(8,128)(2,1)S(1)}, bf16[2,4,16,128]{3,2,1,0:T(8,128)(2,1)S(1)}, u32[]{:S(2)}, u32[]{:S(2)}) collective-permute-start(bf16[2,4,16,128]{3,2,1,0:T(8,128)(2,1)S(1)} %get-tuple-element.54), channel_id=1, source_target_pairs={{0,192},{64,0},{128,64},{192,128},{1,193},{65,1},{129,65},{193,129... | collective-permute-start | bytes 98312 | tf_op jit(solution)/shard_map/ppermute | solution.py:406

commit v4 on v3

--- a/solution.py
+++ b/solution.py
@@ -71,28 +71,33 @@
     )(in_hbm(rows), in_hbm(w_kv))
 
 
-def forward_kernel(scalars, src_len, tgt_len, mine, mate, kv_ref, qc_ref, stat_ref):
+def key_places(seat, keys, targets):
+    at = lax.broadcasted_iota(jnp.int32, (2 * keys, targets), 0)
+    other = seat + 1 - 2 * lax.rem(seat, 2)
+    return at + jnp.where(at < keys, seat * keys, other * keys - keys)
+
+
+def live_targets(core, targets, block, head, limit):
+    at = lax.broadcasted_iota(jnp.int32, (targets, head), 0)
+    return (at // block) * (2 * block) + core * block + lax.rem(at, block) < limit
+
+
+def forward_kernel(block, scalars, src_len, tgt_len, mine, kv_ref, mate_ref, stat_ref):
     seat, core = scalars[0], scalars[1]
     layers, count, _ = kv_ref.shape
-    _, _, samples, rows, head = qc_ref.shape
-    shards = stat_ref.shape[0]
+    _, _, samples, rows, head = mine.shape
     keys = count // samples
     scale = head ** (-0.5)
-    first = core == 0
 
     def one(b, carry):
-        live = lax.broadcasted_iota(jnp.int32, (rows, head), 0) < tgt_len[b]
-        key_live = seat * keys + lax.broadcasted_iota(jnp.int32, (keys, rows), 0) < src_len[b]
+        live = live_targets(core, rows, block, head, tgt_len[b])
+        key_live = key_places(seat, keys, rows) < src_len[b]
+        at = pl.ds(pl.multiple_of(b * keys, keys), keys)
         tops, deltas = [], []
         for r in range(layers):
-            whole = []
-            for kind in range(2):
-                a, c = wide(mine[r, kind, b]), wide(mate[r, kind, b])
-                whole.append(jnp.concatenate([jnp.where(first, a, c), jnp.where(first, c, a)], axis=0))
-            query, grad = low(whole[0]), low(jnp.where(live, whole[1], 0.0))
-            qc_ref[0, r, b] = query
-            qc_ref[1, r, b] = grad
-            pair = kv_ref[r, pl.ds(pl.multiple_of(b * keys, keys), keys), :]
+            query = mine[r, 0, b]
+            grad = low(jnp.where(live, wide(mine[r, 1, b]), 0.0))
+            pair = jnp.concatenate([kv_ref[r, at, :], mate_ref[r, at, :]], axis=0)
             scores = jnp.where(key_live, dot(pair[:, :head], query, NT) * scale, masked_score)
             top = jnp.max(scores, axis=0, keepdims=True)
             power = jnp.exp(scores - top)
@@ -101,27 +106,23 @@
             tops.append(top + jnp.log(total))
             deltas.append(part / total)
         stats = jnp.concatenate(tops + deltas, axis=0)
-        for peer in range(shards):
+        for peer in range(stat_ref.shape[0]):
             stat_ref[peer, b] = stats
         return carry
 
     lax.fori_loop(0, samples, one, 0)
 
 
-def forward(shards, scalars, src_len, tgt_len, mine, mate, kv):
-    layers, _, samples, half, head = mine.shape
-    rows = 2 * half
-    return pl.pallas_call(
-        forward_kernel,
-        out_shape=(
-            kept_here(2, layers, samples, rows, head),
-            kept_here(shards, samples, 2 * layers, rows, dtype=jnp.float32),
-        ),
+def forward(chips, block, scalars, src_len, tgt_len, mine, kv, mate):
+    layers, _, samples, rows, _ = mine.shape
+    return pl.pallas_call(
+        functools.partial(forward_kernel, block),
+        out_shape=kept_here(chips, samples, 2 * layers, rows, dtype=jnp.float32),
         in_specs=[SCALAR] * 3 + [FAST] * 3,
-        out_specs=(FAST, FAST),
+        out_specs=FAST,
         compiler_params=ROOM,
         name="forward",
-    )(scalars, src_len, tgt_len, *held(mine, mate, kv))
+    )(scalars, src_len, tgt_len, *held(mine, kv, mate))
 
 
 def terms_of(grads, w_ref, place):
@@ -134,25 +135,20 @@
     return low(terms)
 
 
-def backward_kernel(start, keys, scalars, src_len, kv_ref, qc_ref, stat_ref, w_in,
-                    keep_ref, give_ref, grads, up_ref, down_ref, *rest):
+def backward_kernel(start, keys, scalars, src_len, tgt_len, mine, kv_ref, mate_ref, stat_ref, w_hbm,
+                    keep_ref, give_ref, grads_ref, mate_grads_ref, *rest):
     layers, _, _ = kv_ref.shape
-    rows, head = qc_ref.shape[3:]
-    shards = stat_ref.shape[0]
-    samples = keep_ref.shape[3]
+    rows, head = mine.shape[3:]
+    half, _, _, samples, block, _ = keep_ref.shape
     scale = head ** (-0.5)
-    seat = scalars[0]
-    even = scalars[1] == 0
+    seat, core = scalars[0], scalars[1]
+    even = scalars[9] == 0
     takes = []
     if rest:
         w_ref, w_sem = rest
-        part = w_ref.shape[1] // 4
-        for k in range(4):
-            at = pl.ds(pl.multiple_of(scalars[4 + k] * part, part), part)
-            takes.append(pltpu.make_async_copy(w_in.at[:, at], w_ref.at[:, at], w_sem.at[k]))
-            takes[k].start()
-    else:
-        w_ref = w_in
+        take = pltpu.make_async_copy(w_hbm, w_ref, w_sem)
+        take.start()
+        takes.append(take)
 
     def one(k, carry):
         b = start + k
@@ -162,60 +158,75 @@
         weight = jnp.exp(lse - top[None])
         inverse = 1.0 / jnp.sum(weight, axis=0)
         delta = jnp.sum(weight * stat[:, layers:], axis=0) * inverse
-        down_live = seat * keys + lax.broadcasted_iota(jnp.int32, (keys, rows), 0) < src_len[b]
+        live = live_targets(core, rows, block, head, tgt_len[b])
+        key_live = key_places(seat, keys, rows) < src_len[b]
         taken = pl.ds(pl.multiple_of(b * keys, keys), keys)
         at = pl.ds(pl.multiple_of(k * keys, keys), keys)
         for r in range(layers):
-            pair = kv_ref[r, taken, :]
+            pair = jnp.concatenate([kv_ref[r, taken, :], mate_ref[r, taken, :]], axis=0)
             key, value = pair[:, :head], pair[:, head:]
-            query, grad = qc_ref[0, r, b], qc_ref[1, r, b]
-            scores = jnp.where(down_live, dot(key, query, NT) * scale, masked_score)
+            query = mine[r, 0, b]
+            grad = low(jnp.where(live, wide(mine[r, 1, b]), 0.0))
+            scores = jnp.where(key_live, dot(key, query, NT) * scale, masked_score)
             prob = jnp.exp(scores - top[r:r + 1, :]) * inverse[r:r + 1, :]
             slope = low(prob * (dot(value, grad, NT) - delta[r:r + 1, :]))
             prob = low(prob)
-            grads[r, at, :head] = low(dot(slope, query, NN) * scale)
-            grads[r, at, head:] = low(dot(prob, grad, NN))
+            both = (low(dot(slope, query, NN) * scale), low(dot(prob, grad, NN)))
+            for side in range(2):
+                columns = slice(side * head, (side + 1) * head)
+                grads_ref[r, at, columns] = both[side][:keys]
+                mate_grads_ref[r, at, columns] = both[side][keys:]
             for kind, out in enumerate((dot(prob, value, TN), dot(slope, key, TN) * scale)):
-                out = out.reshape(shards // 2, 2, rows // shards, head)
+                out = out.reshape(half, 2, block, head)
                 keep_ref[:, kind, r, k] = low(jnp.where(even, out[:, 0], out[:, 1]))
                 give_ref[:, kind, r, k] = low(jnp.where(even, out[:, 1], out[:, 0]))
         return carry
 
     lax.fori_loop(0, samples, one, 0)
-    for take in takes[:1]:
+    for take in takes:
         take.wait()
-    terms = terms_of(grads, w_ref, scalars[4])
-    half = keys // 2
-    for k in range(samples):
-        up_ref[k * half:(k + 1) * half] = terms[k * keys:k * keys + half]
-        down_ref[k * half:(k + 1) * half] = terms[k * keys + half:(k + 1) * keys]
-    for take in takes[1:]:
-        take.wait()
-
-
-def backward(chunk, scalars, src_len, kv, qc, stats, weights):
-    _, layers, samples, rows, head = qc.shape
-    shards = stats.shape[0]
+
+
+def backward(chunk, block, scalars, src_len, tgt_len, mine, kv, mate, stats, weights):
+    layers, _, samples, rows, head = mine.shape
     keys = kv.shape[1] // samples
     samples = samples // CHUNKS
-    half = kept_here(shards // 2, 2, layers, samples, rows // shards, head)
-    far = kept_here(samples * keys // 2, weights.shape[1] // 4)
-    outs = (half, half, kept_here(layers, samples * keys, kv.shape[2]), far, far)
+    half = kept_here(rows // block // 2, 2, layers, samples, block, head)
+    grads = kept_here(layers, samples * keys, kv.shape[2])
+    outs = (half, half, grads, grads)
     scratch = []
     if chunk == 0:
         outs += (kept_here(*weights.shape),)
-        scratch = [pltpu.SemaphoreType.DMA((4,))]
-        weights = in_hbm(weights)
-    else:
-        (weights,) = held(weights)
+        scratch = [pltpu.SemaphoreType.DMA]
     return pl.pallas_call(
         functools.partial(backward_kernel, chunk * samples, keys),
         out_shape=outs,
-        in_specs=[SCALAR] * 2 + [FAST] * 3 + [FAST if chunk else SLOW],
+        in_specs=[SCALAR] * 3 + [FAST] * 4 + [SLOW],
         out_specs=(FAST,) * len(outs),
         scratch_shapes=scratch,
         compiler_params=ROOM,
-    )(scalars, src_len, *held(kv, qc, stats), weights)
+    )(scalars, src_len, tgt_len, *held(mine, kv, mate, stats), in_hbm(weights))
+
+
+def join_kernel(keys, scalars, grads_in, came, w_ref, grads, up_ref, down_ref):
+    grads[...] = low(wide(grads_in[...]) + wide(came[...]))
+    terms = terms_of(grads, w_ref, scalars[4])
+    half = keys // 2
+    for k in range(grads.shape[1] // keys):
+        up_ref[k * half:(k + 1) * half] = terms[k * keys:k * keys + half]
+        down_ref[k * half:(k + 1) * half] = terms[k * keys + half:(k + 1) * keys]
+
+
+def join(keys, scalars, grads, came, weights):
+    far = kept_here(grads.shape[1] // 2, weights.shape[1] // 4)
+    outs = (kept_here(*grads.shape), far, far)
+    return pl.pallas_call(
+        functools.partial(join_kernel, keys),
+        out_shape=outs,
+        in_specs=[SCALAR] + [FAST] * 3,
+        out_specs=(FAST,) * 3,
+        compiler_params=ROOM,
+    )(scalars, *held(grads, came, weights))
 
 
 def near_kernel(scalars, *refs):
@@ -408,26 +419,36 @@
     def swap(a, axis):
         return lax.all_to_all(a, axis, 0, 0, tiled=True)
 
-    halves = [
-        jnp.transpose(lax.dynamic_slice_in_dim(a[0], core * half, half, 1), (2, 0, 1, 3)) for a in (queries, cotangent)
-    ]
+    block = rows // shards
+    halves = []
+    for source in (queries, cotangent):
+        picked = source[0].reshape(samples, shards // 2, 2, block, *source.shape[3:])
+        picked = lax.dynamic_index_in_dim(picked, core, 2, keepdims=False)
+        picked = picked.reshape(samples, half, *source.shape[3:])
+        halves.append(jnp.transpose(picked, (2, 0, 1, 3)))
     mine = swap(jnp.stack(halves, 1), "section")
     kv = project(encoder_states.reshape(samples * src_rows, width), w_kv)
+    mate = lax.ppermute(kv, "seq", flip(shards, 1))
     mine, kv = lax.optimization_barrier((mine, kv))
-    mate = lax.ppermute(mine, "seq", flip(shards, 1))
-    qc, stats = forward(shards, scalars, src_len, tgt_len, mine, mate, kv)
-    stats = swap(stats, "seq")
+    stats = forward(shards // 2, block, scalars, src_len, tgt_len, mine, kv, mate)
+    same_core = [list(range(c, shards, 2)) for c in range(2)]
+    stats = lax.all_to_all(stats, "seq", 0, 0, axis_index_groups=same_core, tiled=True)
 
     heads = lax.axis_size("head")
+    kept, came, parts, grads, ups, downs = [], [], [], [], [], []
     weights = w_kv
-    kept, came, grads, ups, downs = [], [], [], [], []
     for c in range(CHUNKS):
-        keep, give, part, far_up, far_down, *copied = backward(c, scalars, src_len, kv, qc, stats, weights)
+        keep, give, own, other, *copied = backward(
+            c, block, scalars, src_len, tgt_len, mine, kv, mate, stats, w_kv
+        )
         weights = copied[0] if copied else weights
+        parts.append((own, lax.ppermute(other, "seq", flip(shards, 1))))
+        came.append(lax.ppermute(give, "seq", flip(shards, 2)))
+        kept.append(keep)
+    for c in range(CHUNKS):
+        part, far_up, far_down = join(src_rows, scalars, *parts[c], weights)
         ups.append(up(far_up))
         downs.append(down(far_down))
-        came.append(lax.ppermute(give, "seq", flip(shards, 1)))
-        kept.append(keep)
         grads.append(part)
     sides = near(scalars, grads, weights, src_rows)
     own = here(scalars, grads, weights)
@@ -441,7 +462,7 @@
         start += group
     source_grads = finish(pieces).reshape(samples, src_rows, cols)
 
-    for bit, run in ((1, 1), (3, 2), (2, 1)):
+    for bit, run in ((3, 2), (2, 1)):
         keep, give = halve(bits[bit].astype(jnp.int32), kept, came, run)
         kept, came = [keep], [lax.ppermute(give, "seq", flip(shards, 1 << bit))]
     own, to_up, to_far, to_down = deal(scalars, kept[0], came[0])

time: 152 us -> 159 us (1.046)
  waiting for transfers between devices: 63.5 us -> 76.7 us
  blocking collectives: 15 us -> 10.8 us
    ppermute x5, waiting for transfers between devices: 2.49 us -> 21.4 us  [up(): return lax.ppermute(a, 'section', turn(4, 1))]
    ppermute x5, waiting for transfers between devices: 24.2 us -> 8.4 us  [down(): return lax.ppermute(a, 'section', turn(4, 3))]
    all_to_all x3, waiting for transfers between devices: 8.83 us -> 20.3 us  [swap(): return lax.all_to_all(a, axis, 0, 0, tiled=True)]
    all_to_all x1, blocking collectives: 15 us -> 10.8 us  [body(): lax.all_to_all(stats, 'seq', 0, 0, axis_index_groups=same_core, tiled=True)]
    ppermute x3 -> x5, waiting for transfers between devices: 2.57 us -> 0.01 us  [the longest x2 0.01 us: body(): parts.append((own, lax.ppermute(other, 'seq', flip(shards, 1))))]
    pallas_call x1 -> x3, Pallas kernels: 2.19 us -> 4.73 us  [the longest x2 2.56 us: join(): pl.pallas_call(functools.partial(join_kernel, keys), out_shape=outs, in_s...]
    ppermute x3 -> x2, starting transfers between devices: 3.82 us -> 1.64 us  [body(): kept, came = ([keep], [lax.ppermute(give, 'seq', flip(shards, 1 << bit))])]
    ppermute x3 -> x5, starting transfers between devices: 0.51 us -> 2.63 us  [the longest x2 2.03 us: body(): came.append(lax.ppermute(give, 'seq', flip(shards, 2)))]
  transfers between devices with their start and end apart: 20 -> 21, of which waited for: 12 -> 12; matrix products, arithmetic and copies ran while one was open for 1% -> 3% of each run, Pallas kernels for 15% -> 10%
where the time goes in v4:
time: 159 us; the launch traced here: 157 us
  waiting for transfers between devices  76.7 us (48%)
  starting transfers between devices  31.7 us (20%)
  Pallas kernels  30.8 us (19%)
  blocking collectives  10.8 us (7%)
  local copies, waits for them, and re-layouts  4.67 us (3%)
    ppermute x2, waiting for transfers between devices, body(): kept, came = ([keep], [lax.ppermute(give, 'seq', flip(shards, 1 << bit))])  24.6 us
    ppermute x5, waiting for transfers between devices, up(): return lax.ppermute(a, 'section', turn(4, 1))  21.4 us
    all_to_all x3, waiting for transfers between devices, swap(): return lax.all_to_all(a, axis, 0, 0, tiled=True)  20.3 us
    all_to_all x3, starting transfers between devices, swap(): return lax.all_to_all(a, axis, 0, 0, tiled=True)  15.7 us
    all_to_all x1, blocking collectives, body(): lax.all_to_all(stats, 'seq', 0, 0, axis_index_groups=same_core, tiled=True)  10.8 us
    ppermute x5, waiting for transfers between devices, down(): return lax.ppermute(a, 'section', turn(4, 3))  8.4 us
    pallas_call x1, Pallas kernels, project(): pl.pallas_call(project_kernel, out_shape=kept_here(layers, count, cols),...  8.37 us
    ppermute x5, starting transfers between devices, up(): return lax.ppermute(a, 'section', turn(4, 1))  7.98 us
  transfers between devices with their start and end apart: 21, of which 12 were waited for; matrix products, arithmetic and copies ran while one was open for 3% of the time, Pallas kernels for 10%

profile of v4, /device:TPU:56, one launch (start us, length us, event | category | flops | bytes accessed | tf_op | source)
XLA Modules:
  0.0 156.7 jit_solution(9237479388347947721)
XLA Ops:
  0.7 8.4 %project.1.kv_ref = bf16[4,512,256]{2,1,0:T(8,128)(2,1)S(1)} custom-call(bf16[512,4096]{1,0:T(8,128)(2,1)} %bitcast.37, bf16[4,4096,256]{2,1,0:T(8,128)(2,1)} %w_hbm.3), custom_call_target="tpu_custom_call" | custom-call | tf_op jit(solution)/shard_map/project/pallas_call | solution.py:60
  9.2 1.6 %constant_dynamic-slice_fusion = (bf16[4,8,1,16,4,128]{5,4,3,2,1,0:T(4,128)(2,1)S(1)}, bf16[4,8,1,16,4,128]{5,4,3,2,1,0:T(4,128)(2,1)S(1)}) fusion(bf16[4,8,2,16,4,128]{5,4,3,2,1,0:T(4,128)(2,1)S(1)} %bitcast.40, s32[]{:T(128)S(6)} %select_n.87, bf16[4,8,2,16,4,128]{5,4,3,2,1,0:T(4,128)(2,1)} %bitcast.41), kind=kLoop, calls=%fused_computation.7 | loop fusion | bytes 2097156 | tf_op jit(solution)/shard_map/jit(dynamic_index_in_dim)/dynamic_slice | solution.py:426
  11.0 1.1 pad_maximum_fusion
  12.1 4.7 %all-to-all-start = ((bf16[4,2,4,128,128]{4,3,2,1,0:T(8,128)(2,1)}), bf16[4,2,4,128,128]{4,3,2,1,0:T(8,128)(2,1)S(1)}, u32[]{:S(2)}, u32[]{:S(2)}) async-start(bf16[4,2,4,128,128]{4,3,2,1,0:T(8,128)(2,1)} %pad_maximum_fusion), calls=%async_computation | async-start | bytes 2097152 | tf_op jit(solution)/shard_map/all_to_all | solution.py:420
  16.8 13.6 %all-to-all-done.mine = bf16[4,2,4,128,128]{4,3,2,1,0:T(8,128)(2,1)S(1)} async-done(((bf16[4,2,4,128,128]{4,3,2,1,0:T(8,128)(2,1)}), bf16[4,2,4,128,128]{4,3,2,1,0:T(8,128)(2,1)S(1)}, u32[]{:S(2)}, u32[]{:S(2)}) %all-to-all-start) | async-done | bytes 1048608 | tf_op jit(solution)/shard_map/all_to_all | solution.py:420
  30.4 2.2 %forward.1 = f32[8,4,8,128]{3,2,1,0:T(8,128)S(1)} custom-call(s32[12]{0:T(128)S(1)} %stack.84.scalars, s32[4]{0:T(128)S(1)} %copy-done.2, s32[4]{0:T(128)S(1)} %copy-done.3, bf16[4,2,4,128,128]{4,3,2,1,0:T(8,128)(2,1)S(1)} %all-to-all-done.mine, bf16[4,512,256]{2,1,0:T(8,128)(2,1)S(1)} %project.1.kv_ref, bf16[4,512,256]{2,1,0:T(8,128)(2,1)S(1)} %collective-permute-done.mate_ref), custom_call_target="tpu_custom_call" | custom-call | tf_op jit(solution)/shard_map/forward/pallas_call | solution.py:118
  32.6 10.8 %all_to_all.20.stat_ref = f32[8,4,8,128]{3,2,1,0:T(8,128)S(1)} all-to-all(f32[8,4,8,128]{3,2,1,0:T(8,128)S(1)} %forward.1), channel_id=1, replica_groups={{0,8,16,24,32,40,48,56},{4,12,20,28,36,44,52,60},{1,9,17,25,33,41,49,57..., dimensions={0} | all-to-all | bytes 262144 | tf_op jit(solution)/shard_map/all_to_all | solution.py:435
  43.4 3.0 %shard_map.86 = (bf16[4,2,4,2,16,128]{5,4,3,2,1,0:T(8,128)(2,1)S(1)}, bf16[4,2,4,2,16,128]{5,4,3,2,1,0:T(8,128)(2,1)S(1)}, bf16[4,256,256]{2,1,0:T(8,128)(2,1)S(1)}, bf16[4,256,256]{2,1,0:T(8,128)(2,1)S(1)}) custom-call(s32[12]{0:T(128)S(1)} %stack.84.scalars, s32[4]{0:T(128)S(1)} %copy-done.2, s32[4]{0:T(128)S(1)} %copy-done.3, ...), custom_call_target="tpu_custom_call" | custom-call | tf_op jit(solution)/shard_map/pallas_call | solution.py:201
  46.4 0.7 copy-done.4
  47.1 3.9 %shard_map.85 = (bf16[4,2,4,2,16,128]{5,4,3,2,1,0:T(8,128)(2,1)S(1)}, bf16[4,2,4,2,16,128]{5,4,3,2,1,0:T(8,128)(2,1)S(1)}, bf16[4,256,256]{2,1,0:T(8,128)(2,1)S(...) custom-call(s32[12]{0:T(128)S(1)} %stack.84.scalars, s32[4]{0:T(128)S(1)} %copy-done.2, s32[4]{0:T(128)S(1)} %copy-done.3, ...), custom_call_target="tpu_custom_call" | custom-call | tf_op jit(solution)/shard_map/pallas_call | solution.py:201
  51.0 0.7 copy-done.5
  51.7 0.5 collective-permute-start.8
  52.2 1.3 shard_map.90
  53.5 2.1 %collective-permute-start.14 = (bf16[128,1024]{1,0:T(8,128)(2,1)S(1)}, bf16[128,1024]{1,0:T(8,128)(2,1)S(1)}, u32[]{:S(2)}, u32[]{:S(2)}) collective-permute-start(bf16[128,1024]{1,0:T(8,128)(2,1)S(1)} %get-tuple-element.65), channel_id=1, source_target_pairs={{0,64},{64,128},{128,192},{192,0},{1,65},{65,129},{129,193},{193,1... | collective-permute-start | bytes 786440 | tf_op jit(solution)/shard_map/ppermute | solution.py:414
  55.7 1.3 shard_map.89
  57.0 3.3 %collective-permute-start.10 = (bf16[128,1024]{1,0:T(8,128)(2,1)S(1)}, bf16[128,1024]{1,0:T(8,128)(2,1)S(1)}, u32[]{:S(2)}, u32[]{:S(2)}) collective-permute-start(bf16[128,1024]{1,0:T(8,128)(2,1)S(1)} %get-tuple-element.59), channel_id=1, source_target_pairs={{0,64},{64,128},{128,192},{192,0},{1,65},{65,129},{129,193},{193,1... | collective-permute-start | bytes 786440 | tf_op jit(solution)/shard_map/ppermute | solution.py:414
  60.3 2.9 %near.1 = (bf16[128,1024]{1,0:T(8,128)(2,1)S(1)}, bf16[384,1024]{1,0:T(8,128)(2,1)S(1)}, bf16[128,1024]{1,0:T(8,128)(2,1)S(1)}, bf16[384,1024]{1,0:T(8,128)(2,1)S(1)}) custom-call(s32[12]{0:T(128)S(1)} %stack.84.scalars, bf16[4,256,256]{2,1,0:T(8,128)(2,1)S(1)} %get-tuple-element.53.refs_0_, bf16[4,256,256]{2,1,0:T(8,128)(2,1)S(1)} %get-tuple-element.56.refs_1_, ...), custom_call_target="tpu_custom_call" | custom-call | tf_op jit(solution)/shard_map/near/pallas_call | solution.py:252
  63.2 2.8 %collective-permute-done.15.refs_3_ = bf16[128,1024]{1,0:T(8,128)(2,1)S(1)} collective-permute-done((bf16[128,1024]{1,0:T(8,128)(2,1)S(1)}, bf16[128,1024]{1,0:T(8,128)(2,1)S(1)}, u32[]{:S(2)}, u32[]{:S(2)}) %collective-permute-start.15) | collective-permute-done | bytes 262176 | tf_op jit(solution)/shard_map/ppermute | solution.py:417
  66.1 1.4 collective-permute-done.10.refs_0_
  67.4 3.0 %collective-permute-done.11.refs_1_.refs_2_ = bf16[128,1024]{1,0:T(8,128)(2,1)S(1)} collective-permute-done((bf16[128,1024]{1,0:T(8,128)(2,1)S(1)}, bf16[128,1024]{1,0:T(8,128)(2,1)S(1)}, u32[]{:S(2)}, u32[]{:S(2)}) %collective-permute-start.11) | collective-permute-done | bytes 262176 | tf_op jit(solution)/shard_map/ppermute | solution.py:417
  70.4 1.3 shard_map.93
  72.1 1.7 %collective-permute-start.17 = (bf16[384,1024]{1,0:T(8,128)(2,1)}, bf16[384,1024]{1,0:T(8,128)(2,1)S(1)}, u32[]{:S(2)}, u32[]{:S(2)}) collective-permute-start(bf16[384,1024]{1,0:T(8,128)(2,1)} %get-tuple-element.68), channel_id=1, source_target_pairs={{0,192},{64,0},{128,64},{192,128},{1,193},{65,1},{129,65},{193,129... | collective-permute-start | bytes 2359304 | tf_op jit(solution)/shard_map/ppermute | solution.py:417
  73.9 1.6 %collective-permute-start.12 = (bf16[128,1024]{1,0:T(8,128)(2,1)S(1)}, bf16[128,1024]{1,0:T(8,128)(2,1)S(1)}, u32[]{:S(2)}, u32[]{:S(2)}) collective-permute-start(bf16[128,1024]{1,0:T(8,128)(2,1)S(1)} %get-tuple-element.61), channel_id=1, source_target_pairs={{0,64},{64,128},{128,192},{192,0},{1,65},{65,129},{129,193},{193,1... | collective-permute-start | bytes 786440 | tf_op jit(solution)/shard_map/ppermute | solution.py:414
  75.5 0.5 collective-permute-start.13
  76.0 1.8 %here.1.own = bf16[512,1024]{1,0:T(8,128)(2,1)S(1)} custom-call(s32[12]{0:T(128)S(1)} %stack.84.scalars, bf16[4,256,256]{2,1,0:T(8,128)(2,1)S(1)} %get-tuple-element.53.refs_0_, bf16[4,256,256]{2,1,0:T(8,128)(2,1)S(1)} %get-tuple-element.56.refs_1_, bf16[4,4096,256]{2,1,0:T(8,128)(2,1)S(1)} %get-tuple-element.52.w_ref.refs_2_), custom_call_target="tpu_custom_call" | custom-call | tf_op jit(solution)/shard_map/here/pallas_call | solution.py:271
  77.8 18.1 %collective-permute-done.12.from_down = bf16[128,1024]{1,0:T(8,128)(2,1)S(1)} collective-permute-done((bf16[128,1024]{1,0:T(8,128)(2,1)S(1)}, bf16[128,1024]{1,0:T(8,128)(2,1)S(1)}, u32[]{:S(2)}, u32[]{:S(2)}) %collective-permute-start.12) | collective-permute-done | bytes 262176 | tf_op jit(solution)/shard_map/ppermute | solution.py:414
  95.9 1.5 collective-permute-done.13.from_up
  97.4 0.8 shard_map.92
  98.3 7.6 %all-to-all-start.2 = ((bf16[4,128,256]{2,1,0:T(8,128)(2,1)}), bf16[4,128,256]{2,1,0:T(8,128)(2,1)S(1)}, u32[]{:S(2)}, u32[]{:S(2)}) async-start(bf16[4,128,256]{2,1,0:T(8,128)(2,1)} %shard_map.92), calls=%async_computation.2 | async-start | bytes 524288 | tf_op jit(solution)/shard_map/all_to_all | solution.py:420
  105.8 0.7 collective-permute-start.2
  106.5 1.3 collective-permute-start.1
  107.8 1.2 shard_map.94
  109.0 6.7 %all-to-all-done.2.refs_0_ = bf16[4,128,256]{2,1,0:T(8,128)(2,1)S(1)} async-done(((bf16[4,128,256]{2,1,0:T(8,128)(2,1)}), bf16[4,128,256]{2,1,0:T(8,128)(2,1)S(1)}, u32[]{:S(2)}, u32[]{:S(2)}) %all-to-all-start.2) | async-done | bytes 262176 | tf_op jit(solution)/shard_map/all_to_all | solution.py:420
  115.7 3.5 %all-to-all-start.3 = ((bf16[4,384,256]{2,1,0:T(8,128)(2,1)}), bf16[4,384,256]{2,1,0:T(8,128)(2,1)S(1)}, u32[]{:S(2)}, u32[]{:S(2)}) async-start(bf16[4,384,256]{2,1,0:T(8,128)(2,1)} %shard_map.94), calls=%async_computation.3 | async-start | bytes 1572864 | tf_op jit(solution)/shard_map/all_to_all | solution.py:420
  119.3 1.2 shard_map.87
  120.4 0.7 collective-permute-start.3
  121.1 18.9 %collective-permute-done.3.refs_1_ = bf16[2,2,4,4,16,128]{5,4,3,2,1,0:T(8,128)(2,1)S(1)} collective-permute-done((bf16[2,2,4,4,16,128]{5,4,3,2,1,0:T(8,128)(2,1)S(1)}, bf16[2,2,4,4,16,128]{5,4,3,2,1,0:T(8,128)(2,1)S(1)}, u32[]{:S(2)}, u32[]{:S(2)}) %collective-permute-start.3) | collective-permute-done | bytes 262176 | tf_op jit(solution)/shard_map/ppermute | solution.py:467
  140.1 0.9 collective-permute-start.4
  141.1 5.6 %collective-permute-done.4.came = bf16[1,2,4,4,16,128]{5,4,3,2,1,0:T(8,128)(2,1)S(1)} collective-permute-done((bf16[1,2,4,4,16,128]{5,4,3,2,1,0:T(8,128)(2,1)S(1)}, bf16[1,2,4,4,16,128]{5,4,3,2,1,0:T(8,128)(2,1)S(1)}, u32[]{:S(2)}, u32[]{:S(2)}) %collective-permute-start.4) | collective-permute-done | bytes 131104 | tf_op jit(solution)/shard_map/ppermute | solution.py:467
  146.7 0.6 deal.1
  147.3 0.7 collective-permute-start.5
  147.9 1.4 collective-permute-start.6
  149.4 1.9 %collective-permute-done.5 = bf16[2,4,16,128]{3,2,1,0:T(8,128)(2,1)S(1)} collective-permute-done((bf16[2,4,16,128]{3,2,1,0:T(8,128)(2,1)S(1)}, bf16[2,4,16,128]{3,2,1,0:T(8,128)(2,1)S(1)}, u32[]{:S(2)}, u32[]{:S(2)}) %collective-permute-start.5) | collective-permute-done | bytes 32800 | tf_op jit(solution)/shard_map/ppermute | solution.py:414
  151.3 2.1 %collective-permute-done.6 = bf16[2,4,16,128]{3,2,1,0:T(8,128)(2,1)S(1)} collective-permute-done((bf16[2,4,16,128]{3,2,1,0:T(8,128)(2,1)S(1)}, bf16[2,4,16,128]{3,2,1,0:T(8,128)(2,1)S(1)}, u32[]{:S(2)}, u32[]{:S(2)}) %collective-permute-start.6) | collective-permute-done | bytes 32800 | tf_op jit(solution)/shard_map/ppermute | solution.py:470
  153.4 1.1 collective-permute-done.7
  154.5 0.7 copy.14
  155.2 0.7 copy.13
  155.9 0.8 finish.1
  (36 shorter events, 1.0 us)
Async XLA Ops:
  0.6 8.5 %copy-start.6 = (bf16[1,4,256,4,128]{4,3,2,1,0:T(4,128)(2,1)S(1)}, bf16[1,4,256,4,128]{4,3,2,1,0:T(4,128)(2,1)}, u32[]{:S(2)}) copy-start(bf16[1,4,256,4,128]{4,3,2,1,0:T(4,128)(2,1)} %param.9) | copy-start | bytes 3145732
  0.6 29.8 %copy-start.2 = (s32[4]{0:T(128)S(1)}, s32[4]{0:T(128)}, u32[]{:S(2)}) copy-start(s32[4]{0:T(128)} %src_len.5) | copy-start | bytes 52
  0.7 29.8 %copy-start.3 = (s32[4]{0:T(128)S(1)}, s32[4]{0:T(128)}, u32[]{:S(2)}) copy-start(s32[4]{0:T(128)} %tgt_len.5) | copy-start | bytes 52
  9.0 21.4 %collective-permute-start = (bf16[4,512,256]{2,1,0:T(8,128)(2,1)S(1)}, bf16[4,512,256]{2,1,0:T(8,128)(2,1)S(1)}, u32[]{:S(2)}, u32[]{:S(2)}) collective-permute-start(bf16[4,512,256]{2,1,0:T(8,128)(2,1)S(1)} %project.1.kv_ref), channel_id=1, source_target_pairs={{0,4},{4,0},{8,12},{12,8},{16,20},{20,16},{24,28},{28,24},{32,36},... | collective-permute-start | bytes 3145736 | tf_op jit(solution)/shard_map/ppermute | solution.py:431
  12.1 18.3 %all-to-all-start = ((bf16[4,2,4,128,128]{4,3,2,1,0:T(8,128)(2,1)}), bf16[4,2,4,128,128]{4,3,2,1,0:T(8,128)(2,1)S(1)}, u32[]{:S(2)}, u32[]{:S(2)}) async-start(bf16[4,2,4,128,128]{4,3,2,1,0:T(8,128)(2,1)} %pad_maximum_fusion), calls=%async_computation | async-start | bytes 2097152 | tf_op jit(solution)/shard_map/all_to_all | solution.py:420
  46.4 0.7 copy-start.4
  47.1 5.2 %collective-permute-start.9 = (bf16[4,256,256]{2,1,0:T(8,128)(2,1)S(1)}, bf16[4,256,256]{2,1,0:T(8,128)(2,1)S(1)}, u32[]{:S(2)}, u32[]{:S(2)}) collective-permute-start(bf16[4,256,256]{2,1,0:T(8,128)(2,1)S(1)} %get-tuple-element.55), channel_id=1, source_target_pairs={{0,4},{4,0},{8,12},{12,8},{16,20},{20,16},{24,28},{28,24},{32,36},... | collective-permute-start | bytes 1572872 | tf_op jit(solution)/shard_map/ppermute | solution.py:445
  51.0 0.7 copy-start.5
  51.7 5.3 %copy-start = (bf16[4,2,4,2,16,128]{5,4,3,2,1,0:T(8,128)(2,1)}, bf16[4,2,4,2,16,128]{5,4,3,2,1,0:T(8,128)(2,1)S(1)}, u32[]{:S(2)}) copy-start(bf16[4,2,4,2,16,128]{5,4,3,2,1,0:T(8,128)(2,1)S(1)} %get-tuple-element.38.refs_0_) | copy-start | bytes 786436
  51.7 4.0 %collective-permute-start.8 = (bf16[4,256,256]{2,1,0:T(8,128)(2,1)S(1)}, bf16[4,256,256]{2,1,0:T(8,128)(2,1)S(1)}, u32[]{:S(2)}, u32[]{:S(2)}) collective-permute-start(bf16[4,256,256]{2,1,0:T(8,128)(2,1)S(1)} %get-tuple-element.51), channel_id=1, source_target_pairs={{0,4},{4,0},{8,12},{12,8},{16,20},{20,16},{24,28},{28,24},{32,36},... | collective-permute-start | bytes 1572872 | tf_op jit(solution)/shard_map/ppermute | solution.py:445
  53.5 9.7 %collective-permute-start.14 = (bf16[128,1024]{1,0:T(8,128)(2,1)S(1)}, bf16[128,1024]{1,0:T(8,128)(2,1)S(1)}, u32[]{:S(2)}, u32[]{:S(2)}) collective-permute-start(bf16[128,1024]{1,0:T(8,128)(2,1)S(1)} %get-tuple-element.65), channel_id=1, source_target_pairs={{0,64},{64,128},{128,192},{192,0},{1,65},{65,129},{129,193},{193,1... | collective-permute-start | bytes 786440 | tf_op jit(solution)/shard_map/ppermute | solution.py:414
  55.7 10.4 %collective-permute-start.15 = (bf16[128,1024]{1,0:T(8,128)(2,1)S(1)}, bf16[128,1024]{1,0:T(8,128)(2,1)S(1)}, u32[]{:S(2)}, u32[]{:S(2)}) collective-permute-start(bf16[128,1024]{1,0:T(8,128)(2,1)S(1)} %get-tuple-element.66), channel_id=1, source_target_pairs={{0,192},{64,0},{128,64},{192,128},{1,193},{65,1},{129,65},{193,129... | collective-permute-start | bytes 786440 | tf_op jit(solution)/shard_map/ppermute | solution.py:417
  57.0 10.5 %collective-permute-start.10 = (bf16[128,1024]{1,0:T(8,128)(2,1)S(1)}, bf16[128,1024]{1,0:T(8,128)(2,1)S(1)}, u32[]{:S(2)}, u32[]{:S(2)}) collective-permute-start(bf16[128,1024]{1,0:T(8,128)(2,1)S(1)} %get-tuple-element.59), channel_id=1, source_target_pairs={{0,64},{64,128},{128,192},{192,0},{1,65},{65,129},{129,193},{193,1... | collective-permute-start | bytes 786440 | tf_op jit(solution)/shard_map/ppermute | solution.py:414
  60.3 10.2 %collective-permute-start.11 = (bf16[128,1024]{1,0:T(8,128)(2,1)S(1)}, bf16[128,1024]{1,0:T(8,128)(2,1)S(1)}, u32[]{:S(2)}, u32[]{:S(2)}) collective-permute-start(bf16[128,1024]{1,0:T(8,128)(2,1)S(1)} %get-tuple-element.60), channel_id=1, source_target_pairs={{0,192},{64,0},{128,64},{192,128},{1,193},{65,1},{129,65},{193,129... | collective-permute-start | bytes 786440 | tf_op jit(solution)/shard_map/ppermute | solution.py:417
  71.8 36.0 %collective-permute-start.16 = (bf16[384,1024]{1,0:T(8,128)(2,1)}, bf16[384,1024]{1,0:T(8,128)(2,1)S(1)}, u32[]{:S(2)}, u32[]{:S(2)}) collective-permute-start(bf16[384,1024]{1,0:T(8,128)(2,1)} %get-tuple-element.67), channel_id=1, source_target_pairs={{0,64},{64,128},{128,192},{192,0},{1,65},{65,129},{129,193},{193,1... | collective-permute-start | bytes 2359304 | tf_op jit(solution)/shard_map/ppermute | solution.py:414
  72.1 35.8 %collective-permute-start.17 = (bf16[384,1024]{1,0:T(8,128)(2,1)}, bf16[384,1024]{1,0:T(8,128)(2,1)S(1)}, u32[]{:S(2)}, u32[]{:S(2)}) collective-permute-start(bf16[384,1024]{1,0:T(8,128)(2,1)} %get-tuple-element.68), channel_id=1, source_target_pairs={{0,192},{64,0},{128,64},{192,128},{1,193},{65,1},{129,65},{193,129... | collective-permute-start | bytes 2359304 | tf_op jit(solution)/shard_map/ppermute | solution.py:417
  73.9 22.1 %collective-permute-start.12 = (bf16[128,1024]{1,0:T(8,128)(2,1)S(1)}, bf16[128,1024]{1,0:T(8,128)(2,1)S(1)}, u32[]{:S(2)}, u32[]{:S(2)}) collective-permute-start(bf16[128,1024]{1,0:T(8,128)(2,1)S(1)} %get-tuple-element.61), channel_id=1, source_target_pairs={{0,64},{64,128},{128,192},{192,0},{1,65},{65,129},{129,193},{193,1... | collective-permute-start | bytes 786440 | tf_op jit(solution)/shard_map/ppermute | solution.py:414
  75.5 43.8 %copy-start.1 = (bf16[4,2,4,2,16,128]{5,4,3,2,1,0:T(8,128)(2,1)S(1)}, bf16[4,2,4,2,16,128]{5,4,3,2,1,0:T(8,128)(2,1)}, u32[]{:S(2)}) copy-start(bf16[4,2,4,2,16,128]{5,4,3,2,1,0:T(8,128)(2,1)} %copy-done) | copy-start | bytes 786436
  75.5 22.0 %collective-permute-start.13 = (bf16[128,1024]{1,0:T(8,128)(2,1)S(1)}, bf16[128,1024]{1,0:T(8,128)(2,1)S(1)}, u32[]{:S(2)}, u32[]{:S(2)}) collective-permute-start(bf16[128,1024]{1,0:T(8,128)(2,1)S(1)} %get-tuple-element.62), channel_id=1, source_target_pairs={{0,192},{64,0},{128,64},{192,128},{1,193},{65,1},{129,65},{193,129... | collective-permute-start | bytes 786440 | tf_op jit(solution)/shard_map/ppermute | solution.py:417
  98.3 17.5 %all-to-all-start.2 = ((bf16[4,128,256]{2,1,0:T(8,128)(2,1)}), bf16[4,128,256]{2,1,0:T(8,128)(2,1)S(1)}, u32[]{:S(2)}, u32[]{:S(2)}) async-start(bf16[4,128,256]{2,1,0:T(8,128)(2,1)} %shard_map.92), calls=%async_computation.2 | async-start | bytes 524288 | tf_op jit(solution)/shard_map/all_to_all | solution.py:420
  105.8 13.4 %collective-permute-start.2 = (bf16[4,2,4,2,16,128]{5,4,3,2,1,0:T(8,128)(2,1)}, bf16[4,2,4,2,16,128]{5,4,3,2,1,0:T(8,128)(2,1)}, u32[]{:S(2)}, u32[]{:S(2)}) collective-permute-start(bf16[4,2,4,2,16,128]{5,4,3,2,1,0:T(8,128)(2,1)} %copy-done.4), channel_id=1, source_target_pairs={{0,8},{4,12},{8,0},{12,4},{16,24},{20,28},{24,16},{28,20},{32,40},... | collective-permute-start | bytes 786440 | tf_op jit(solution)/shard_map/ppermute | solution.py:446
  106.5 12.7 %collective-permute-start.1 = (bf16[4,2,4,2,16,128]{5,4,3,2,1,0:T(8,128)(2,1)}, bf16[4,2,4,2,16,128]{5,4,3,2,1,0:T(8,128)(2,1)}, u32[]{:S(2)}, u32[]{:S(2)}) collective-permute-start(bf16[4,2,4,2,16,128]{5,4,3,2,1,0:T(8,128)(2,1)} %copy-done.5), channel_id=1, source_target_pairs={{0,8},{4,12},{8,0},{12,4},{16,24},{20,28},{24,16},{28,20},{32,40},... | collective-permute-start | bytes 786440 | tf_op jit(solution)/shard_map/ppermute | solution.py:446
  115.7 40.2 %all-to-all-start.3 = ((bf16[4,384,256]{2,1,0:T(8,128)(2,1)}), bf16[4,384,256]{2,1,0:T(8,128)(2,1)S(1)}, u32[]{:S(2)}, u32[]{:S(2)}) async-start(bf16[4,384,256]{2,1,0:T(8,128)(2,1)} %shard_map.94), calls=%async_computation.3 | async-start | bytes 1572864 | tf_op jit(solution)/shard_map/all_to_all | solution.py:420
  120.4 19.7 %collective-permute-start.3 = (bf16[2,2,4,4,16,128]{5,4,3,2,1,0:T(8,128)(2,1)S(1)}, bf16[2,2,4,4,16,128]{5,4,3,2,1,0:T(8,128)(2,1)S(1)}, u32[]{:S(2)}, u32[]{:S(2)}) collective-permute-start(bf16[2,2,4,4,16,128]{5,4,3,2,1,0:T(8,128)(2,1)S(1)} %get-tuple-element.43), channel_id=1, source_target_pairs={{0,32},{4,36},{8,40},{12,44},{16,48},{20,52},{24,56},{28,60},{32,0... | collective-permute-start | bytes 786440 | tf_op jit(solution)/shard_map/ppermute | solution.py:467
  140.1 6.6 %collective-permute-start.4 = (bf16[1,2,4,4,16,128]{5,4,3,2,1,0:T(8,128)(2,1)S(1)}, bf16[1,2,4,4,16,128]{5,4,3,2,1,0:T(8,128)(2,1)S(1)}, u32[]{:S(2)}, u32[]{:S(2)}) collective-permute-start(bf16[1,2,4,4,16,128]{5,4,3,2,1,0:T(8,128)(2,1)S(1)} %get-tuple-element.45), channel_id=1, source_target_pairs={{0,16},{4,20},{8,24},{12,28},{16,0},{20,4},{24,8},{28,12},{32,48},... | collective-permute-start | bytes 393224 | tf_op jit(solution)/shard_map/ppermute | solution.py:467
  147.3 4.0 %collective-permute-start.5 = (bf16[2,4,16,128]{3,2,1,0:T(8,128)(2,1)S(1)}, bf16[2,4,16,128]{3,2,1,0:T(8,128)(2,1)S(1)}, u32[]{:S(2)}, u32[]{:S(2)}) collective-permute-start(bf16[2,4,16,128]{3,2,1,0:T(8,128)(2,1)S(1)} %get-tuple-element.47), channel_id=1, source_target_pairs={{0,64},{64,128},{128,192},{192,0},{1,65},{65,129},{129,193},{193,1... | collective-permute-start | bytes 98312 | tf_op jit(solution)/shard_map/ppermute | solution.py:414
  147.9 5.4 %collective-permute-start.6 = (bf16[2,4,16,128]{3,2,1,0:T(8,128)(2,1)S(1)}, bf16[2,4,16,128]{3,2,1,0:T(8,128)(2,1)S(1)}, u32[]{:S(2)}, u32[]{:S(2)}) collective-permute-start(bf16[2,4,16,128]{3,2,1,0:T(8,128)(2,1)S(1)} %get-tuple-element.48), channel_id=1, source_target_pairs={{0,128},{64,192},{128,0},{192,64},{1,129},{65,193},{129,1},{193,65... | collective-permute-start | bytes 98312 | tf_op jit(solution)/shard_map/ppermute | solution.py:470
  149.3 5.1 %collective-permute-start.7 = (bf16[2,4,16,128]{3,2,1,0:T(8,128)(2,1)S(1)}, bf16[2,4,16,128]{3,2,1,0:T(8,128)(2,1)S(1)}, u32[]{:S(2)}, u32[]{:S(2)}) collective-permute-start(bf16[2,4,16,128]{3,2,1,0:T(8,128)(2,1)S(1)} %get-tuple-element.49), channel_id=1, source_target_pairs={{0,192},{64,0},{128,64},{192,128},{1,193},{65,1},{129,65},{193,129... | collective-permute-start | bytes 98312 | tf_op jit(solution)/shard_map/ppermute | solution.py:417

commit v5 on v4

--- a/solution.py
+++ b/solution.py
@@ -13,7 +13,7 @@
 NN = (((1,), (0,)), ((), ()))
 TN = (((0,), (0,)), ((), ()))
 CHUNKS = 2
-GROUPED = (1, 3)
+LEAVING = 3
 
 
 def dot(a, b, dims):
@@ -125,12 +125,10 @@
     )(scalars, src_len, tgt_len, *held(mine, kv, mate))
 
 
-def terms_of(grads, w_ref, place):
+def terms_of(grads, weights):
     terms = None
-    part = w_ref.shape[1] // 4
-    at = pl.ds(pl.multiple_of(place * part, part), part)
     for r in range(grads.shape[0]):
-        term = dot(grads[r], w_ref[r, at, :], NT)
+        term = dot(grads[r], weights[r], NT)
         terms = term if terms is None else terms + term
     return low(terms)
 
@@ -146,9 +144,12 @@
     takes = []
     if rest:
         w_ref, w_sem = rest
-        take = pltpu.make_async_copy(w_hbm, w_ref, w_sem)
-        take.start()
-        takes.append(take)
+        part = w_ref.shape[2]
+        for k in range(LEAVING):
+            at = pl.ds(pl.multiple_of(scalars[4 + k] * part, part), part)
+            take = pltpu.make_async_copy(w_hbm.at[:, at], w_ref.at[k], w_sem.at[k])
+            take.start()
+            takes.append(take)
 
     def one(k, carry):
         b = start + k
@@ -196,8 +197,8 @@
     outs = (half, half, grads, grads)
     scratch = []
     if chunk == 0:
-        outs += (kept_here(*weights.shape),)
-        scratch = [pltpu.SemaphoreType.DMA]
+        outs += (kept_here(LEAVING, layers, weights.shape[1] // 4, weights.shape[2]),)
+        scratch = [pltpu.SemaphoreType.DMA((LEAVING,))]
     return pl.pallas_call(
         functools.partial(backward_kernel, chunk * samples, keys),
         out_shape=outs,
@@ -208,74 +209,71 @@
     )(scalars, src_len, tgt_len, *held(mine, kv, mate, stats), in_hbm(weights))
 
 
-def join_kernel(keys, scalars, grads_in, came, w_ref, grads, up_ref, down_ref):
+def join_kernel(keys, grads_in, came, w_ref, grads, up_ref, down_ref):
     grads[...] = low(wide(grads_in[...]) + wide(came[...]))
-    terms = terms_of(grads, w_ref, scalars[4])
+    terms = terms_of(grads, w_ref.at[0])
     half = keys // 2
     for k in range(grads.shape[1] // keys):
         up_ref[k * half:(k + 1) * half] = terms[k * keys:k * keys + half]
         down_ref[k * half:(k + 1) * half] = terms[k * keys + half:(k + 1) * keys]
 
 
-def join(keys, scalars, grads, came, weights):
-    far = kept_here(grads.shape[1] // 2, weights.shape[1] // 4)
+def join(keys, grads, came, weights):
+    far = kept_here(grads.shape[1] // 2, weights.shape[2])
     outs = (kept_here(*grads.shape), far, far)
     return pl.pallas_call(
         functools.partial(join_kernel, keys),
         out_shape=outs,
-        in_specs=[SCALAR] + [FAST] * 3,
+        in_specs=[FAST] * 3,
         out_specs=(FAST,) * 3,
         compiler_params=ROOM,
-    )(scalars, *held(grads, came, weights))
-
-
-def near_kernel(scalars, *refs):
-    grads, w_ref, outs = refs[:CHUNKS], refs[CHUNKS], refs[CHUNKS + 1:]
-    groups = len(outs) // 2
-    for side in range(2):
-        done = 0
-        terms = [terms_of(g, w_ref, scalars[5 + side]) for g in grads]
-        size = terms[0].shape[0]
-        for k in range(groups):
-            ref = outs[side * groups + k]
-            filled = 0
-            while filled < ref.shape[0]:
-                chunk, at = divmod(done + filled, size)
-                count = min(ref.shape[0] - filled, size - at)
-                ref[filled:filled + count] = terms[chunk][at:at + count]
-                filled += count
-            done += filled
-
-
-def near(scalars, grads, weights, keys):
-    outs = tuple(kept_here(g * keys, weights.shape[1] // 4) for g in GROUPED) * 2
-    return pl.pallas_call(
-        near_kernel,
-        out_shape=outs,
-        in_specs=[SCALAR] + [FAST] * (len(grads) + 1),
-        out_specs=(FAST,) * len(outs),
-        compiler_params=ROOM,
-        name="near",
-    )(scalars, *held(*grads, weights))
+    )(*held(grads, came, weights))
+
+
+def near_kernel(keys, grads, w_ref, add_up, dir_up, dir_down, add_down):
+    half = keys // 2
+    for side, (first, second) in enumerate(((add_up, dir_up), (dir_down, add_down))):
+        terms = terms_of(grads, w_ref.at[1 + side])
+        for k in range(grads.shape[1] // keys):
+            first[k * half:(k + 1) * half] = terms[k * keys:k * keys + half]
+            second[k * half:(k + 1) * half] = terms[k * keys + half:(k + 1) * keys]
+
+
+def near(keys, grads, weights):
+    out = kept_here(grads.shape[1] // 2, weights.shape[2])
+    return pl.pallas_call(
+        functools.partial(near_kernel, keys),
+        out_shape=(out,) * 4,
+        in_specs=[FAST] * 2,
+        out_specs=(FAST,) * 4,
+        compiler_params=ROOM,
+    )(*held(grads, weights))
 
 
 def here_kernel(scalars, *refs):
-    grads, w_ref, out_ref = refs[:-2], refs[-2], refs[-1]
+    grads, (w_hbm, out_ref, w_ref, w_sem) = refs[:-4], refs[-4:]
+    part = w_ref.shape[1]
+    at = pl.ds(pl.multiple_of(scalars[7] * part, part), part)
+    take = pltpu.make_async_copy(w_hbm.at[:, at], w_ref, w_sem)
+    take.start()
+    take.wait()
     size = grads[0].shape[1]
     for k, part in enumerate(grads):
-        out_ref[k * size:(k + 1) * size] = terms_of(part, w_ref, scalars[7])
+        out_ref[k * size:(k + 1) * size] = terms_of(part, w_ref)
 
 
 def here(scalars, grads, weights):
+    layers, width, cols = weights.shape
     count = sum(g.shape[1] for g in grads)
     return pl.pallas_call(
         here_kernel,
-        out_shape=kept_here(count, weights.shape[1] // 4),
-        in_specs=[SCALAR] + [FAST] * (len(grads) + 1),
+        out_shape=kept_here(count, width // 4),
+        in_specs=[SCALAR] + [FAST] * len(grads) + [SLOW],
         out_specs=FAST,
+        scratch_shapes=[pltpu.VMEM((layers, width // 4, cols), jnp.bfloat16), pltpu.SemaphoreType.DMA],
         compiler_params=ROOM,
         name="here",
-    )(scalars, *held(*grads, weights))
+    )(scalars, *held(*grads), in_hbm(weights))
 
 
 def halve_kernel(parts, run, side, *refs):
@@ -319,52 +317,49 @@
     )(scalars, *held(kept, came))
 
 
-def pass_kernel(keys, start, up_in, down_in, *refs):
-    ups, downs = refs[:(len(refs) - 2) // 2], refs[(len(refs) - 2) // 2:-2]
-    up_ref, down_ref = refs[-2:]
+def pass_kernel(add_up, from_down, add_down, from_up, up_ref, down_ref):
+    up_ref[...] = low(wide(add_up[...]) + wide(from_down[...]))
+    down_ref[...] = low(wide(add_down[...]) + wide(from_up[...]))
+
+
+def pass_on(add_up, from_down, add_down, from_up):
+    out = kept_here(*add_up.shape)
+    return pl.pallas_call(
+        pass_kernel,
+        out_shape=(out, out),
+        in_specs=[FAST] * 4,
+        out_specs=(FAST, FAST),
+        compiler_params=ROOM,
+    )(*held(add_up, from_down, add_down, from_up))
+
+
+def gather_kernel(keys, own, *refs):
+    out_ref = refs[-1]
+    heads, _, part = out_ref.shape
     half = keys // 2
-    per = ups[0].shape[0] // half
-    first = start // per
-    for k in range(up_in.shape[0] // keys):
-        chunk, place = divmod(start + k, per)
-        came = slice(place * half, (place + 1) * half)
-        top, bottom = slice(k * keys, k * keys + half), slice(k * keys + half, (k + 1) * keys)
-        up_ref[top] = low(wide(up_in[top]) + wide(ups[chunk - first][came]))
-        down_ref[bottom] = low(wide(down_in[bottom]) + wide(downs[chunk - first][came]))
-        up_ref[bottom] = up_in[bottom]
-        down_ref[top] = down_in[top]
-
-
-def pass_on(keys, start, up_in, down_in, ups, downs):
-    per = ups[0].shape[0] // (keys // 2)
-    last = (start + up_in.shape[0] // keys - 1) // per
-    ups, downs = ups[start // per:last + 1], downs[start // per:last + 1]
-    out = kept_here(*up_in.shape)
-    return pl.pallas_call(
-        functools.partial(pass_kernel, keys, start),
-        out_shape=(out, out),
-        in_specs=[FAST] * (2 + 2 * len(ups)),
-        out_specs=(FAST, FAST),
-        compiler_params=ROOM,
-    )(*held(up_in, down_in, *ups, *downs))
-
-
-def gather_kernel(start, own, from_down, from_up, out_ref):
-    heads, count, part = out_ref.shape
-    for h in range(heads):
-        at = slice(h * part, (h + 1) * part)
-        out_ref[h] = low(wide(own[start:start + count, at]) + wide(from_down[:, at]) + wide(from_up[:, at]))
-
-
-def gather(start, own, from_down, from_up, heads):
-    count, width = from_down.shape
-    return pl.pallas_call(
-        functools.partial(gather_kernel, start),
+    for c in range(CHUNKS):
+        arrived = refs[4 * c:4 * c + 4]
+        for k in range(arrived[0].shape[0] // half):
+            came = slice(k * half, (k + 1) * half)
+            for side in range(2):
+                start = (c * (arrived[0].shape[0] // half) + k) * keys + side * half
+                to = slice(start, start + half)
+                for h in range(heads):
+                    at = slice(h * part, (h + 1) * part)
+                    total = wide(own[to, at]) + wide(arrived[2 * side][came, at])
+                    out_ref[h, to] = low(total + wide(arrived[2 * side + 1][came, at]))
+
+
+def gather(keys, own, arrived, heads):
+    count, width = own.shape
+    return pl.pallas_call(
+        functools.partial(gather_kernel, keys),
         out_shape=kept_here(heads, count, width // heads),
-        in_specs=[FAST] * 3,
+        in_specs=[FAST] * (1 + len(arrived)),
         out_specs=FAST,
         compiler_params=ROOM,
-    )(*held(own, from_down, from_up))
+        name="gather",
+    )(*held(own, *arrived))
 
 
 def finish_kernel(*refs):
@@ -435,31 +430,27 @@
     stats = lax.all_to_all(stats, "seq", 0, 0, axis_index_groups=same_core, tiled=True)
 
     heads = lax.axis_size("head")
-    kept, came, parts, grads, ups, downs = [], [], [], [], [], []
-    weights = w_kv
+    kept, came, grads, arrived = [], [], [], []
     for c in range(CHUNKS):
         keep, give, own, other, *copied = backward(
             c, block, scalars, src_len, tgt_len, mine, kv, mate, stats, w_kv
         )
-        weights = copied[0] if copied else weights
-        parts.append((own, lax.ppermute(other, "seq", flip(shards, 1))))
+        if copied:
+            (leaving,) = copied
+        other = lax.ppermute(other, "seq", flip(shards, 1))
         came.append(lax.ppermute(give, "seq", flip(shards, 2)))
         kept.append(keep)
-    for c in range(CHUNKS):
-        part, far_up, far_down = join(src_rows, scalars, *parts[c], weights)
-        ups.append(up(far_up))
-        downs.append(down(far_down))
+        part, far_up, far_down = join(src_rows, own, other, leaving)
         grads.append(part)
-    sides = near(scalars, grads, weights, src_rows)
-    own = here(scalars, grads, weights)
-    pieces = []
-    start = 0
-    for c, group in enumerate(GROUPED):
-        to_up, to_down = pass_on(src_rows, start, sides[c], sides[len(GROUPED) + c], ups, downs)
-        to_up, to_down = up(to_up), down(to_down)
-        joined = gather(start * src_rows, own, to_up, to_down, heads)
-        pieces.append(swap(joined, "head"))
-        start += group
+        far_up, far_down = up(far_up), down(far_down)
+        add_up, dir_up, dir_down, add_down = near(src_rows, part, leaving)
+        dir_up, dir_down = up(dir_up), down(dir_down)
+        add_up, add_down = pass_on(add_up, far_up, add_down, far_down)
+        add_up, add_down = up(add_up), down(add_down)
+        arrived += [add_up, dir_down, dir_up, add_down]
+    own = here(scalars, grads, w_kv)
+    joined = gather(src_rows, own, arrived, heads)
+    pieces = [swap(joined, "head")]
     source_grads = finish(pieces).reshape(samples, src_rows, cols)
 
     for bit, run in ((3, 2), (2, 1)):

time: 159 us -> 149 us (0.937)
  waiting for transfers between devices: 76.7 us -> 66 us
  starting transfers between devices: 31.7 us -> 35.1 us
  Pallas kernels: 30.8 us -> 27.7 us
    ppermute x5 -> x7, waiting for transfers between devices: 21.4 us -> 5.66 us  [up(): return lax.ppermute(a, 'section', turn(4, 1))]
    ppermute x2, waiting for transfers between devices: 0.01 us -> 10.4 us  [body(): came.append(lax.ppermute(give, 'seq', flip(shards, 2)))]
    ppermute x5 -> x7, starting transfers between devices: 7.98 us -> 15.9 us  [up(): return lax.ppermute(a, 'section', turn(4, 1))]
    all_to_all x3 -> x2, waiting for transfers between devices: 20.3 us -> 13.6 us  [swap(): return lax.all_to_all(a, axis, 0, 0, tiled=True)]
    ppermute x5 -> x7, waiting for transfers between devices: 8.4 us -> 13.6 us  [down(): return lax.ppermute(a, 'section', turn(4, 3))]
    ppermute x2, waiting for transfers between devices: 24.6 us -> 20.7 us  [body(): kept, came = ([keep], [lax.ppermute(give, 'seq', flip(shards, 1 << bit))])]
    all_to_all x3 -> x2, starting transfers between devices: 15.7 us -> 12.2 us  [swap(): return lax.all_to_all(a, axis, 0, 0, tiled=True)]
  transfers between devices with their start and end apart: 21 -> 24, of which waited for: 12 -> 15; matrix products, arithmetic and copies ran while one was open for 3% -> 3% of each run, Pallas kernels for 10% -> 8%
where the time goes in v5:
time: 149 us; the launch traced here: 146 us
  waiting for transfers between devices  66 us (44%)
  starting transfers between devices  35.1 us (24%)
  Pallas kernels  27.7 us (19%)
  blocking collectives  10.8 us (7%)
  local copies, waits for them, and re-layouts  4.71 us (3%)
    ppermute x2, waiting for transfers between devices, body(): kept, came = ([keep], [lax.ppermute(give, 'seq', flip(shards, 1 << bit))])  20.7 us
    ppermute x7, starting transfers between devices, up(): return lax.ppermute(a, 'section', turn(4, 1))  15.9 us
    ppermute x7, waiting for transfers between devices, down(): return lax.ppermute(a, 'section', turn(4, 3))  13.6 us
    all_to_all x2, waiting for transfers between devices, swap(): return lax.all_to_all(a, axis, 0, 0, tiled=True)  13.6 us
    all_to_all x2, starting transfers between devices, swap(): return lax.all_to_all(a, axis, 0, 0, tiled=True)  12.2 us
    all_to_all x1, blocking collectives, body(): lax.all_to_all(stats, 'seq', 0, 0, axis_index_groups=same_core, tiled=True)  10.8 us
    ppermute x2, waiting for transfers between devices, body(): came.append(lax.ppermute(give, 'seq', flip(shards, 2)))  10.4 us
    pallas_call x1, Pallas kernels, project(): pl.pallas_call(project_kernel, out_shape=kept_here(layers, count, cols),...  8.38 us
  transfers between devices with their start and end apart: 24, of which 15 were waited for; matrix products, arithmetic and copies ran while one was open for 3% of the time, Pallas kernels for 8%

profile of v5, /device:TPU:56, one launch (start us, length us, event | category | flops | bytes accessed | tf_op | source)
XLA Modules:
  0.0 146.4 jit_solution(7100860725808454546)
XLA Ops:
  0.6 8.4 %project.1.kv_ref = bf16[4,512,256]{2,1,0:T(8,128)(2,1)S(1)} custom-call(bf16[512,4096]{1,0:T(8,128)(2,1)} %bitcast.37, bf16[4,4096,256]{2,1,0:T(8,128)(2,1)} %refs_2_.1), custom_call_target="tpu_custom_call" | custom-call | tf_op jit(solution)/shard_map/project/pallas_call | solution.py:60
  9.2 1.6 %constant_dynamic-slice_fusion = (bf16[4,8,1,16,4,128]{5,4,3,2,1,0:T(4,128)(2,1)S(1)}, bf16[4,8,1,16,4,128]{5,4,3,2,1,0:T(4,128)(2,1)S(1)}) fusion(bf16[4,8,2,16,4,128]{5,4,3,2,1,0:T(4,128)(2,1)S(1)} %bitcast.40, s32[]{:T(128)S(6)} %select_n.87, bf16[4,8,2,16,4,128]{5,4,3,2,1,0:T(4,128)(2,1)} %bitcast.41), kind=kLoop, calls=%fused_computation.7 | loop fusion | bytes 2097156 | tf_op jit(solution)/shard_map/jit(dynamic_index_in_dim)/dynamic_slice | solution.py:421
  11.0 1.1 pad_maximum_fusion
  12.1 4.7 %all-to-all-start = ((bf16[4,2,4,128,128]{4,3,2,1,0:T(8,128)(2,1)}), bf16[4,2,4,128,128]{4,3,2,1,0:T(8,128)(2,1)S(1)}, u32[]{:S(2)}, u32[]{:S(2)}) async-start(bf16[4,2,4,128,128]{4,3,2,1,0:T(8,128)(2,1)} %pad_maximum_fusion), calls=%async_computation | async-start | bytes 2097152 | tf_op jit(solution)/shard_map/all_to_all | solution.py:415
  16.9 13.6 %all-to-all-done.mine = bf16[4,2,4,128,128]{4,3,2,1,0:T(8,128)(2,1)S(1)} async-done(((bf16[4,2,4,128,128]{4,3,2,1,0:T(8,128)(2,1)}), bf16[4,2,4,128,128]{4,3,2,1,0:T(8,128)(2,1)S(1)}, u32[]{:S(2)}, u32[]{:S(2)}) %all-to-all-start) | async-done | bytes 1048608 | tf_op jit(solution)/shard_map/all_to_all | solution.py:415
  30.4 2.2 %forward.1 = f32[8,4,8,128]{3,2,1,0:T(8,128)S(1)} custom-call(s32[12]{0:T(128)S(1)} %stack.84.scalars, s32[4]{0:T(128)S(1)} %copy-done.2, s32[4]{0:T(128)S(1)} %copy-done.3, bf16[4,2,4,128,128]{4,3,2,1,0:T(8,128)(2,1)S(1)} %all-to-all-done.mine, bf16[4,512,256]{2,1,0:T(8,128)(2,1)S(1)} %project.1.kv_ref, bf16[4,512,256]{2,1,0:T(8,128)(2,1)S(1)} %collective-permute-done.mate_ref), custom_call_target="tpu_custom_call" | custom-call | tf_op jit(solution)/shard_map/forward/pallas_call | solution.py:118
  32.6 10.8 %all_to_all.15.stat_ref = f32[8,4,8,128]{3,2,1,0:T(8,128)S(1)} all-to-all(f32[8,4,8,128]{3,2,1,0:T(8,128)S(1)} %forward.1), channel_id=1, replica_groups={{0,8,16,24,32,40,48,56},{4,12,20,28,36,44,52,60},{1,9,17,25,33,41,49,57..., dimensions={0} | all-to-all | bytes 262144 | tf_op jit(solution)/shard_map/all_to_all | solution.py:430
  43.4 3.0 %shard_map.86 = (bf16[4,2,4,2,16,128]{5,4,3,2,1,0:T(8,128)(2,1)S(1)}, bf16[4,2,4,2,16,128]{5,4,3,2,1,0:T(8,128)(2,1)S(1)}, bf16[4,256,256]{2,1,0:T(8,128)(2,1)S(1)}, bf16[4,256,256]{2,1,0:T(8,128)(2,1)S(1)}) custom-call(s32[12]{0:T(128)S(1)} %stack.84.scalars, s32[4]{0:T(128)S(1)} %copy-done.2, s32[4]{0:T(128)S(1)} %copy-done.3, ...), custom_call_target="tpu_custom_call" | custom-call | tf_op jit(solution)/shard_map/pallas_call | solution.py:202
  46.5 3.4 %shard_map.85 = (bf16[4,2,4,2,16,128]{5,4,3,2,1,0:T(8,128)(2,1)S(1)}, bf16[4,2,4,2,16,128]{5,4,3,2,1,0:T(8,128)(2,1)S(1)}, bf16[4,256,256]{2,1,0:T(8,128)(2,1)S(...) custom-call(s32[12]{0:T(128)S(1)} %stack.84.scalars, s32[4]{0:T(128)S(1)} %copy-done.2, s32[4]{0:T(128)S(1)} %copy-done.3, ...), custom_call_target="tpu_custom_call" | custom-call | tf_op jit(solution)/shard_map/pallas_call | solution.py:202
  50.0 0.7 copy-done
  50.7 0.7 copy-done.6
  51.4 0.5 collective-permute-start.8
  51.9 0.7 shard_map.90
  52.6 2.1 %collective-permute-start.16 = (bf16[128,1024]{1,0:T(8,128)(2,1)S(1)}, bf16[128,1024]{1,0:T(8,128)(2,1)S(1)}, u32[]{:S(2)}, u32[]{:S(2)}) collective-permute-start(bf16[128,1024]{1,0:T(8,128)(2,1)S(1)} %get-tuple-element.70), channel_id=1, source_target_pairs={{0,64},{64,128},{128,192},{192,0},{1,65},{65,129},{129,193},{193,1... | collective-permute-start | bytes 786440 | tf_op jit(solution)/shard_map/ppermute | solution.py:409
  54.8 0.7 shard_map.89
  55.5 3.3 %collective-permute-start.10 = (bf16[128,1024]{1,0:T(8,128)(2,1)S(1)}, bf16[128,1024]{1,0:T(8,128)(2,1)S(1)}, u32[]{:S(2)}, u32[]{:S(2)}) collective-permute-start(bf16[128,1024]{1,0:T(8,128)(2,1)S(1)} %get-tuple-element.62), channel_id=1, source_target_pairs={{0,64},{64,128},{128,192},{192,0},{1,65},{65,129},{129,193},{193,1... | collective-permute-start | bytes 786440 | tf_op jit(solution)/shard_map/ppermute | solution.py:409
  58.8 1.3 shard_map.93
  60.1 1.3 shard_map.91
  61.9 3.3 %collective-permute-start.20 = (bf16[128,1024]{1,0:T(8,128)(2,1)S(1)}, bf16[128,1024]{1,0:T(8,128)(2,1)S(1)}, u32[]{:S(2)}, u32[]{:S(2)}) collective-permute-start(bf16[128,1024]{1,0:T(8,128)(2,1)S(1)} %get-tuple-element.75), channel_id=1, source_target_pairs={{0,64},{64,128},{128,192},{192,0},{1,65},{65,129},{129,193},{193,1... | collective-permute-start | bytes 786440 | tf_op jit(solution)/shard_map/ppermute | solution.py:409
  65.3 2.2 %collective-permute-done.10.from_down = bf16[128,1024]{1,0:T(8,128)(2,1)S(1)} collective-permute-done((bf16[128,1024]{1,0:T(8,128)(2,1)S(1)}, bf16[128,1024]{1,0:T(8,128)(2,1)S(1)}, u32[]{:S(2)}, u32[]{:S(2)}) %collective-permute-start.10) | collective-permute-done | bytes 262176 | tf_op jit(solution)/shard_map/ppermute | solution.py:409
  67.5 3.3 %collective-permute-start.14 = (bf16[128,1024]{1,0:T(8,128)(2,1)S(1)}, bf16[128,1024]{1,0:T(8,128)(2,1)S(1)}, u32[]{:S(2)}, u32[]{:S(2)}) collective-permute-start(bf16[128,1024]{1,0:T(8,128)(2,1)S(1)} %get-tuple-element.67), channel_id=1, source_target_pairs={{0,64},{64,128},{128,192},{192,0},{1,65},{65,129},{129,193},{193,1... | collective-permute-start | bytes 786440 | tf_op jit(solution)/shard_map/ppermute | solution.py:409
  70.9 5.5 %collective-permute-done.19.refs_5_ = bf16[128,1024]{1,0:T(8,128)(2,1)S(1)} collective-permute-done((bf16[128,1024]{1,0:T(8,128)(2,1)S(1)}, bf16[128,1024]{1,0:T(8,128)(2,1)S(1)}, u32[]{:S(2)}, u32[]{:S(2)}) %collective-permute-start.19) | collective-permute-done | bytes 262176 | tf_op jit(solution)/shard_map/ppermute | solution.py:412
  76.4 3.2 %collective-permute-start.12 = (bf16[128,1024]{1,0:T(8,128)(2,1)S(1)}, bf16[128,1024]{1,0:T(8,128)(2,1)S(1)}, u32[]{:S(2)}, u32[]{:S(2)}) collective-permute-start(bf16[128,1024]{1,0:T(8,128)(2,1)S(1)} %get-tuple-element.65), channel_id=1, source_target_pairs={{0,64},{64,128},{128,192},{192,0},{1,65},{65,129},{129,193},{193,1... | collective-permute-start | bytes 786440 | tf_op jit(solution)/shard_map/ppermute | solution.py:409
  79.6 2.4 %collective-permute-done.13.refs_1_ = bf16[128,1024]{1,0:T(8,128)(2,1)S(1)} collective-permute-done((bf16[128,1024]{1,0:T(8,128)(2,1)S(1)}, bf16[128,1024]{1,0:T(8,128)(2,1)S(1)}, u32[]{:S(2)}, u32[]{:S(2)}) %collective-permute-start.13) | collective-permute-done | bytes 262176 | tf_op jit(solution)/shard_map/ppermute | solution.py:412
  82.0 3.4 %here.1.own = bf16[512,1024]{1,0:T(8,128)(2,1)S(1)} custom-call(s32[12]{0:T(128)S(1)} %stack.84.scalars, bf16[4,256,256]{2,1,0:T(8,128)(2,1)S(1)} %get-tuple-element.57.refs_0_.grads, bf16[4,256,256]{2,1,0:T(8,128)(2,1)S(1)} %get-tuple-element.60.refs_1_.grads, bf16[4,4096,256]{2,1,0:T(8,128)(2,1)} %refs_2_.1), custom_call_target="tpu_custom_call" | custom-call | tf_op jit(solution)/shard_map/here/pallas_call | solution.py:268
  85.5 2.1 %collective-permute-done.21.refs_7_ = bf16[128,1024]{1,0:T(8,128)(2,1)S(1)} collective-permute-done((bf16[128,1024]{1,0:T(8,128)(2,1)S(1)}, bf16[128,1024]{1,0:T(8,128)(2,1)S(1)}, u32[]{:S(2)}, u32[]{:S(2)}) %collective-permute-start.21) | collective-permute-done | bytes 262176 | tf_op jit(solution)/shard_map/ppermute | solution.py:412
  87.6 1.4 collective-permute-done.12.refs_0_
  89.0 3.0 %collective-permute-done.15.refs_3_ = bf16[128,1024]{1,0:T(8,128)(2,1)S(1)} collective-permute-done((bf16[128,1024]{1,0:T(8,128)(2,1)S(1)}, bf16[128,1024]{1,0:T(8,128)(2,1)S(1)}, u32[]{:S(2)}, u32[]{:S(2)}) %collective-permute-start.15) | collective-permute-done | bytes 262176 | tf_op jit(solution)/shard_map/ppermute | solution.py:412
  92.0 1.4 gather.1
  93.4 7.6 %all-to-all-start.2 = ((bf16[4,512,256]{2,1,0:T(8,128)(2,1)}), bf16[4,512,256]{2,1,0:T(8,128)(2,1)S(1)}, u32[]{:S(2)}, u32[]{:S(2)}) async-start(bf16[4,512,256]{2,1,0:T(8,128)(2,1)} %gather.1), calls=%async_computation.2 | async-start | bytes 2097152 | tf_op jit(solution)/shard_map/all_to_all | solution.py:415
  101.0 0.7 collective-permute-start.2
  101.7 1.3 collective-permute-start.1
  103.0 7.1 %collective-permute-done.2.refs_3_ = bf16[4,2,4,2,16,128]{5,4,3,2,1,0:T(8,128)(2,1)S(1)} collective-permute-done((bf16[4,2,4,2,16,128]{5,4,3,2,1,0:T(8,128)(2,1)S(1)}, bf16[4,2,4,2,16,128]{5,4,3,2,1,0:T(8,128)(2,1)S(1)}, u32[]{:S(2)}, u32[]{:S(2)}) %collective-permute-start.2) | collective-permute-done | bytes 262176 | tf_op jit(solution)/shard_map/ppermute | solution.py:441
  110.1 3.3 %collective-permute-done.1.refs_2_ = bf16[4,2,4,2,16,128]{5,4,3,2,1,0:T(8,128)(2,1)S(1)} collective-permute-done((bf16[4,2,4,2,16,128]{5,4,3,2,1,0:T(8,128)(2,1)S(1)}, bf16[4,2,4,2,16,128]{5,4,3,2,1,0:T(8,128)(2,1)S(1)}, u32[]{:S(2)}, u32[]{:S(2)}) %collective-permute-start.1) | collective-permute-done | bytes 262176 | tf_op jit(solution)/shard_map/ppermute | solution.py:441
  113.5 1.4 collective-permute-start.3
  115.0 15.2 %collective-permute-done.3.refs_1_ = bf16[2,2,4,4,16,128]{5,4,3,2,1,0:T(8,128)(2,1)S(1)} collective-permute-done((bf16[2,2,4,4,16,128]{5,4,3,2,1,0:T(8,128)(2,1)S(1)}, bf16[2,2,4,4,16,128]{5,4,3,2,1,0:T(8,128)(2,1)S(1)}, u32[]{:S(2)}, u32[]{:S(2)}) %collective-permute-start.3) | collective-permute-done | bytes 262176 | tf_op jit(solution)/shard_map/ppermute | solution.py:458
  130.3 1.1 collective-permute-start.4
  131.4 5.5 %collective-permute-done.4.came = bf16[1,2,4,4,16,128]{5,4,3,2,1,0:T(8,128)(2,1)S(1)} collective-permute-done((bf16[1,2,4,4,16,128]{5,4,3,2,1,0:T(8,128)(2,1)S(1)}, bf16[1,2,4,4,16,128]{5,4,3,2,1,0:T(8,128)(2,1)S(1)}, u32[]{:S(2)}, u32[]{:S(2)}) %collective-permute-start.4) | collective-permute-done | bytes 131104 | tf_op jit(solution)/shard_map/ppermute | solution.py:458
  136.8 0.6 deal.1
  137.4 0.6 collective-permute-start.5
  138.0 0.9 collective-permute-start.6
  138.9 0.6 collective-permute-start.7
  139.5 1.9 %collective-permute-done.5 = bf16[2,4,16,128]{3,2,1,0:T(8,128)(2,1)S(1)} collective-permute-done((bf16[2,4,16,128]{3,2,1,0:T(8,128)(2,1)S(1)}, bf16[2,4,16,128]{3,2,1,0:T(8,128)(2,1)S(1)}, u32[]{:S(2)}, u32[]{:S(2)}) %collective-permute-start.5) | collective-permute-done | bytes 32800 | tf_op jit(solution)/shard_map/ppermute | solution.py:409
  141.4 2.1 %collective-permute-done.6 = bf16[2,4,16,128]{3,2,1,0:T(8,128)(2,1)S(1)} collective-permute-done((bf16[2,4,16,128]{3,2,1,0:T(8,128)(2,1)S(1)}, bf16[2,4,16,128]{3,2,1,0:T(8,128)(2,1)S(1)}, u32[]{:S(2)}, u32[]{:S(2)}) %collective-permute-start.6) | collective-permute-done | bytes 32800 | tf_op jit(solution)/shard_map/ppermute | solution.py:461
  143.5 0.6 collective-permute-done.7
  144.2 0.7 copy.14
  144.9 0.7 copy.13
  145.5 0.8 finish.1
  (46 shorter events, 1.5 us)
Async XLA Ops:
  0.6 8.5 %copy-start.8 = (bf16[1,4,256,4,128]{4,3,2,1,0:T(4,128)(2,1)S(1)}, bf16[1,4,256,4,128]{4,3,2,1,0:T(4,128)(2,1)}, u32[]{:S(2)}) copy-start(bf16[1,4,256,4,128]{4,3,2,1,0:T(4,128)(2,1)} %param.9) | copy-start | bytes 3145732
  9.0 21.4 %copy-start.2 = (s32[4]{0:T(128)S(1)}, s32[4]{0:T(128)}, u32[]{:S(2)}) copy-start(s32[4]{0:T(128)} %src_len.5) | copy-start | bytes 52
  9.0 21.4 %copy-start.3 = (s32[4]{0:T(128)S(1)}, s32[4]{0:T(128)}, u32[]{:S(2)}) copy-start(s32[4]{0:T(128)} %tgt_len.5) | copy-start | bytes 52
  9.0 21.4 %collective-permute-start = (bf16[4,512,256]{2,1,0:T(8,128)(2,1)S(1)}, bf16[4,512,256]{2,1,0:T(8,128)(2,1)S(1)}, u32[]{:S(2)}, u32[]{:S(2)}) collective-permute-start(bf16[4,512,256]{2,1,0:T(8,128)(2,1)S(1)} %project.1.kv_ref), channel_id=1, source_target_pairs={{0,4},{4,0},{8,12},{12,8},{16,20},{20,16},{24,28},{28,24},{32,36},... | collective-permute-start | bytes 3145736 | tf_op jit(solution)/shard_map/ppermute | solution.py:426
  12.1 18.3 %all-to-all-start = ((bf16[4,2,4,128,128]{4,3,2,1,0:T(8,128)(2,1)}), bf16[4,2,4,128,128]{4,3,2,1,0:T(8,128)(2,1)S(1)}, u32[]{:S(2)}, u32[]{:S(2)}) async-start(bf16[4,2,4,128,128]{4,3,2,1,0:T(8,128)(2,1)} %pad_maximum_fusion), calls=%async_computation | async-start | bytes 2097152 | tf_op jit(solution)/shard_map/all_to_all | solution.py:415
  46.4 6.2 %copy-start.4 = (bf16[4,2,4,2,16,128]{5,4,3,2,1,0:T(8,128)(2,1)}, bf16[4,2,4,2,16,128]{5,4,3,2,1,0:T(8,128)(2,1)S(1)}, u32[]{:S(2)}) copy-start(bf16[4,2,4,2,16,128]{5,4,3,2,1,0:T(8,128)(2,1)S(1)} %get-tuple-element.45) | copy-start | bytes 786436
  46.4 5.5 %collective-permute-start.9 = (bf16[4,256,256]{2,1,0:T(8,128)(2,1)S(1)}, bf16[4,256,256]{2,1,0:T(8,128)(2,1)S(1)}, u32[]{:S(2)}, u32[]{:S(2)}) collective-permute-start(bf16[4,256,256]{2,1,0:T(8,128)(2,1)S(1)} %get-tuple-element.59), channel_id=1, source_target_pairs={{0,4},{4,0},{8,12},{12,8},{16,20},{20,16},{24,28},{28,24},{32,36},... | collective-permute-start | bytes 1572872 | tf_op jit(solution)/shard_map/ppermute | solution.py:440
  50.0 0.7 copy-start
  50.7 0.7 copy-start.6
  51.4 3.4 %collective-permute-start.8 = (bf16[4,256,256]{2,1,0:T(8,128)(2,1)S(1)}, bf16[4,256,256]{2,1,0:T(8,128)(2,1)S(1)}, u32[]{:S(2)}, u32[]{:S(2)}) collective-permute-start(bf16[4,256,256]{2,1,0:T(8,128)(2,1)S(1)} %get-tuple-element.55), channel_id=1, source_target_pairs={{0,4},{4,0},{8,12},{12,8},{16,20},{20,16},{24,28},{28,24},{32,36},... | collective-permute-start | bytes 1572872 | tf_op jit(solution)/shard_map/ppermute | solution.py:440
  52.6 9.3 %collective-permute-start.16 = (bf16[128,1024]{1,0:T(8,128)(2,1)S(1)}, bf16[128,1024]{1,0:T(8,128)(2,1)S(1)}, u32[]{:S(2)}, u32[]{:S(2)}) collective-permute-start(bf16[128,1024]{1,0:T(8,128)(2,1)S(1)} %get-tuple-element.70), channel_id=1, source_target_pairs={{0,64},{64,128},{128,192},{192,0},{1,65},{65,129},{129,193},{193,1... | collective-permute-start | bytes 786440 | tf_op jit(solution)/shard_map/ppermute | solution.py:409
  54.8 10.4 %collective-permute-start.17 = (bf16[128,1024]{1,0:T(8,128)(2,1)S(1)}, bf16[128,1024]{1,0:T(8,128)(2,1)S(1)}, u32[]{:S(2)}, u32[]{:S(2)}) collective-permute-start(bf16[128,1024]{1,0:T(8,128)(2,1)S(1)} %get-tuple-element.72), channel_id=1, source_target_pairs={{0,192},{64,0},{128,64},{192,128},{1,193},{65,1},{129,65},{193,129... | collective-permute-start | bytes 786440 | tf_op jit(solution)/shard_map/ppermute | solution.py:412
  55.5 12.0 %collective-permute-start.10 = (bf16[128,1024]{1,0:T(8,128)(2,1)S(1)}, bf16[128,1024]{1,0:T(8,128)(2,1)S(1)}, u32[]{:S(2)}, u32[]{:S(2)}) collective-permute-start(bf16[128,1024]{1,0:T(8,128)(2,1)S(1)} %get-tuple-element.62), channel_id=1, source_target_pairs={{0,64},{64,128},{128,192},{192,0},{1,65},{65,129},{129,193},{193,1... | collective-permute-start | bytes 786440 | tf_op jit(solution)/shard_map/ppermute | solution.py:409
  58.8 11.9 %collective-permute-start.11 = (bf16[128,1024]{1,0:T(8,128)(2,1)S(1)}, bf16[128,1024]{1,0:T(8,128)(2,1)S(1)}, u32[]{:S(2)}, u32[]{:S(2)}) collective-permute-start(bf16[128,1024]{1,0:T(8,128)(2,1)S(1)} %get-tuple-element.64), channel_id=1, source_target_pairs={{0,192},{64,0},{128,64},{192,128},{1,193},{65,1},{129,65},{193,129... | collective-permute-start | bytes 786440 | tf_op jit(solution)/shard_map/ppermute | solution.py:412
  61.4 15.0 %collective-permute-start.19 = (bf16[128,1024]{1,0:T(8,128)(2,1)S(1)}, bf16[128,1024]{1,0:T(8,128)(2,1)S(1)}, u32[]{:S(2)}, u32[]{:S(2)}) collective-permute-start(bf16[128,1024]{1,0:T(8,128)(2,1)S(1)} %get-tuple-element.74), channel_id=1, source_target_pairs={{0,192},{64,0},{128,64},{192,128},{1,193},{65,1},{129,65},{193,129... | collective-permute-start | bytes 786440 | tf_op jit(solution)/shard_map/ppermute | solution.py:412
  61.9 14.5 %collective-permute-start.20 = (bf16[128,1024]{1,0:T(8,128)(2,1)S(1)}, bf16[128,1024]{1,0:T(8,128)(2,1)S(1)}, u32[]{:S(2)}, u32[]{:S(2)}) collective-permute-start(bf16[128,1024]{1,0:T(8,128)(2,1)S(1)} %get-tuple-element.75), channel_id=1, source_target_pairs={{0,64},{64,128},{128,192},{192,0},{1,65},{65,129},{129,193},{193,1... | collective-permute-start | bytes 786440 | tf_op jit(solution)/shard_map/ppermute | solution.py:409
  65.2 16.8 %collective-permute-start.13 = (bf16[128,1024]{1,0:T(8,128)(2,1)S(1)}, bf16[128,1024]{1,0:T(8,128)(2,1)S(1)}, u32[]{:S(2)}, u32[]{:S(2)}) collective-permute-start(bf16[128,1024]{1,0:T(8,128)(2,1)S(1)} %get-tuple-element.66), channel_id=1, source_target_pairs={{0,192},{64,0},{128,64},{192,128},{1,193},{65,1},{129,65},{193,129... | collective-permute-start | bytes 786440 | tf_op jit(solution)/shard_map/ppermute | solution.py:412
  67.5 18.0 %collective-permute-start.14 = (bf16[128,1024]{1,0:T(8,128)(2,1)S(1)}, bf16[128,1024]{1,0:T(8,128)(2,1)S(1)}, u32[]{:S(2)}, u32[]{:S(2)}) collective-permute-start(bf16[128,1024]{1,0:T(8,128)(2,1)S(1)} %get-tuple-element.67), channel_id=1, source_target_pairs={{0,64},{64,128},{128,192},{192,0},{1,65},{65,129},{129,193},{193,1... | collective-permute-start | bytes 786440 | tf_op jit(solution)/shard_map/ppermute | solution.py:409
  70.8 14.7 %collective-permute-start.18 = (bf16[128,1024]{1,0:T(8,128)(2,1)S(1)}, bf16[128,1024]{1,0:T(8,128)(2,1)S(1)}, u32[]{:S(2)}, u32[]{:S(2)}) collective-permute-start(bf16[128,1024]{1,0:T(8,128)(2,1)S(1)} %get-tuple-element.73), channel_id=1, source_target_pairs={{0,64},{64,128},{128,192},{192,0},{1,65},{65,129},{129,193},{193,1... | collective-permute-start | bytes 786440 | tf_op jit(solution)/shard_map/ppermute | solution.py:409
  76.4 11.2 %collective-permute-start.21 = (bf16[128,1024]{1,0:T(8,128)(2,1)S(1)}, bf16[128,1024]{1,0:T(8,128)(2,1)S(1)}, u32[]{:S(2)}, u32[]{:S(2)}) collective-permute-start(bf16[128,1024]{1,0:T(8,128)(2,1)S(1)} %get-tuple-element.76), channel_id=1, source_target_pairs={{0,192},{64,0},{128,64},{192,128},{1,193},{65,1},{129,65},{193,129... | collective-permute-start | bytes 786440 | tf_op jit(solution)/shard_map/ppermute | solution.py:412
  76.4 12.6 %collective-permute-start.12 = (bf16[128,1024]{1,0:T(8,128)(2,1)S(1)}, bf16[128,1024]{1,0:T(8,128)(2,1)S(1)}, u32[]{:S(2)}, u32[]{:S(2)}) collective-permute-start(bf16[128,1024]{1,0:T(8,128)(2,1)S(1)} %get-tuple-element.65), channel_id=1, source_target_pairs={{0,64},{64,128},{128,192},{192,0},{1,65},{65,129},{129,193},{193,1... | collective-permute-start | bytes 786440 | tf_op jit(solution)/shard_map/ppermute | solution.py:409
  82.0 18.9 %copy-start.5 = (bf16[4,2,4,2,16,128]{5,4,3,2,1,0:T(8,128)(2,1)S(1)}, bf16[4,2,4,2,16,128]{5,4,3,2,1,0:T(8,128)(2,1)}, u32[]{:S(2)}) copy-start(bf16[4,2,4,2,16,128]{5,4,3,2,1,0:T(8,128)(2,1)} %copy-done.4) | copy-start | bytes 786436
  82.0 19.7 %copy-start.7 = (bf16[4,2,4,2,16,128]{5,4,3,2,1,0:T(8,128)(2,1)S(1)}, bf16[4,2,4,2,16,128]{5,4,3,2,1,0:T(8,128)(2,1)}, u32[]{:S(2)}) copy-start(bf16[4,2,4,2,16,128]{5,4,3,2,1,0:T(8,128)(2,1)} %copy-done.6) | copy-start | bytes 786436
  82.0 31.4 %copy-start.1 = (bf16[4,2,4,2,16,128]{5,4,3,2,1,0:T(8,128)(2,1)S(1)}, bf16[4,2,4,2,16,128]{5,4,3,2,1,0:T(8,128)(2,1)}, u32[]{:S(2)}) copy-start(bf16[4,2,4,2,16,128]{5,4,3,2,1,0:T(8,128)(2,1)} %copy-done) | copy-start | bytes 786436
  82.0 10.0 %collective-permute-start.15 = (bf16[128,1024]{1,0:T(8,128)(2,1)S(1)}, bf16[128,1024]{1,0:T(8,128)(2,1)S(1)}, u32[]{:S(2)}, u32[]{:S(2)}) collective-permute-start(bf16[128,1024]{1,0:T(8,128)(2,1)S(1)} %get-tuple-element.68), channel_id=1, source_target_pairs={{0,192},{64,0},{128,64},{192,128},{1,193},{65,1},{129,65},{193,129... | collective-permute-start | bytes 786440 | tf_op jit(solution)/shard_map/ppermute | solution.py:412
  93.4 52.1 %all-to-all-start.2 = ((bf16[4,512,256]{2,1,0:T(8,128)(2,1)}), bf16[4,512,256]{2,1,0:T(8,128)(2,1)S(1)}, u32[]{:S(2)}, u32[]{:S(2)}) async-start(bf16[4,512,256]{2,1,0:T(8,128)(2,1)} %gather.1), calls=%async_computation.2 | async-start | bytes 2097152 | tf_op jit(solution)/shard_map/all_to_all | solution.py:415
  101.0 9.2 %collective-permute-start.2 = (bf16[4,2,4,2,16,128]{5,4,3,2,1,0:T(8,128)(2,1)S(1)}, bf16[4,2,4,2,16,128]{5,4,3,2,1,0:T(8,128)(2,1)S(1)}, u32[]{:S(2)}, u32[]{:S(2)}) collective-permute-start(bf16[4,2,4,2,16,128]{5,4,3,2,1,0:T(8,128)(2,1)S(1)} %copy-done.5), channel_id=1, source_target_pairs={{0,8},{4,12},{8,0},{12,4},{16,24},{20,28},{24,16},{28,20},{32,40},... | collective-permute-start | bytes 786440 | tf_op jit(solution)/shard_map/ppermute | solution.py:441
  101.7 11.7 %collective-permute-start.1 = (bf16[4,2,4,2,16,128]{5,4,3,2,1,0:T(8,128)(2,1)S(1)}, bf16[4,2,4,2,16,128]{5,4,3,2,1,0:T(8,128)(2,1)S(1)}, u32[]{:S(2)}, u32[]{:S(2)}) collective-permute-start(bf16[4,2,4,2,16,128]{5,4,3,2,1,0:T(8,128)(2,1)S(1)} %copy-done.7), channel_id=1, source_target_pairs={{0,8},{4,12},{8,0},{12,4},{16,24},{20,28},{24,16},{28,20},{32,40},... | collective-permute-start | bytes 786440 | tf_op jit(solution)/shard_map/ppermute | solution.py:441
  113.5 16.7 %collective-permute-start.3 = (bf16[2,2,4,4,16,128]{5,4,3,2,1,0:T(8,128)(2,1)S(1)}, bf16[2,2,4,4,16,128]{5,4,3,2,1,0:T(8,128)(2,1)S(1)}, u32[]{:S(2)}, u32[]{:S(2)}) collective-permute-start(bf16[2,2,4,4,16,128]{5,4,3,2,1,0:T(8,128)(2,1)S(1)} %get-tuple-element.47), channel_id=1, source_target_pairs={{0,32},{4,36},{8,40},{12,44},{16,48},{20,52},{24,56},{28,60},{32,0... | collective-permute-start | bytes 786440 | tf_op jit(solution)/shard_map/ppermute | solution.py:458
  130.3 6.6 %collective-permute-start.4 = (bf16[1,2,4,4,16,128]{5,4,3,2,1,0:T(8,128)(2,1)S(1)}, bf16[1,2,4,4,16,128]{5,4,3,2,1,0:T(8,128)(2,1)S(1)}, u32[]{:S(2)}, u32[]{:S(2)}) collective-permute-start(bf16[1,2,4,4,16,128]{5,4,3,2,1,0:T(8,128)(2,1)S(1)} %get-tuple-element.49), channel_id=1, source_target_pairs={{0,16},{4,20},{8,24},{12,28},{16,0},{20,4},{24,8},{28,12},{32,48},... | collective-permute-start | bytes 393224 | tf_op jit(solution)/shard_map/ppermute | solution.py:458
  137.4 4.0 %collective-permute-start.5 = (bf16[2,4,16,128]{3,2,1,0:T(8,128)(2,1)S(1)}, bf16[2,4,16,128]{3,2,1,0:T(8,128)(2,1)S(1)}, u32[]{:S(2)}, u32[]{:S(2)}) collective-permute-start(bf16[2,4,16,128]{3,2,1,0:T(8,128)(2,1)S(1)} %get-tuple-element.51), channel_id=1, source_target_pairs={{0,64},{64,128},{128,192},{192,0},{1,65},{65,129},{129,193},{193,1... | collective-permute-start | bytes 98312 | tf_op jit(solution)/shard_map/ppermute | solution.py:409
  138.0 5.4 %collective-permute-start.6 = (bf16[2,4,16,128]{3,2,1,0:T(8,128)(2,1)S(1)}, bf16[2,4,16,128]{3,2,1,0:T(8,128)(2,1)S(1)}, u32[]{:S(2)}, u32[]{:S(2)}) collective-permute-start(bf16[2,4,16,128]{3,2,1,0:T(8,128)(2,1)S(1)} %get-tuple-element.52), channel_id=1, source_target_pairs={{0,128},{64,192},{128,0},{192,64},{1,129},{65,193},{129,1},{193,65... | collective-permute-start | bytes 98312 | tf_op jit(solution)/shard_map/ppermute | solution.py:461
  138.9 5.2 %collective-permute-start.7 = (bf16[2,4,16,128]{3,2,1,0:T(8,128)(2,1)S(1)}, bf16[2,4,16,128]{3,2,1,0:T(8,128)(2,1)S(1)}, u32[]{:S(2)}, u32[]{:S(2)}) collective-permute-start(bf16[2,4,16,128]{3,2,1,0:T(8,128)(2,1)S(1)} %get-tuple-element.53), channel_id=1, source_target_pairs={{0,192},{64,0},{128,64},{192,128},{1,193},{65,1},{129,65},{193,129... | collective-permute-start | bytes 98312 | tf_op jit(solution)/shard_map/ppermute | solution.py:412

commit v6 on v5

--- a/solution.py
+++ b/solution.py
@@ -140,7 +140,7 @@
     half, _, _, samples, block, _ = keep_ref.shape
     scale = head ** (-0.5)
     seat, core = scalars[0], scalars[1]
-    even = scalars[9] == 0
+    low_side = scalars[11] == 0
     takes = []
     if rest:
         w_ref, w_sem = rest
@@ -178,9 +178,9 @@
                 grads_ref[r, at, columns] = both[side][:keys]
                 mate_grads_ref[r, at, columns] = both[side][keys:]
             for kind, out in enumerate((dot(prob, value, TN), dot(slope, key, TN) * scale)):
-                out = out.reshape(half, 2, block, head)
-                keep_ref[:, kind, r, k] = low(jnp.where(even, out[:, 0], out[:, 1]))
-                give_ref[:, kind, r, k] = low(jnp.where(even, out[:, 1], out[:, 0]))
+                out = out.reshape(2, half, block, head)
+                keep_ref[:, kind, r, k] = low(jnp.where(low_side, out[0], out[1]))
+                give_ref[:, kind, r, k] = low(jnp.where(low_side, out[1], out[0]))
         return carry
 
     lax.fori_loop(0, samples, one, 0)
@@ -250,30 +250,25 @@
     )(*held(grads, weights))
 
 
-def here_kernel(scalars, *refs):
-    grads, (w_hbm, out_ref, w_ref, w_sem) = refs[:-4], refs[-4:]
+def here_kernel(scalars, grads, w_hbm, out_ref, w_ref, w_sem):
     part = w_ref.shape[1]
     at = pl.ds(pl.multiple_of(scalars[7] * part, part), part)
     take = pltpu.make_async_copy(w_hbm.at[:, at], w_ref, w_sem)
     take.start()
     take.wait()
-    size = grads[0].shape[1]
-    for k, part in enumerate(grads):
-        out_ref[k * size:(k + 1) * size] = terms_of(part, w_ref)
+    out_ref[...] = terms_of(grads, w_ref)
 
 
 def here(scalars, grads, weights):
     layers, width, cols = weights.shape
-    count = sum(g.shape[1] for g in grads)
     return pl.pallas_call(
         here_kernel,
-        out_shape=kept_here(count, width // 4),
-        in_specs=[SCALAR] + [FAST] * len(grads) + [SLOW],
+        out_shape=kept_here(grads.shape[1], width // 4),
+        in_specs=[SCALAR, FAST, SLOW],
         out_specs=FAST,
         scratch_shapes=[pltpu.VMEM((layers, width // 4, cols), jnp.bfloat16), pltpu.SemaphoreType.DMA],
         compiler_params=ROOM,
-        name="here",
-    )(scalars, *held(*grads), in_hbm(weights))
+    )(scalars, *held(grads), in_hbm(weights))
 
 
 def halve_kernel(parts, run, side, *refs):
@@ -334,20 +329,17 @@
 
 
 def gather_kernel(keys, own, *refs):
-    out_ref = refs[-1]
-    heads, _, part = out_ref.shape
+    arrived, out_ref = refs[:-1], refs[-1]
+    heads, count, part = out_ref.shape
     half = keys // 2
-    for c in range(CHUNKS):
-        arrived = refs[4 * c:4 * c + 4]
-        for k in range(arrived[0].shape[0] // half):
-            came = slice(k * half, (k + 1) * half)
-            for side in range(2):
-                start = (c * (arrived[0].shape[0] // half) + k) * keys + side * half
-                to = slice(start, start + half)
-                for h in range(heads):
-                    at = slice(h * part, (h + 1) * part)
-                    total = wide(own[to, at]) + wide(arrived[2 * side][came, at])
-                    out_ref[h, to] = low(total + wide(arrived[2 * side + 1][came, at]))
+    for k in range(count // keys):
+        came = slice(k * half, (k + 1) * half)
+        for side in range(2):
+            to = slice(k * keys + side * half, k * keys + (side + 1) * half)
+            for h in range(heads):
+                at = slice(h * part, (h + 1) * part)
+                total = wide(own[to, at]) + wide(arrived[2 * side][came, at])
+                out_ref[h, to] = low(total + wide(arrived[2 * side + 1][came, at]))
 
 
 def gather(keys, own, arrived, heads):
@@ -358,7 +350,6 @@
         in_specs=[FAST] * (1 + len(arrived)),
         out_specs=FAST,
         compiler_params=ROOM,
-        name="gather",
     )(*held(own, *arrived))
 
 
@@ -430,7 +421,7 @@
     stats = lax.all_to_all(stats, "seq", 0, 0, axis_index_groups=same_core, tiled=True)
 
     heads = lax.axis_size("head")
-    kept, came, grads, arrived = [], [], [], []
+    kept, came, pieces = [], [], []
     for c in range(CHUNKS):
         keep, give, own, other, *copied = backward(
             c, block, scalars, src_len, tgt_len, mine, kv, mate, stats, w_kv
@@ -438,22 +429,20 @@
         if copied:
             (leaving,) = copied
         other = lax.ppermute(other, "seq", flip(shards, 1))
-        came.append(lax.ppermute(give, "seq", flip(shards, 2)))
+        came.append(lax.ppermute(give, "seq", flip(shards, 8)))
         kept.append(keep)
         part, far_up, far_down = join(src_rows, own, other, leaving)
-        grads.append(part)
         far_up, far_down = up(far_up), down(far_down)
         add_up, dir_up, dir_down, add_down = near(src_rows, part, leaving)
         dir_up, dir_down = up(dir_up), down(dir_down)
         add_up, add_down = pass_on(add_up, far_up, add_down, far_down)
         add_up, add_down = up(add_up), down(add_down)
-        arrived += [add_up, dir_down, dir_up, add_down]
-    own = here(scalars, grads, w_kv)
-    joined = gather(src_rows, own, arrived, heads)
-    pieces = [swap(joined, "head")]
+        own = here(scalars, part, w_kv)
+        joined = gather(src_rows, own, [add_up, dir_down, dir_up, add_down], heads)
+        pieces.append(swap(joined, "head"))
     source_grads = finish(pieces).reshape(samples, src_rows, cols)
 
-    for bit, run in ((3, 2), (2, 1)):
+    for bit, run in ((1, 1), (2, 1)):
         keep, give = halve(bits[bit].astype(jnp.int32), kept, came, run)
         kept, came = [keep], [lax.ppermute(give, "seq", flip(shards, 1 << bit))]
     own, to_up, to_far, to_down = deal(scalars, kept[0], came[0])

time: 149 us -> 138 us (0.926)
  the two profiles are of different devices: /device:TPU:56 before, /device:TPU:2 now
where the time goes in v6:
time: 138 us
  starting transfers between devices  46.2 us (33%)
  waiting for transfers between devices  40.1 us (29%)
  Pallas kernels  31.4 us (23%)
  blocking collectives  11.1 us (8%)
  local copies, waits for them, and re-layouts  6.81 us (5%)
    all_to_all x3, starting transfers between devices, swap(): return lax.all_to_all(a, axis, 0, 0, tiled=True)  18.8 us
    all_to_all x3, waiting for transfers between devices, swap(): return lax.all_to_all(a, axis, 0, 0, tiled=True)  15.6 us
    ppermute x7, starting transfers between devices, down(): return lax.ppermute(a, 'section', turn(4, 3))  14.7 us
    all_to_all x1, blocking collectives, body(): lax.all_to_all(stats, 'seq', 0, 0, axis_index_groups=same_core, tiled=True)  11.1 us
    ppermute x7, waiting for transfers between devices, up(): return lax.ppermute(a, 'section', turn(4, 1))  9.24 us
    pallas_call x1, Pallas kernels, project(): pl.pallas_call(project_kernel, out_shape=kept_here(layers, count, cols),...  8.38 us
    pallas_call x2, Pallas kernels, backward(): pl.pallas_call(functools.partial(backward_kernel, chunk * samples, keys),...  7.23 us
    ppermute x2, waiting for transfers between devices, body(): kept, came = ([keep], [lax.ppermute(give, 'seq', flip(shards, 1 << bit))])  6.14 us
  transfers between devices with their start and end apart: 25, of which 11 were waited for; matrix products, arithmetic and copies ran while one was open for 3% of the time, Pallas kernels for 12%

profile of v6, /device:TPU:2, one launch (start us, length us, event | category | flops | bytes accessed | tf_op | source)
XLA Modules:
  0.0 137.8 jit_solution(2278703119418797310)
XLA Ops:
  0.6 8.4 %project.1.kv_ref = bf16[4,512,256]{2,1,0:T(8,128)(2,1)S(1)} custom-call(bf16[512,4096]{1,0:T(8,128)(2,1)} %bitcast.37, bf16[4,4096,256]{2,1,0:T(8,128)(2,1)} %w_hbm.7), custom_call_target="tpu_custom_call" | custom-call | tf_op jit(solution)/shard_map/project/pallas_call | solution.py:60
  9.2 1.6 %constant_dynamic-slice_fusion = (bf16[4,8,1,16,4,128]{5,4,3,2,1,0:T(4,128)(2,1)S(1)}, bf16[4,8,1,16,4,128]{5,4,3,2,1,0:T(4,128)(2,1)S(1)}) fusion(bf16[4,8,2,16,4,128]{5,4,3,2,1,0:T(4,128)(2,1)S(1)} %bitcast.40, s32[]{:T(128)S(6)} %select_n.87, bf16[4,8,2,16,4,128]{5,4,3,2,1,0:T(4,128)(2,1)} %bitcast.41), kind=kLoop, calls=%fused_computation.7 | loop fusion | bytes 2097156 | tf_op jit(solution)/shard_map/jit(dynamic_index_in_dim)/dynamic_slice | solution.py:412
  11.0 1.1 pad_maximum_fusion
  12.1 4.5 %all-to-all-start = ((bf16[4,2,4,128,128]{4,3,2,1,0:T(8,128)(2,1)}), bf16[4,2,4,128,128]{4,3,2,1,0:T(8,128)(2,1)S(1)}, u32[]{:S(2)}, u32[]{:S(2)}) async-start(bf16[4,2,4,128,128]{4,3,2,1,0:T(8,128)(2,1)} %pad_maximum_fusion), calls=%async_computation | async-start | bytes 2097152 | tf_op jit(solution)/shard_map/all_to_all | solution.py:406
  16.6 15.6 %all-to-all-done.mine = bf16[4,2,4,128,128]{4,3,2,1,0:T(8,128)(2,1)S(1)} async-done(((bf16[4,2,4,128,128]{4,3,2,1,0:T(8,128)(2,1)}), bf16[4,2,4,128,128]{4,3,2,1,0:T(8,128)(2,1)S(1)}, u32[]{:S(2)}, u32[]{:S(2)}) %all-to-all-start) | async-done | bytes 1048608 | tf_op jit(solution)/shard_map/all_to_all | solution.py:406
  32.3 2.2 %forward.1 = f32[8,4,8,128]{3,2,1,0:T(8,128)S(1)} custom-call(s32[12]{0:T(128)S(1)} %stack.84.scalars, s32[4]{0:T(128)S(1)} %copy-done.7, s32[4]{0:T(128)S(1)} %copy-done.8, bf16[4,2,4,128,128]{4,3,2,1,0:T(8,128)(2,1)S(1)} %all-to-all-done.mine, bf16[4,512,256]{2,1,0:T(8,128)(2,1)S(1)} %project.1.kv_ref, bf16[4,512,256]{2,1,0:T(8,128)(2,1)S(1)} %collective-permute-done.mate_ref), custom_call_target="tpu_custom_call" | custom-call | tf_op jit(solution)/shard_map/forward/pallas_call | solution.py:118
  34.5 11.1 %all_to_all.20.stat_ref = f32[8,4,8,128]{3,2,1,0:T(8,128)S(1)} all-to-all(f32[8,4,8,128]{3,2,1,0:T(8,128)S(1)} %forward.1), channel_id=1, replica_groups={{0,8,16,24,32,40,48,56},{4,12,20,28,36,44,52,60},{1,9,17,25,33,41,49,57..., dimensions={0} | all-to-all | bytes 262144 | tf_op jit(solution)/shard_map/all_to_all | solution.py:421
  45.5 3.0 %shard_map.86 = (bf16[4,2,4,2,16,128]{5,4,3,2,1,0:T(8,128)(2,1)S(1)}, bf16[4,2,4,2,16,128]{5,4,3,2,1,0:T(8,128)(2,1)S(1)}, bf16[4,256,256]{2,1,0:T(8,128)(2,1)S(1)}, bf16[4,256,256]{2,1,0:T(8,128)(2,1)S(1)}) custom-call(s32[12]{0:T(128)S(1)} %stack.84.scalars, s32[4]{0:T(128)S(1)} %copy-done.7, s32[4]{0:T(128)S(1)} %copy-done.8, ...), custom_call_target="tpu_custom_call" | custom-call | tf_op jit(solution)/shard_map/pallas_call | solution.py:202
  48.5 0.7 copy-done.9
  49.2 4.2 %shard_map.85 = (bf16[4,2,4,2,16,128]{5,4,3,2,1,0:T(8,128)(2,1)S(1)}, bf16[4,2,4,2,16,128]{5,4,3,2,1,0:T(8,128)(2,1)S(1)}, bf16[4,256,256]{2,1,0:T(8,128)(2,1)S(...) custom-call(s32[12]{0:T(128)S(1)} %stack.84.scalars, s32[4]{0:T(128)S(1)} %copy-done.7, s32[4]{0:T(128)S(1)} %copy-done.8, ...), custom_call_target="tpu_custom_call" | custom-call | tf_op jit(solution)/shard_map/pallas_call | solution.py:202
  53.5 0.7 shard_map.94
  54.3 0.6 collective-permute-start.16
  54.9 2.7 %collective-permute-start.17 = (bf16[128,1024]{1,0:T(8,128)(2,1)S(1)}, bf16[128,1024]{1,0:T(8,128)(2,1)S(1)}, u32[]{:S(2)}, u32[]{:S(2)}) collective-permute-start(bf16[128,1024]{1,0:T(8,128)(2,1)S(1)} %get-tuple-element.72), channel_id=1, source_target_pairs={{0,192},{64,0},{128,64},{192,128},{1,193},{65,1},{129,65},{193,129... | collective-permute-start | bytes 786440 | tf_op jit(solution)/shard_map/ppermute | solution.py:403
  57.6 1.3 shard_map.96
  59.2 1.8 %collective-permute-start.20 = (bf16[128,1024]{1,0:T(8,128)(2,1)S(1)}, bf16[128,1024]{1,0:T(8,128)(2,1)S(1)}, u32[]{:S(2)}, u32[]{:S(2)}) collective-permute-start(bf16[128,1024]{1,0:T(8,128)(2,1)S(1)} %get-tuple-element.75), channel_id=1, source_target_pairs={{0,64},{64,128},{128,192},{192,0},{1,65},{65,129},{129,193},{193,1... | collective-permute-start | bytes 786440 | tf_op jit(solution)/shard_map/ppermute | solution.py:400
  61.0 3.7 %collective-permute-done.16.from_down = bf16[128,1024]{1,0:T(8,128)(2,1)S(1)} collective-permute-done((bf16[128,1024]{1,0:T(8,128)(2,1)S(1)}, bf16[128,1024]{1,0:T(8,128)(2,1)S(1)}, u32[]{:S(2)}, u32[]{:S(2)}) %collective-permute-start.16) | collective-permute-done | bytes 262176 | tf_op jit(solution)/shard_map/ppermute | solution.py:400
  65.0 3.5 %collective-permute-start.21 = (bf16[128,1024]{1,0:T(8,128)(2,1)S(1)}, bf16[128,1024]{1,0:T(8,128)(2,1)S(1)}, u32[]{:S(2)}, u32[]{:S(2)}) collective-permute-start(bf16[128,1024]{1,0:T(8,128)(2,1)S(1)} %get-tuple-element.76), channel_id=1, source_target_pairs={{0,192},{64,0},{128,64},{192,128},{1,193},{65,1},{129,65},{193,129... | collective-permute-start | bytes 786440 | tf_op jit(solution)/shard_map/ppermute | solution.py:403
  68.5 2.9 %shard_map.95.own = bf16[256,1024]{1,0:T(8,128)(2,1)S(1)} custom-call(s32[12]{0:T(128)S(1)} %stack.84.scalars, bf16[4,256,256]{2,1,0:T(8,128)(2,1)S(1)} %get-tuple-element.68.grads, bf16[4,4096,256]{2,1,0:T(8,128)(2,1)} %w_hbm.7), custom_call_target="tpu_custom_call" | custom-call | tf_op jit(solution)/shard_map/pallas_call | solution.py:264
  71.4 4.1 %collective-permute-done.18.refs_0_ = bf16[128,1024]{1,0:T(8,128)(2,1)S(1)} collective-permute-done((bf16[128,1024]{1,0:T(8,128)(2,1)S(1)}, bf16[128,1024]{1,0:T(8,128)(2,1)S(1)}, u32[]{:S(2)}, u32[]{:S(2)}) %collective-permute-start.18) | collective-permute-done | bytes 262176 | tf_op jit(solution)/shard_map/ppermute | solution.py:400
  75.5 1.0 shard_map.98
  76.5 7.6 %all-to-all-start.3 = ((bf16[4,256,256]{2,1,0:T(8,128)(2,1)}), bf16[4,256,256]{2,1,0:T(8,128)(2,1)S(1)}, u32[]{:S(2)}, u32[]{:S(2)}) async-start(bf16[4,256,256]{2,1,0:T(8,128)(2,1)} %shard_map.98), calls=%async_computation.3 | async-start | bytes 1048576 | tf_op jit(solution)/shard_map/all_to_all | solution.py:406
  84.1 2.8 %copy-done.1 = bf16[3,4,1024,256]{3,2,1,0:T(8,128)(2,1)S(1)} copy-done((bf16[3,4,1024,256]{3,2,1,0:T(8,128)(2,1)S(1)}, bf16[3,4,1024,256]{3,2,1,0:T(8,128)(2,1)}, u32[]{:S(2)}) %copy-start.1) | copy-done | bytes 6291480
  86.9 0.7 shard_map.89
  87.7 3.2 %collective-permute-start.10 = (bf16[128,1024]{1,0:T(8,128)(2,1)S(1)}, bf16[128,1024]{1,0:T(8,128)(2,1)S(1)}, u32[]{:S(2)}, u32[]{:S(2)}) collective-permute-start(bf16[128,1024]{1,0:T(8,128)(2,1)S(1)} %get-tuple-element.61), channel_id=1, source_target_pairs={{0,192},{64,0},{128,64},{192,128},{1,193},{65,1},{129,65},{193,129... | collective-permute-start | bytes 786440 | tf_op jit(solution)/shard_map/ppermute | solution.py:403
  90.9 0.9 collective-permute-start.2
  91.8 1.1 collective-permute-start.1
  92.9 1.3 shard_map.91
  94.2 1.8 %collective-permute-start.12 = (bf16[128,1024]{1,0:T(8,128)(2,1)S(1)}, bf16[128,1024]{1,0:T(8,128)(2,1)S(1)}, u32[]{:S(2)}, u32[]{:S(2)}) collective-permute-start(bf16[128,1024]{1,0:T(8,128)(2,1)S(1)} %get-tuple-element.63), channel_id=1, source_target_pairs={{0,192},{64,0},{128,64},{192,128},{1,193},{65,1},{129,65},{193,129... | collective-permute-start | bytes 786440 | tf_op jit(solution)/shard_map/ppermute | solution.py:403
  96.1 0.4 collective-permute-done.9.from_down
  96.5 0.9 collective-permute-done.10.from_up
  97.5 2.0 %collective-permute-start.11 = (bf16[128,1024]{1,0:T(8,128)(2,1)S(1)}, bf16[128,1024]{1,0:T(8,128)(2,1)S(1)}, u32[]{:S(2)}, u32[]{:S(2)}) collective-permute-start(bf16[128,1024]{1,0:T(8,128)(2,1)S(1)} %get-tuple-element.62), channel_id=1, source_target_pairs={{0,64},{64,128},{128,192},{192,0},{1,65},{65,129},{129,193},{193,1... | collective-permute-start | bytes 786440 | tf_op jit(solution)/shard_map/ppermute | solution.py:400
  99.4 3.9 %collective-permute-done.2.refs_3_ = bf16[4,2,4,2,16,128]{5,4,3,2,1,0:T(8,128)(2,1)S(1)} collective-permute-done((bf16[4,2,4,2,16,128]{5,4,3,2,1,0:T(8,128)(2,1)S(1)}, bf16[4,2,4,2,16,128]{5,4,3,2,1,0:T(8,128)(2,1)S(1)}, u32[]{:S(2)}, u32[]{:S(2)}) %collective-permute-start.2) | collective-permute-done | bytes 262176 | tf_op jit(solution)/shard_map/ppermute | solution.py:432
  103.3 3.2 %collective-permute-start.14 = (bf16[128,1024]{1,0:T(8,128)(2,1)S(1)}, bf16[128,1024]{1,0:T(8,128)(2,1)S(1)}, u32[]{:S(2)}, u32[]{:S(2)}) collective-permute-start(bf16[128,1024]{1,0:T(8,128)(2,1)S(1)} %get-tuple-element.65), channel_id=1, source_target_pairs={{0,192},{64,0},{128,64},{192,128},{1,193},{65,1},{129,65},{193,129... | collective-permute-start | bytes 786440 | tf_op jit(solution)/shard_map/ppermute | solution.py:403
  106.5 1.4 %collective-permute-done.1.refs_2_ = bf16[4,2,4,2,16,128]{5,4,3,2,1,0:T(8,128)(2,1)S(1)} collective-permute-done((bf16[4,2,4,2,16,128]{5,4,3,2,1,0:T(8,128)(2,1)S(1)}, bf16[4,2,4,2,16,128]{5,4,3,2,1,0:T(8,128)(2,1)S(1)}, u32[]{:S(2)}, u32[]{:S(2)}) %collective-permute-start.1) | collective-permute-done | bytes 262176 | tf_op jit(solution)/shard_map/ppermute | solution.py:432
  108.0 1.4 %collective-permute-start.3 = (bf16[2,2,4,4,16,128]{5,4,3,2,1,0:T(8,128)(2,1)S(1)}, bf16[2,2,4,4,16,128]{5,4,3,2,1,0:T(8,128)(2,1)S(1)}, u32[]{:S(2)}, u32[]{:S(2)}) collective-permute-start(bf16[2,2,4,4,16,128]{5,4,3,2,1,0:T(8,128)(2,1)S(1)} %get-tuple-element.47), channel_id=1, source_target_pairs={{0,8},{4,12},{8,0},{12,4},{16,24},{20,28},{24,16},{28,20},{32,40},... | collective-permute-start | bytes 786440 | tf_op jit(solution)/shard_map/ppermute | solution.py:447
  109.4 2.9 %shard_map.90.own = bf16[256,1024]{1,0:T(8,128)(2,1)S(1)} custom-call(s32[12]{0:T(128)S(1)} %stack.84.scalars, bf16[4,256,256]{2,1,0:T(8,128)(2,1)S(1)} %get-tuple-element.57.grads, bf16[4,4096,256]{2,1,0:T(8,128)(2,1)} %w_hbm.7), custom_call_target="tpu_custom_call" | custom-call | tf_op jit(solution)/shard_map/pallas_call | solution.py:264
  112.4 1.0 shard_map.93
  113.3 6.8 %all-to-all-start.2 = ((bf16[4,256,256]{2,1,0:T(8,128)(2,1)}), bf16[4,256,256]{2,1,0:T(8,128)(2,1)S(1)}, u32[]{:S(2)}, u32[]{:S(2)}) async-start(bf16[4,256,256]{2,1,0:T(8,128)(2,1)} %shard_map.93), calls=%async_computation.2 | async-start | bytes 1048576 | tf_op jit(solution)/shard_map/all_to_all | solution.py:406
  120.2 0.4 collective-permute-start.4
  120.6 6.1 %collective-permute-done.4.came = bf16[1,2,4,4,16,128]{5,4,3,2,1,0:T(8,128)(2,1)S(1)} collective-permute-done((bf16[1,2,4,4,16,128]{5,4,3,2,1,0:T(8,128)(2,1)S(1)}, bf16[1,2,4,4,16,128]{5,4,3,2,1,0:T(8,128)(2,1)S(1)}, u32[]{:S(2)}, u32[]{:S(2)}) %collective-permute-start.4) | collective-permute-done | bytes 131104 | tf_op jit(solution)/shard_map/ppermute | solution.py:447
  126.7 0.6 deal.1
  127.4 4.1 %collective-permute-start.6 = (bf16[2,4,16,128]{3,2,1,0:T(8,128)(2,1)S(1)}, bf16[2,4,16,128]{3,2,1,0:T(8,128)(2,1)S(1)}, u32[]{:S(2)}, u32[]{:S(2)}) collective-permute-start(bf16[2,4,16,128]{3,2,1,0:T(8,128)(2,1)S(1)} %get-tuple-element.52), channel_id=1, source_target_pairs={{0,128},{64,192},{128,0},{192,64},{1,129},{65,193},{129,1},{193,65... | collective-permute-start | bytes 98312 | tf_op jit(solution)/shard_map/ppermute | solution.py:450
  131.5 1.0 collective-permute-done.5
  132.5 1.3 collective-permute-done.6
  133.8 1.7 %collective-permute-done.7 = bf16[2,4,16,128]{3,2,1,0:T(8,128)(2,1)S(1)} collective-permute-done((bf16[2,4,16,128]{3,2,1,0:T(8,128)(2,1)S(1)}, bf16[2,4,16,128]{3,2,1,0:T(8,128)(2,1)S(1)}, u32[]{:S(2)}, u32[]{:S(2)}) %collective-permute-start.7) | collective-permute-done | bytes 32800 | tf_op jit(solution)/shard_map/ppermute | solution.py:403
  135.6 0.7 copy.14
  136.2 0.7 copy.13
  136.9 0.8 finish.1
  (60 shorter events, 1.5 us)
Async XLA Ops:
  0.6 8.5 %copy-start.13 = (bf16[1,4,256,4,128]{4,3,2,1,0:T(4,128)(2,1)S(1)}, bf16[1,4,256,4,128]{4,3,2,1,0:T(4,128)(2,1)}, u32[]{:S(2)}) copy-start(bf16[1,4,256,4,128]{4,3,2,1,0:T(4,128)(2,1)} %param.9) | copy-start | bytes 3145732
  9.0 23.2 %copy-start.7 = (s32[4]{0:T(128)S(1)}, s32[4]{0:T(128)}, u32[]{:S(2)}) copy-start(s32[4]{0:T(128)} %src_len.5) | copy-start | bytes 52
  9.0 23.2 %copy-start.8 = (s32[4]{0:T(128)S(1)}, s32[4]{0:T(128)}, u32[]{:S(2)}) copy-start(s32[4]{0:T(128)} %tgt_len.5) | copy-start | bytes 52
  9.1 23.2 %collective-permute-start = (bf16[4,512,256]{2,1,0:T(8,128)(2,1)S(1)}, bf16[4,512,256]{2,1,0:T(8,128)(2,1)S(1)}, u32[]{:S(2)}, u32[]{:S(2)}) collective-permute-start(bf16[4,512,256]{2,1,0:T(8,128)(2,1)S(1)} %project.1.kv_ref), channel_id=1, source_target_pairs={{0,4},{4,0},{8,12},{12,8},{16,20},{20,16},{24,28},{28,24},{32,36},... | collective-permute-start | bytes 3145736 | tf_op jit(solution)/shard_map/ppermute | solution.py:417
  12.1 20.2 %all-to-all-start = ((bf16[4,2,4,128,128]{4,3,2,1,0:T(8,128)(2,1)}), bf16[4,2,4,128,128]{4,3,2,1,0:T(8,128)(2,1)S(1)}, u32[]{:S(2)}, u32[]{:S(2)}) async-start(bf16[4,2,4,128,128]{4,3,2,1,0:T(8,128)(2,1)} %pad_maximum_fusion), calls=%async_computation | async-start | bytes 2097152 | tf_op jit(solution)/shard_map/all_to_all | solution.py:406
  48.5 0.7 copy-start.9
  49.2 4.3 %collective-permute-start.15 = (bf16[4,256,256]{2,1,0:T(8,128)(2,1)S(1)}, bf16[4,256,256]{2,1,0:T(8,128)(2,1)S(1)}, u32[]{:S(2)}, u32[]{:S(2)}) collective-permute-start(bf16[4,256,256]{2,1,0:T(8,128)(2,1)S(1)} %get-tuple-element.67), channel_id=1, source_target_pairs={{0,4},{4,0},{8,12},{12,8},{16,20},{20,16},{24,28},{28,24},{32,36},... | collective-permute-start | bytes 1572872 | tf_op jit(solution)/shard_map/ppermute | solution.py:431
  53.5 5.4 %copy-start = (bf16[3,4,1024,256]{3,2,1,0:T(8,128)(2,1)}, bf16[3,4,1024,256]{3,2,1,0:T(8,128)(2,1)S(1)}, u32[]{:S(2)}) copy-start(bf16[3,4,1024,256]{3,2,1,0:T(8,128)(2,1)S(1)} %get-tuple-element.56.w_ref) | copy-start | bytes 18874372
  53.5 5.4 %copy-start.3 = (bf16[4,256,256]{2,1,0:T(8,128)(2,1)}, bf16[4,256,256]{2,1,0:T(8,128)(2,1)S(1)}, u32[]{:S(2)}) copy-start(bf16[4,256,256]{2,1,0:T(8,128)(2,1)S(1)} %get-tuple-element.54.grads_in) | copy-start | bytes 1572868
  53.5 5.4 %copy-start.5 = (bf16[4,2,4,2,16,128]{5,4,3,2,1,0:T(8,128)(2,1)}, bf16[4,2,4,2,16,128]{5,4,3,2,1,0:T(8,128)(2,1)S(1)}, u32[]{:S(2)}) copy-start(bf16[4,2,4,2,16,128]{5,4,3,2,1,0:T(8,128)(2,1)S(1)} %get-tuple-element.42.refs_0_) | copy-start | bytes 786436
  53.5 5.4 %copy-start.11 = (bf16[4,2,4,2,16,128]{5,4,3,2,1,0:T(8,128)(2,1)}, bf16[4,2,4,2,16,128]{5,4,3,2,1,0:T(8,128)(2,1)S(1)}, u32[]{:S(2)}) copy-start(bf16[4,2,4,2,16,128]{5,4,3,2,1,0:T(8,128)(2,1)S(1)} %get-tuple-element.44) | copy-start | bytes 786436
  54.3 10.5 %collective-permute-start.16 = (bf16[128,1024]{1,0:T(8,128)(2,1)S(1)}, bf16[128,1024]{1,0:T(8,128)(2,1)S(1)}, u32[]{:S(2)}, u32[]{:S(2)}) collective-permute-start(bf16[128,1024]{1,0:T(8,128)(2,1)S(1)} %get-tuple-element.70), channel_id=1, source_target_pairs={{0,64},{64,128},{128,192},{192,0},{1,65},{65,129},{129,193},{193,1... | collective-permute-start | bytes 786440 | tf_op jit(solution)/shard_map/ppermute | solution.py:400
  54.9 9.8 %collective-permute-start.17 = (bf16[128,1024]{1,0:T(8,128)(2,1)S(1)}, bf16[128,1024]{1,0:T(8,128)(2,1)S(1)}, u32[]{:S(2)}, u32[]{:S(2)}) collective-permute-start(bf16[128,1024]{1,0:T(8,128)(2,1)S(1)} %get-tuple-element.72), channel_id=1, source_target_pairs={{0,192},{64,0},{128,64},{192,128},{1,193},{65,1},{129,65},{193,129... | collective-permute-start | bytes 786440 | tf_op jit(solution)/shard_map/ppermute | solution.py:403
  57.6 26.5 %collective-permute-start.8 = (bf16[4,256,256]{2,1,0:T(8,128)(2,1)}, bf16[4,256,256]{2,1,0:T(8,128)(2,1)S(1)}, u32[]{:S(2)}, u32[]{:S(2)}) collective-permute-start(bf16[4,256,256]{2,1,0:T(8,128)(2,1)} %get-tuple-element.55), channel_id=1, source_target_pairs={{0,4},{4,0},{8,12},{12,8},{16,20},{20,16},{24,28},{28,24},{32,36},... | collective-permute-start | bytes 1572872 | tf_op jit(solution)/shard_map/ppermute | solution.py:431
  58.9 12.5 %collective-permute-start.19 = (bf16[128,1024]{1,0:T(8,128)(2,1)S(1)}, bf16[128,1024]{1,0:T(8,128)(2,1)S(1)}, u32[]{:S(2)}, u32[]{:S(2)}) collective-permute-start(bf16[128,1024]{1,0:T(8,128)(2,1)S(1)} %get-tuple-element.74), channel_id=1, source_target_pairs={{0,192},{64,0},{128,64},{192,128},{1,193},{65,1},{129,65},{193,129... | collective-permute-start | bytes 786440 | tf_op jit(solution)/shard_map/ppermute | solution.py:403
  59.2 12.2 %collective-permute-start.20 = (bf16[128,1024]{1,0:T(8,128)(2,1)S(1)}, bf16[128,1024]{1,0:T(8,128)(2,1)S(1)}, u32[]{:S(2)}, u32[]{:S(2)}) collective-permute-start(bf16[128,1024]{1,0:T(8,128)(2,1)S(1)} %get-tuple-element.75), channel_id=1, source_target_pairs={{0,64},{64,128},{128,192},{192,0},{1,65},{65,129},{129,193},{193,1... | collective-permute-start | bytes 786440 | tf_op jit(solution)/shard_map/ppermute | solution.py:400
  64.9 10.6 %collective-permute-start.18 = (bf16[128,1024]{1,0:T(8,128)(2,1)S(1)}, bf16[128,1024]{1,0:T(8,128)(2,1)S(1)}, u32[]{:S(2)}, u32[]{:S(2)}) collective-permute-start(bf16[128,1024]{1,0:T(8,128)(2,1)S(1)} %get-tuple-element.73), channel_id=1, source_target_pairs={{0,64},{64,128},{128,192},{192,0},{1,65},{65,129},{129,193},{193,1... | collective-permute-start | bytes 786440 | tf_op jit(solution)/shard_map/ppermute | solution.py:400
  65.0 19.1 %copy-start.4 = (bf16[4,256,256]{2,1,0:T(8,128)(2,1)S(1)}, bf16[4,256,256]{2,1,0:T(8,128)(2,1)}, u32[]{:S(2)}) copy-start(bf16[4,256,256]{2,1,0:T(8,128)(2,1)} %copy-done.3) | copy-start | bytes 1572868
  65.0 10.5 %collective-permute-start.21 = (bf16[128,1024]{1,0:T(8,128)(2,1)S(1)}, bf16[128,1024]{1,0:T(8,128)(2,1)S(1)}, u32[]{:S(2)}, u32[]{:S(2)}) collective-permute-start(bf16[128,1024]{1,0:T(8,128)(2,1)S(1)} %get-tuple-element.76), channel_id=1, source_target_pairs={{0,192},{64,0},{128,64},{192,128},{1,193},{65,1},{129,65},{193,129... | collective-permute-start | bytes 786440 | tf_op jit(solution)/shard_map/ppermute | solution.py:403
  71.3 19.6 %copy-start.10 = (bf16[4,2,4,2,16,128]{5,4,3,2,1,0:T(8,128)(2,1)S(1)}, bf16[4,2,4,2,16,128]{5,4,3,2,1,0:T(8,128)(2,1)}, u32[]{:S(2)}) copy-start(bf16[4,2,4,2,16,128]{5,4,3,2,1,0:T(8,128)(2,1)} %copy-done.9) | copy-start | bytes 786436
  71.4 20.5 %copy-start.12 = (bf16[4,2,4,2,16,128]{5,4,3,2,1,0:T(8,128)(2,1)S(1)}, bf16[4,2,4,2,16,128]{5,4,3,2,1,0:T(8,128)(2,1)}, u32[]{:S(2)}) copy-start(bf16[4,2,4,2,16,128]{5,4,3,2,1,0:T(8,128)(2,1)} %copy-done.11) | copy-start | bytes 786436
  76.5 36.9 %all-to-all-start.3 = ((bf16[4,256,256]{2,1,0:T(8,128)(2,1)}), bf16[4,256,256]{2,1,0:T(8,128)(2,1)S(1)}, u32[]{:S(2)}, u32[]{:S(2)}) async-start(bf16[4,256,256]{2,1,0:T(8,128)(2,1)} %shard_map.98), calls=%async_computation.3 | async-start | bytes 1048576 | tf_op jit(solution)/shard_map/all_to_all | solution.py:406
  84.1 2.8 %copy-start.1 = (bf16[3,4,1024,256]{3,2,1,0:T(8,128)(2,1)S(1)}, bf16[3,4,1024,256]{3,2,1,0:T(8,128)(2,1)}, u32[]{:S(2)}) copy-start(bf16[3,4,1024,256]{3,2,1,0:T(8,128)(2,1)} %copy-done) | copy-start | bytes 18874372
  86.8 6.1 %copy-start.2 = (bf16[3,4,1024,256]{3,2,1,0:T(8,128)(2,1)S(1)}, bf16[3,4,1024,256]{3,2,1,0:T(8,128)(2,1)}, u32[]{:S(2)}) copy-start(bf16[3,4,1024,256]{3,2,1,0:T(8,128)(2,1)} %copy-done) | copy-start | bytes 18874372
  86.9 21.1 %copy-start.6 = (bf16[4,2,4,2,16,128]{5,4,3,2,1,0:T(8,128)(2,1)S(1)}, bf16[4,2,4,2,16,128]{5,4,3,2,1,0:T(8,128)(2,1)}, u32[]{:S(2)}) copy-start(bf16[4,2,4,2,16,128]{5,4,3,2,1,0:T(8,128)(2,1)} %copy-done.5) | copy-start | bytes 786436
  87.6 8.9 %collective-permute-start.9 = (bf16[128,1024]{1,0:T(8,128)(2,1)S(1)}, bf16[128,1024]{1,0:T(8,128)(2,1)S(1)}, u32[]{:S(2)}, u32[]{:S(2)}) collective-permute-start(bf16[128,1024]{1,0:T(8,128)(2,1)S(1)} %get-tuple-element.59), channel_id=1, source_target_pairs={{0,64},{64,128},{128,192},{192,0},{1,65},{65,129},{129,193},{193,1... | collective-permute-start | bytes 786440 | tf_op jit(solution)/shard_map/ppermute | solution.py:400
  87.7 9.6 %collective-permute-start.10 = (bf16[128,1024]{1,0:T(8,128)(2,1)S(1)}, bf16[128,1024]{1,0:T(8,128)(2,1)S(1)}, u32[]{:S(2)}, u32[]{:S(2)}) collective-permute-start(bf16[128,1024]{1,0:T(8,128)(2,1)S(1)} %get-tuple-element.61), channel_id=1, source_target_pairs={{0,192},{64,0},{128,64},{192,128},{1,193},{65,1},{129,65},{193,129... | collective-permute-start | bytes 786440 | tf_op jit(solution)/shard_map/ppermute | solution.py:403
  90.9 12.4 %collective-permute-start.2 = (bf16[4,2,4,2,16,128]{5,4,3,2,1,0:T(8,128)(2,1)S(1)}, bf16[4,2,4,2,16,128]{5,4,3,2,1,0:T(8,128)(2,1)S(1)}, u32[]{:S(2)}, u32[]{:S(2)}) collective-permute-start(bf16[4,2,4,2,16,128]{5,4,3,2,1,0:T(8,128)(2,1)S(1)} %copy-done.10), channel_id=1, source_target_pairs={{0,32},{4,36},{8,40},{12,44},{16,48},{20,52},{24,56},{28,60},{32,0... | collective-permute-start | bytes 786440 | tf_op jit(solution)/shard_map/ppermute | solution.py:432
  91.8 16.1 %collective-permute-start.1 = (bf16[4,2,4,2,16,128]{5,4,3,2,1,0:T(8,128)(2,1)S(1)}, bf16[4,2,4,2,16,128]{5,4,3,2,1,0:T(8,128)(2,1)S(1)}, u32[]{:S(2)}, u32[]{:S(2)}) collective-permute-start(bf16[4,2,4,2,16,128]{5,4,3,2,1,0:T(8,128)(2,1)S(1)} %copy-done.12), channel_id=1, source_target_pairs={{0,32},{4,36},{8,40},{12,44},{16,48},{20,52},{24,56},{28,60},{32,0... | collective-permute-start | bytes 786440 | tf_op jit(solution)/shard_map/ppermute | solution.py:432
  94.2 18.1 %collective-permute-start.12 = (bf16[128,1024]{1,0:T(8,128)(2,1)S(1)}, bf16[128,1024]{1,0:T(8,128)(2,1)S(1)}, u32[]{:S(2)}, u32[]{:S(2)}) collective-permute-start(bf16[128,1024]{1,0:T(8,128)(2,1)S(1)} %get-tuple-element.63), channel_id=1, source_target_pairs={{0,192},{64,0},{128,64},{192,128},{1,193},{65,1},{129,65},{193,129... | collective-permute-start | bytes 786440 | tf_op jit(solution)/shard_map/ppermute | solution.py:403
  96.5 15.9 %collective-permute-start.13 = (bf16[128,1024]{1,0:T(8,128)(2,1)S(1)}, bf16[128,1024]{1,0:T(8,128)(2,1)S(1)}, u32[]{:S(2)}, u32[]{:S(2)}) collective-permute-start(bf16[128,1024]{1,0:T(8,128)(2,1)S(1)} %get-tuple-element.64), channel_id=1, source_target_pairs={{0,64},{64,128},{128,192},{192,0},{1,65},{65,129},{129,193},{193,1... | collective-permute-start | bytes 786440 | tf_op jit(solution)/shard_map/ppermute | solution.py:400
  97.5 14.9 %collective-permute-start.11 = (bf16[128,1024]{1,0:T(8,128)(2,1)S(1)}, bf16[128,1024]{1,0:T(8,128)(2,1)S(1)}, u32[]{:S(2)}, u32[]{:S(2)}) collective-permute-start(bf16[128,1024]{1,0:T(8,128)(2,1)S(1)} %get-tuple-element.62), channel_id=1, source_target_pairs={{0,64},{64,128},{128,192},{192,0},{1,65},{65,129},{129,193},{193,1... | collective-permute-start | bytes 786440 | tf_op jit(solution)/shard_map/ppermute | solution.py:400
  103.3 9.1 %collective-permute-start.14 = (bf16[128,1024]{1,0:T(8,128)(2,1)S(1)}, bf16[128,1024]{1,0:T(8,128)(2,1)S(1)}, u32[]{:S(2)}, u32[]{:S(2)}) collective-permute-start(bf16[128,1024]{1,0:T(8,128)(2,1)S(1)} %get-tuple-element.65), channel_id=1, source_target_pairs={{0,192},{64,0},{128,64},{192,128},{1,193},{65,1},{129,65},{193,129... | collective-permute-start | bytes 786440 | tf_op jit(solution)/shard_map/ppermute | solution.py:403
  108.0 12.1 %collective-permute-start.3 = (bf16[2,2,4,4,16,128]{5,4,3,2,1,0:T(8,128)(2,1)S(1)}, bf16[2,2,4,4,16,128]{5,4,3,2,1,0:T(8,128)(2,1)S(1)}, u32[]{:S(2)}, u32[]{:S(2)}) collective-permute-start(bf16[2,2,4,4,16,128]{5,4,3,2,1,0:T(8,128)(2,1)S(1)} %get-tuple-element.47), channel_id=1, source_target_pairs={{0,8},{4,12},{8,0},{12,4},{16,24},{20,28},{24,16},{28,20},{32,40},... | collective-permute-start | bytes 786440 | tf_op jit(solution)/shard_map/ppermute | solution.py:447
  113.3 23.6 %all-to-all-start.2 = ((bf16[4,256,256]{2,1,0:T(8,128)(2,1)}), bf16[4,256,256]{2,1,0:T(8,128)(2,1)S(1)}, u32[]{:S(2)}, u32[]{:S(2)}) async-start(bf16[4,256,256]{2,1,0:T(8,128)(2,1)} %shard_map.93), calls=%async_computation.2 | async-start | bytes 1048576 | tf_op jit(solution)/shard_map/all_to_all | solution.py:406
  120.2 6.6 %collective-permute-start.4 = (bf16[1,2,4,4,16,128]{5,4,3,2,1,0:T(8,128)(2,1)S(1)}, bf16[1,2,4,4,16,128]{5,4,3,2,1,0:T(8,128)(2,1)S(1)}, u32[]{:S(2)}, u32[]{:S(2)}) collective-permute-start(bf16[1,2,4,4,16,128]{5,4,3,2,1,0:T(8,128)(2,1)S(1)} %get-tuple-element.49), channel_id=1, source_target_pairs={{0,16},{4,20},{8,24},{12,28},{16,0},{20,4},{24,8},{28,12},{32,48},... | collective-permute-start | bytes 393224 | tf_op jit(solution)/shard_map/ppermute | solution.py:447
  127.3 5.2 %collective-permute-start.5 = (bf16[2,4,16,128]{3,2,1,0:T(8,128)(2,1)S(1)}, bf16[2,4,16,128]{3,2,1,0:T(8,128)(2,1)S(1)}, u32[]{:S(2)}, u32[]{:S(2)}) collective-permute-start(bf16[2,4,16,128]{3,2,1,0:T(8,128)(2,1)S(1)} %get-tuple-element.51), channel_id=1, source_target_pairs={{0,64},{64,128},{128,192},{192,0},{1,65},{65,129},{129,193},{193,1... | collective-permute-start | bytes 98312 | tf_op jit(solution)/shard_map/ppermute | solution.py:400
  127.4 6.4 %collective-permute-start.6 = (bf16[2,4,16,128]{3,2,1,0:T(8,128)(2,1)S(1)}, bf16[2,4,16,128]{3,2,1,0:T(8,128)(2,1)S(1)}, u32[]{:S(2)}, u32[]{:S(2)}) collective-permute-start(bf16[2,4,16,128]{3,2,1,0:T(8,128)(2,1)S(1)} %get-tuple-element.52), channel_id=1, source_target_pairs={{0,128},{64,192},{128,0},{192,64},{1,129},{65,193},{129,1},{193,65... | collective-permute-start | bytes 98312 | tf_op jit(solution)/shard_map/ppermute | solution.py:450
  131.5 3.9 %collective-permute-start.7 = (bf16[2,4,16,128]{3,2,1,0:T(8,128)(2,1)S(1)}, bf16[2,4,16,128]{3,2,1,0:T(8,128)(2,1)S(1)}, u32[]{:S(2)}, u32[]{:S(2)}) collective-permute-start(bf16[2,4,16,128]{3,2,1,0:T(8,128)(2,1)S(1)} %get-tuple-element.53), channel_id=1, source_target_pairs={{0,192},{64,0},{128,64},{192,128},{1,193},{65,1},{129,65},{193,129... | collective-permute-start | bytes 98312 | tf_op jit(solution)/shard_map/ppermute | solution.py:403

commit v7 on v4

--- a/solution.py
+++ b/solution.py
@@ -14,6 +14,7 @@
 TN = (((0,), (0,)), ((), ()))
 CHUNKS = 2
 GROUPED = (1, 3)
+LEAVING = 3
 
 
 def dot(a, b, dims):
@@ -125,12 +126,10 @@
     )(scalars, src_len, tgt_len, *held(mine, kv, mate))
 
 
-def terms_of(grads, w_ref, place):
+def terms_of(grads, weights):
     terms = None
-    part = w_ref.shape[1] // 4
-    at = pl.ds(pl.multiple_of(place * part, part), part)
     for r in range(grads.shape[0]):
-        term = dot(grads[r], w_ref[r, at, :], NT)
+        term = dot(grads[r], weights[r], NT)
         terms = term if terms is None else terms + term
     return low(terms)
 
@@ -146,9 +145,12 @@
     takes = []
     if rest:
         w_ref, w_sem = rest
-        take = pltpu.make_async_copy(w_hbm, w_ref, w_sem)
-        take.start()
-        takes.append(take)
+        part = w_ref.shape[2]
+        for k in range(LEAVING):
+            at = pl.ds(pl.multiple_of(scalars[4 + k] * part, part), part)
+            take = pltpu.make_async_copy(w_hbm.at[:, at], w_ref.at[k], w_sem.at[k])
+            take.start()
+            takes.append(take)
 
     def one(k, carry):
         b = start + k
@@ -196,8 +198,8 @@
     outs = (half, half, grads, grads)
     scratch = []
     if chunk == 0:
-        outs += (kept_here(*weights.shape),)
-        scratch = [pltpu.SemaphoreType.DMA]
+        outs += (kept_here(LEAVING, layers, weights.shape[1] // 4, weights.shape[2]),)
+        scratch = [pltpu.SemaphoreType.DMA((LEAVING,))]
     return pl.pallas_call(
         functools.partial(backward_kernel, chunk * samples, keys),
         out_shape=outs,
@@ -208,33 +210,33 @@
     )(scalars, src_len, tgt_len, *held(mine, kv, mate, stats), in_hbm(weights))
 
 
-def join_kernel(keys, scalars, grads_in, came, w_ref, grads, up_ref, down_ref):
+def join_kernel(keys, grads_in, came, w_ref, grads, up_ref, down_ref):
     grads[...] = low(wide(grads_in[...]) + wide(came[...]))
-    terms = terms_of(grads, w_ref, scalars[4])
+    terms = terms_of(grads, w_ref.at[0])
     half = keys // 2
     for k in range(grads.shape[1] // keys):
         up_ref[k * half:(k + 1) * half] = terms[k * keys:k * keys + half]
         down_ref[k * half:(k + 1) * half] = terms[k * keys + half:(k + 1) * keys]
 
 
-def join(keys, scalars, grads, came, weights):
-    far = kept_here(grads.shape[1] // 2, weights.shape[1] // 4)
+def join(keys, grads, came, weights):
+    far = kept_here(grads.shape[1] // 2, weights.shape[2])
     outs = (kept_here(*grads.shape), far, far)
     return pl.pallas_call(
         functools.partial(join_kernel, keys),
         out_shape=outs,
-        in_specs=[SCALAR] + [FAST] * 3,
+        in_specs=[FAST] * 3,
         out_specs=(FAST,) * 3,
         compiler_params=ROOM,
-    )(scalars, *held(grads, came, weights))
-
-
-def near_kernel(scalars, *refs):
+    )(*held(grads, came, weights))
+
+
+def near_kernel(*refs):
     grads, w_ref, outs = refs[:CHUNKS], refs[CHUNKS], refs[CHUNKS + 1:]
     groups = len(outs) // 2
     for side in range(2):
         done = 0
-        terms = [terms_of(g, w_ref, scalars[5 + side]) for g in grads]
+        terms = [terms_of(g, w_ref.at[1 + side]) for g in grads]
         size = terms[0].shape[0]
         for k in range(groups):
             ref = outs[side * groups + k]
@@ -247,35 +249,42 @@
             done += filled
 
 
-def near(scalars, grads, weights, keys):
-    outs = tuple(kept_here(g * keys, weights.shape[1] // 4) for g in GROUPED) * 2
+def near(grads, weights, keys):
+    outs = tuple(kept_here(g * keys, weights.shape[2]) for g in GROUPED) * 2
     return pl.pallas_call(
         near_kernel,
         out_shape=outs,
-        in_specs=[SCALAR] + [FAST] * (len(grads) + 1),
+        in_specs=[FAST] * (len(grads) + 1),
         out_specs=(FAST,) * len(outs),
         compiler_params=ROOM,
         name="near",
-    )(scalars, *held(*grads, weights))
+    )(*held(*grads, weights))
 
 
 def here_kernel(scalars, *refs):
-    grads, w_ref, out_ref = refs[:-2], refs[-2], refs[-1]
+    grads, (w_hbm, out_ref, w_ref, w_sem) = refs[:-4], refs[-4:]
+    part = w_ref.shape[1]
+    at = pl.ds(pl.multiple_of(scalars[7] * part, part), part)
+    take = pltpu.make_async_copy(w_hbm.at[:, at], w_ref, w_sem)
+    take.start()
+    take.wait()
     size = grads[0].shape[1]
     for k, part in enumerate(grads):
-        out_ref[k * size:(k + 1) * size] = terms_of(part, w_ref, scalars[7])
+        out_ref[k * size:(k + 1) * size] = terms_of(part, w_ref)
 
 
 def here(scalars, grads, weights):
+    layers, width, cols = weights.shape
     count = sum(g.shape[1] for g in grads)
     return pl.pallas_call(
         here_kernel,
-        out_shape=kept_here(count, weights.shape[1] // 4),
-        in_specs=[SCALAR] + [FAST] * (len(grads) + 1),
+        out_shape=kept_here(count, width // 4),
+        in_specs=[SCALAR] + [FAST] * len(grads) + [SLOW],
         out_specs=FAST,
+        scratch_shapes=[pltpu.VMEM((layers, width // 4, cols), jnp.bfloat16), pltpu.SemaphoreType.DMA],
         compiler_params=ROOM,
         name="here",
-    )(scalars, *held(*grads, weights))
+    )(scalars, *held(*grads), in_hbm(weights))
 
 
 def halve_kernel(parts, run, side, *refs):
@@ -446,12 +455,12 @@
         came.append(lax.ppermute(give, "seq", flip(shards, 2)))
         kept.append(keep)
     for c in range(CHUNKS):
-        part, far_up, far_down = join(src_rows, scalars, *parts[c], weights)
+        part, far_up, far_down = join(src_rows, *parts[c], weights)
         ups.append(up(far_up))
         downs.append(down(far_down))
         grads.append(part)
-    sides = near(scalars, grads, weights, src_rows)
-    own = here(scalars, grads, weights)
+    sides = near(grads, weights, src_rows)
+    own = here(scalars, grads, w_kv)
     pieces = []
     start = 0
     for c, group in enumerate(GROUPED):

time: 159 us -> 157 us (0.987)
  transfers between devices with their start and end apart: 21 -> 21, of which waited for: 12 -> 13; matrix products, arithmetic and copies ran while one was open for 3% -> 3% of each run, Pallas kernels for 10% -> 9%
where the time goes in v7:
time: 157 us; the launch traced here: 156 us
  waiting for transfers between devices  76.2 us (49%)
  starting transfers between devices  31.7 us (20%)
  Pallas kernels  30.3 us (19%)
  blocking collectives  10.8 us (7%)
  local copies, waits for them, and re-layouts  4.68 us (3%)
    ppermute x2, waiting for transfers between devices, body(): kept, came = ([keep], [lax.ppermute(give, 'seq', flip(shards, 1 << bit))])  24.6 us
    ppermute x5, waiting for transfers between devices, up(): return lax.ppermute(a, 'section', turn(4, 1))  20.4 us
    all_to_all x3, waiting for transfers between devices, swap(): return lax.all_to_all(a, axis, 0, 0, tiled=True)  20.3 us
    all_to_all x3, starting transfers between devices, swap(): return lax.all_to_all(a, axis, 0, 0, tiled=True)  15.7 us
    all_to_all x1, blocking collectives, body(): lax.all_to_all(stats, 'seq', 0, 0, axis_index_groups=same_core, tiled=True)  10.8 us
    ppermute x5, waiting for transfers between devices, down(): return lax.ppermute(a, 'section', turn(4, 3))  8.83 us
    pallas_call x1, Pallas kernels, project(): pl.pallas_call(project_kernel, out_shape=kept_here(layers, count, cols),...  8.38 us
    ppermute x5, starting transfers between devices, up(): return lax.ppermute(a, 'section', turn(4, 1))  7.97 us
  transfers between devices with their start and end apart: 21, of which 13 were waited for; matrix products, arithmetic and copies ran while one was open for 3% of the time, Pallas kernels for 9%

profile of v7, /device:TPU:56, one launch (start us, length us, event | category | flops | bytes accessed | tf_op | source)
XLA Modules:
  0.0 155.7 jit_solution(4684970948886181437)
XLA Ops:
  0.6 8.4 %project.1.kv_ref = bf16[4,512,256]{2,1,0:T(8,128)(2,1)S(1)} custom-call(bf16[512,4096]{1,0:T(8,128)(2,1)} %bitcast.37, bf16[4,4096,256]{2,1,0:T(8,128)(2,1)} %refs_2_.1), custom_call_target="tpu_custom_call" | custom-call | tf_op jit(solution)/shard_map/project/pallas_call | solution.py:61
  9.2 1.6 %constant_dynamic-slice_fusion = (bf16[4,8,1,16,4,128]{5,4,3,2,1,0:T(4,128)(2,1)S(1)}, bf16[4,8,1,16,4,128]{5,4,3,2,1,0:T(4,128)(2,1)S(1)}) fusion(bf16[4,8,2,16,4,128]{5,4,3,2,1,0:T(4,128)(2,1)S(1)} %bitcast.40, s32[]{:T(128)S(6)} %select_n.87, bf16[4,8,2,16,4,128]{5,4,3,2,1,0:T(4,128)(2,1)} %bitcast.41), kind=kLoop, calls=%fused_computation.7 | loop fusion | bytes 2097156 | tf_op jit(solution)/shard_map/jit(dynamic_index_in_dim)/dynamic_slice | solution.py:435
  11.0 1.1 pad_maximum_fusion
  12.1 4.7 %all-to-all-start = ((bf16[4,2,4,128,128]{4,3,2,1,0:T(8,128)(2,1)}), bf16[4,2,4,128,128]{4,3,2,1,0:T(8,128)(2,1)S(1)}, u32[]{:S(2)}, u32[]{:S(2)}) async-start(bf16[4,2,4,128,128]{4,3,2,1,0:T(8,128)(2,1)} %pad_maximum_fusion), calls=%async_computation | async-start | bytes 2097152 | tf_op jit(solution)/shard_map/all_to_all | solution.py:429
  16.9 13.6 %all-to-all-done.mine = bf16[4,2,4,128,128]{4,3,2,1,0:T(8,128)(2,1)S(1)} async-done(((bf16[4,2,4,128,128]{4,3,2,1,0:T(8,128)(2,1)}), bf16[4,2,4,128,128]{4,3,2,1,0:T(8,128)(2,1)S(1)}, u32[]{:S(2)}, u32[]{:S(2)}) %all-to-all-start) | async-done | bytes 1048608 | tf_op jit(solution)/shard_map/all_to_all | solution.py:429
  30.4 2.2 %forward.1 = f32[8,4,8,128]{3,2,1,0:T(8,128)S(1)} custom-call(s32[12]{0:T(128)S(1)} %stack.84.scalars, s32[4]{0:T(128)S(1)} %copy-done.2, s32[4]{0:T(128)S(1)} %copy-done.3, bf16[4,2,4,128,128]{4,3,2,1,0:T(8,128)(2,1)S(1)} %all-to-all-done.mine, bf16[4,512,256]{2,1,0:T(8,128)(2,1)S(1)} %project.1.kv_ref, bf16[4,512,256]{2,1,0:T(8,128)(2,1)S(1)} %collective-permute-done.mate_ref), custom_call_target="tpu_custom_call" | custom-call | tf_op jit(solution)/shard_map/forward/pallas_call | solution.py:119
  32.6 10.8 %all_to_all.20.stat_ref = f32[8,4,8,128]{3,2,1,0:T(8,128)S(1)} all-to-all(f32[8,4,8,128]{3,2,1,0:T(8,128)S(1)} %forward.1), channel_id=1, replica_groups={{0,8,16,24,32,40,48,56},{4,12,20,28,36,44,52,60},{1,9,17,25,33,41,49,57..., dimensions={0} | all-to-all | bytes 262144 | tf_op jit(solution)/shard_map/all_to_all | solution.py:444
  43.4 3.0 %shard_map.86 = (bf16[4,2,4,2,16,128]{5,4,3,2,1,0:T(8,128)(2,1)S(1)}, bf16[4,2,4,2,16,128]{5,4,3,2,1,0:T(8,128)(2,1)S(1)}, bf16[4,256,256]{2,1,0:T(8,128)(2,1)S(1)}, bf16[4,256,256]{2,1,0:T(8,128)(2,1)S(1)}) custom-call(s32[12]{0:T(128)S(1)} %stack.84.scalars, s32[4]{0:T(128)S(1)} %copy-done.2, s32[4]{0:T(128)S(1)} %copy-done.3, ...), custom_call_target="tpu_custom_call" | custom-call | tf_op jit(solution)/shard_map/pallas_call | solution.py:203
  46.4 0.7 copy-done.4
  47.1 3.4 %shard_map.85 = (bf16[4,2,4,2,16,128]{5,4,3,2,1,0:T(8,128)(2,1)S(1)}, bf16[4,2,4,2,16,128]{5,4,3,2,1,0:T(8,128)(2,1)S(1)}, bf16[4,256,256]{2,1,0:T(8,128)(2,1)S(...) custom-call(s32[12]{0:T(128)S(1)} %stack.84.scalars, s32[4]{0:T(128)S(1)} %copy-done.2, s32[4]{0:T(128)S(1)} %copy-done.3, ...), custom_call_target="tpu_custom_call" | custom-call | tf_op jit(solution)/shard_map/pallas_call | solution.py:203
  50.5 0.7 copy-done.5
  51.7 0.7 shard_map.90
  52.5 2.1 %collective-permute-start.14 = (bf16[128,1024]{1,0:T(8,128)(2,1)S(1)}, bf16[128,1024]{1,0:T(8,128)(2,1)S(1)}, u32[]{:S(2)}, u32[]{:S(2)}) collective-permute-start(bf16[128,1024]{1,0:T(8,128)(2,1)S(1)} %get-tuple-element.65), channel_id=1, source_target_pairs={{0,64},{64,128},{128,192},{192,0},{1,65},{65,129},{129,193},{193,1... | collective-permute-start | bytes 786440 | tf_op jit(solution)/shard_map/ppermute | solution.py:423
  54.6 0.7 shard_map.89
  55.4 3.3 %collective-permute-start.10 = (bf16[128,1024]{1,0:T(8,128)(2,1)S(1)}, bf16[128,1024]{1,0:T(8,128)(2,1)S(1)}, u32[]{:S(2)}, u32[]{:S(2)}) collective-permute-start(bf16[128,1024]{1,0:T(8,128)(2,1)S(1)} %get-tuple-element.59), channel_id=1, source_target_pairs={{0,64},{64,128},{128,192},{192,0},{1,65},{65,129},{129,193},{193,1... | collective-permute-start | bytes 786440 | tf_op jit(solution)/shard_map/ppermute | solution.py:423
  58.7 2.4 %near.1 = (bf16[128,1024]{1,0:T(8,128)(2,1)S(1)}, bf16[384,1024]{1,0:T(8,128)(2,1)S(1)}, bf16[128,1024]{1,0:T(8,128)(2,1)S(1)}, bf16[384,1024]{1,0:T(8,128)(2,1)S(1)}) custom-call(bf16[4,256,256]{2,1,0:T(8,128)(2,1)S(1)} %get-tuple-element.53.refs_0_, bf16[4,256,256]{2,1,0:T(8,128)(2,1)S(1)} %get-tuple-element.56.refs_1_, ...), custom_call_target="tpu_custom_call" | custom-call | tf_op jit(solution)/shard_map/near/pallas_call | solution.py:254
  61.1 0.7 collective-permute-done.14.refs_1_
  61.7 3.3 %collective-permute-done.15.refs_3_ = bf16[128,1024]{1,0:T(8,128)(2,1)S(1)} collective-permute-done((bf16[128,1024]{1,0:T(8,128)(2,1)S(1)}, bf16[128,1024]{1,0:T(8,128)(2,1)S(1)}, u32[]{:S(2)}, u32[]{:S(2)}) %collective-permute-start.15) | collective-permute-done | bytes 262176 | tf_op jit(solution)/shard_map/ppermute | solution.py:426
  65.0 1.4 collective-permute-done.10.refs_0_
  66.4 3.0 %collective-permute-done.11.refs_1_.refs_2_ = bf16[128,1024]{1,0:T(8,128)(2,1)S(1)} collective-permute-done((bf16[128,1024]{1,0:T(8,128)(2,1)S(1)}, bf16[128,1024]{1,0:T(8,128)(2,1)S(1)}, u32[]{:S(2)}, u32[]{:S(2)}) %collective-permute-start.11) | collective-permute-done | bytes 262176 | tf_op jit(solution)/shard_map/ppermute | solution.py:426
  69.4 1.3 shard_map.93
  71.0 1.7 %collective-permute-start.17 = (bf16[384,1024]{1,0:T(8,128)(2,1)}, bf16[384,1024]{1,0:T(8,128)(2,1)S(1)}, u32[]{:S(2)}, u32[]{:S(2)}) collective-permute-start(bf16[384,1024]{1,0:T(8,128)(2,1)} %get-tuple-element.68), channel_id=1, source_target_pairs={{0,192},{64,0},{128,64},{192,128},{1,193},{65,1},{129,65},{193,129... | collective-permute-start | bytes 2359304 | tf_op jit(solution)/shard_map/ppermute | solution.py:426
  72.8 1.6 %collective-permute-start.12 = (bf16[128,1024]{1,0:T(8,128)(2,1)S(1)}, bf16[128,1024]{1,0:T(8,128)(2,1)S(1)}, u32[]{:S(2)}, u32[]{:S(2)}) collective-permute-start(bf16[128,1024]{1,0:T(8,128)(2,1)S(1)} %get-tuple-element.61), channel_id=1, source_target_pairs={{0,64},{64,128},{128,192},{192,0},{1,65},{65,129},{129,193},{193,1... | collective-permute-start | bytes 786440 | tf_op jit(solution)/shard_map/ppermute | solution.py:423
  74.4 0.5 collective-permute-start.13
  74.9 3.4 %here.1.own = bf16[512,1024]{1,0:T(8,128)(2,1)S(1)} custom-call(s32[12]{0:T(128)S(1)} %stack.84.scalars, bf16[4,256,256]{2,1,0:T(8,128)(2,1)S(1)} %get-tuple-element.53.refs_0_, bf16[4,256,256]{2,1,0:T(8,128)(2,1)S(1)} %get-tuple-element.56.refs_1_, bf16[4,4096,256]{2,1,0:T(8,128)(2,1)} %refs_2_.1), custom_call_target="tpu_custom_call" | custom-call | tf_op jit(solution)/shard_map/here/pallas_call | solution.py:279
  78.4 16.5 %collective-permute-done.12.from_down = bf16[128,1024]{1,0:T(8,128)(2,1)S(1)} collective-permute-done((bf16[128,1024]{1,0:T(8,128)(2,1)S(1)}, bf16[128,1024]{1,0:T(8,128)(2,1)S(1)}, u32[]{:S(2)}, u32[]{:S(2)}) %collective-permute-start.12) | collective-permute-done | bytes 262176 | tf_op jit(solution)/shard_map/ppermute | solution.py:423
  94.9 1.5 collective-permute-done.13.from_up
  96.4 0.8 shard_map.92
  97.2 7.6 %all-to-all-start.2 = ((bf16[4,128,256]{2,1,0:T(8,128)(2,1)}), bf16[4,128,256]{2,1,0:T(8,128)(2,1)S(1)}, u32[]{:S(2)}, u32[]{:S(2)}) async-start(bf16[4,128,256]{2,1,0:T(8,128)(2,1)} %shard_map.92), calls=%async_computation.2 | async-start | bytes 524288 | tf_op jit(solution)/shard_map/all_to_all | solution.py:429
  104.7 0.7 collective-permute-start.2
  105.5 1.3 collective-permute-start.1
  106.8 1.2 shard_map.94
  108.0 6.7 %all-to-all-done.2.refs_0_ = bf16[4,128,256]{2,1,0:T(8,128)(2,1)S(1)} async-done(((bf16[4,128,256]{2,1,0:T(8,128)(2,1)}), bf16[4,128,256]{2,1,0:T(8,128)(2,1)S(1)}, u32[]{:S(2)}, u32[]{:S(2)}) %all-to-all-start.2) | async-done | bytes 262176 | tf_op jit(solution)/shard_map/all_to_all | solution.py:429
  114.7 3.5 %all-to-all-start.3 = ((bf16[4,384,256]{2,1,0:T(8,128)(2,1)}), bf16[4,384,256]{2,1,0:T(8,128)(2,1)S(1)}, u32[]{:S(2)}, u32[]{:S(2)}) async-start(bf16[4,384,256]{2,1,0:T(8,128)(2,1)} %shard_map.94), calls=%async_computation.3 | async-start | bytes 1572864 | tf_op jit(solution)/shard_map/all_to_all | solution.py:429
  118.2 1.2 shard_map.87
  119.4 0.7 collective-permute-start.3
  120.1 18.9 %collective-permute-done.3.refs_1_ = bf16[2,2,4,4,16,128]{5,4,3,2,1,0:T(8,128)(2,1)S(1)} collective-permute-done((bf16[2,2,4,4,16,128]{5,4,3,2,1,0:T(8,128)(2,1)S(1)}, bf16[2,2,4,4,16,128]{5,4,3,2,1,0:T(8,128)(2,1)S(1)}, u32[]{:S(2)}, u32[]{:S(2)}) %collective-permute-start.3) | collective-permute-done | bytes 262176 | tf_op jit(solution)/shard_map/ppermute | solution.py:476
  139.1 0.9 collective-permute-start.4
  140.0 5.6 %collective-permute-done.4.came = bf16[1,2,4,4,16,128]{5,4,3,2,1,0:T(8,128)(2,1)S(1)} collective-permute-done((bf16[1,2,4,4,16,128]{5,4,3,2,1,0:T(8,128)(2,1)S(1)}, bf16[1,2,4,4,16,128]{5,4,3,2,1,0:T(8,128)(2,1)S(1)}, u32[]{:S(2)}, u32[]{:S(2)}) %collective-permute-start.4) | collective-permute-done | bytes 131104 | tf_op jit(solution)/shard_map/ppermute | solution.py:476
  145.6 0.6 deal.1
  146.2 0.7 collective-permute-start.5
  146.9 1.4 collective-permute-start.6
  148.3 1.9 %collective-permute-done.5 = bf16[2,4,16,128]{3,2,1,0:T(8,128)(2,1)S(1)} collective-permute-done((bf16[2,4,16,128]{3,2,1,0:T(8,128)(2,1)S(1)}, bf16[2,4,16,128]{3,2,1,0:T(8,128)(2,1)S(1)}, u32[]{:S(2)}, u32[]{:S(2)}) %collective-permute-start.5) | collective-permute-done | bytes 32800 | tf_op jit(solution)/shard_map/ppermute | solution.py:423
  150.2 2.1 %collective-permute-done.6 = bf16[2,4,16,128]{3,2,1,0:T(8,128)(2,1)S(1)} collective-permute-done((bf16[2,4,16,128]{3,2,1,0:T(8,128)(2,1)S(1)}, bf16[2,4,16,128]{3,2,1,0:T(8,128)(2,1)S(1)}, u32[]{:S(2)}, u32[]{:S(2)}) %collective-permute-start.6) | collective-permute-done | bytes 32800 | tf_op jit(solution)/shard_map/ppermute | solution.py:479
  152.3 1.1 collective-permute-done.7
  153.5 0.7 copy.14
  154.1 0.7 copy.13
  154.8 0.8 finish.1
  (36 shorter events, 1.5 us)
Async XLA Ops:
  0.6 8.5 %copy-start.6 = (bf16[1,4,256,4,128]{4,3,2,1,0:T(4,128)(2,1)S(1)}, bf16[1,4,256,4,128]{4,3,2,1,0:T(4,128)(2,1)}, u32[]{:S(2)}) copy-start(bf16[1,4,256,4,128]{4,3,2,1,0:T(4,128)(2,1)} %param.9) | copy-start | bytes 3145732
  9.0 21.4 %copy-start.2 = (s32[4]{0:T(128)S(1)}, s32[4]{0:T(128)}, u32[]{:S(2)}) copy-start(s32[4]{0:T(128)} %src_len.5) | copy-start | bytes 52
  9.0 21.4 %copy-start.3 = (s32[4]{0:T(128)S(1)}, s32[4]{0:T(128)}, u32[]{:S(2)}) copy-start(s32[4]{0:T(128)} %tgt_len.5) | copy-start | bytes 52
  9.0 21.4 %collective-permute-start = (bf16[4,512,256]{2,1,0:T(8,128)(2,1)S(1)}, bf16[4,512,256]{2,1,0:T(8,128)(2,1)S(1)}, u32[]{:S(2)}, u32[]{:S(2)}) collective-permute-start(bf16[4,512,256]{2,1,0:T(8,128)(2,1)S(1)} %project.1.kv_ref), channel_id=1, source_target_pairs={{0,4},{4,0},{8,12},{12,8},{16,20},{20,16},{24,28},{28,24},{32,36},... | collective-permute-start | bytes 3145736 | tf_op jit(solution)/shard_map/ppermute | solution.py:440
  12.1 18.3 %all-to-all-start = ((bf16[4,2,4,128,128]{4,3,2,1,0:T(8,128)(2,1)}), bf16[4,2,4,128,128]{4,3,2,1,0:T(8,128)(2,1)S(1)}, u32[]{:S(2)}, u32[]{:S(2)}) async-start(bf16[4,2,4,128,128]{4,3,2,1,0:T(8,128)(2,1)} %pad_maximum_fusion), calls=%async_computation | async-start | bytes 2097152 | tf_op jit(solution)/shard_map/all_to_all | solution.py:429
  46.4 0.7 copy-start.4
  47.1 4.7 %collective-permute-start.9 = (bf16[4,256,256]{2,1,0:T(8,128)(2,1)S(1)}, bf16[4,256,256]{2,1,0:T(8,128)(2,1)S(1)}, u32[]{:S(2)}, u32[]{:S(2)}) collective-permute-start(bf16[4,256,256]{2,1,0:T(8,128)(2,1)S(1)} %get-tuple-element.55), channel_id=1, source_target_pairs={{0,4},{4,0},{8,12},{12,8},{16,20},{20,16},{24,28},{28,24},{32,36},... | collective-permute-start | bytes 1572872 | tf_op jit(solution)/shard_map/ppermute | solution.py:454
  50.5 0.7 copy-start.5
  51.2 4.2 %copy-start = (bf16[4,2,4,2,16,128]{5,4,3,2,1,0:T(8,128)(2,1)}, bf16[4,2,4,2,16,128]{5,4,3,2,1,0:T(8,128)(2,1)S(1)}, u32[]{:S(2)}) copy-start(bf16[4,2,4,2,16,128]{5,4,3,2,1,0:T(8,128)(2,1)S(1)} %get-tuple-element.38.refs_0_) | copy-start | bytes 786436
  51.2 3.4 %collective-permute-start.8 = (bf16[4,256,256]{2,1,0:T(8,128)(2,1)S(1)}, bf16[4,256,256]{2,1,0:T(8,128)(2,1)S(1)}, u32[]{:S(2)}, u32[]{:S(2)}) collective-permute-start(bf16[4,256,256]{2,1,0:T(8,128)(2,1)S(1)} %get-tuple-element.51), channel_id=1, source_target_pairs={{0,4},{4,0},{8,12},{12,8},{16,20},{20,16},{24,28},{28,24},{32,36},... | collective-permute-start | bytes 1572872 | tf_op jit(solution)/shard_map/ppermute | solution.py:454
  52.5 9.3 %collective-permute-start.14 = (bf16[128,1024]{1,0:T(8,128)(2,1)S(1)}, bf16[128,1024]{1,0:T(8,128)(2,1)S(1)}, u32[]{:S(2)}, u32[]{:S(2)}) collective-permute-start(bf16[128,1024]{1,0:T(8,128)(2,1)S(1)} %get-tuple-element.65), channel_id=1, source_target_pairs={{0,64},{64,128},{128,192},{192,0},{1,65},{65,129},{129,193},{193,1... | collective-permute-start | bytes 786440 | tf_op jit(solution)/shard_map/ppermute | solution.py:423
  54.6 10.4 %collective-permute-start.15 = (bf16[128,1024]{1,0:T(8,128)(2,1)S(1)}, bf16[128,1024]{1,0:T(8,128)(2,1)S(1)}, u32[]{:S(2)}, u32[]{:S(2)}) collective-permute-start(bf16[128,1024]{1,0:T(8,128)(2,1)S(1)} %get-tuple-element.66), channel_id=1, source_target_pairs={{0,192},{64,0},{128,64},{192,128},{1,193},{65,1},{129,65},{193,129... | collective-permute-start | bytes 786440 | tf_op jit(solution)/shard_map/ppermute | solution.py:426
  55.4 11.0 %collective-permute-start.10 = (bf16[128,1024]{1,0:T(8,128)(2,1)S(1)}, bf16[128,1024]{1,0:T(8,128)(2,1)S(1)}, u32[]{:S(2)}, u32[]{:S(2)}) collective-permute-start(bf16[128,1024]{1,0:T(8,128)(2,1)S(1)} %get-tuple-element.59), channel_id=1, source_target_pairs={{0,64},{64,128},{128,192},{192,0},{1,65},{65,129},{129,193},{193,1... | collective-permute-start | bytes 786440 | tf_op jit(solution)/shard_map/ppermute | solution.py:423
  58.7 10.7 %collective-permute-start.11 = (bf16[128,1024]{1,0:T(8,128)(2,1)S(1)}, bf16[128,1024]{1,0:T(8,128)(2,1)S(1)}, u32[]{:S(2)}, u32[]{:S(2)}) collective-permute-start(bf16[128,1024]{1,0:T(8,128)(2,1)S(1)} %get-tuple-element.60), channel_id=1, source_target_pairs={{0,192},{64,0},{128,64},{192,128},{1,193},{65,1},{129,65},{193,129... | collective-permute-start | bytes 786440 | tf_op jit(solution)/shard_map/ppermute | solution.py:426
  70.7 36.0 %collective-permute-start.16 = (bf16[384,1024]{1,0:T(8,128)(2,1)}, bf16[384,1024]{1,0:T(8,128)(2,1)S(1)}, u32[]{:S(2)}, u32[]{:S(2)}) collective-permute-start(bf16[384,1024]{1,0:T(8,128)(2,1)} %get-tuple-element.67), channel_id=1, source_target_pairs={{0,64},{64,128},{128,192},{192,0},{1,65},{65,129},{129,193},{193,1... | collective-permute-start | bytes 2359304 | tf_op jit(solution)/shard_map/ppermute | solution.py:423
  71.0 35.8 %collective-permute-start.17 = (bf16[384,1024]{1,0:T(8,128)(2,1)}, bf16[384,1024]{1,0:T(8,128)(2,1)S(1)}, u32[]{:S(2)}, u32[]{:S(2)}) collective-permute-start(bf16[384,1024]{1,0:T(8,128)(2,1)} %get-tuple-element.68), channel_id=1, source_target_pairs={{0,192},{64,0},{128,64},{192,128},{1,193},{65,1},{129,65},{193,129... | collective-permute-start | bytes 2359304 | tf_op jit(solution)/shard_map/ppermute | solution.py:426
  72.8 22.0 %collective-permute-start.12 = (bf16[128,1024]{1,0:T(8,128)(2,1)S(1)}, bf16[128,1024]{1,0:T(8,128)(2,1)S(1)}, u32[]{:S(2)}, u32[]{:S(2)}) collective-permute-start(bf16[128,1024]{1,0:T(8,128)(2,1)S(1)} %get-tuple-element.61), channel_id=1, source_target_pairs={{0,64},{64,128},{128,192},{192,0},{1,65},{65,129},{129,193},{193,1... | collective-permute-start | bytes 786440 | tf_op jit(solution)/shard_map/ppermute | solution.py:423
  74.4 22.0 %collective-permute-start.13 = (bf16[128,1024]{1,0:T(8,128)(2,1)S(1)}, bf16[128,1024]{1,0:T(8,128)(2,1)S(1)}, u32[]{:S(2)}, u32[]{:S(2)}) collective-permute-start(bf16[128,1024]{1,0:T(8,128)(2,1)S(1)} %get-tuple-element.62), channel_id=1, source_target_pairs={{0,192},{64,0},{128,64},{192,128},{1,193},{65,1},{129,65},{193,129... | collective-permute-start | bytes 786440 | tf_op jit(solution)/shard_map/ppermute | solution.py:426
  78.4 39.8 %copy-start.1 = (bf16[4,2,4,2,16,128]{5,4,3,2,1,0:T(8,128)(2,1)S(1)}, bf16[4,2,4,2,16,128]{5,4,3,2,1,0:T(8,128)(2,1)}, u32[]{:S(2)}) copy-start(bf16[4,2,4,2,16,128]{5,4,3,2,1,0:T(8,128)(2,1)} %copy-done) | copy-start | bytes 786436
  97.2 17.5 %all-to-all-start.2 = ((bf16[4,128,256]{2,1,0:T(8,128)(2,1)}), bf16[4,128,256]{2,1,0:T(8,128)(2,1)S(1)}, u32[]{:S(2)}, u32[]{:S(2)}) async-start(bf16[4,128,256]{2,1,0:T(8,128)(2,1)} %shard_map.92), calls=%async_computation.2 | async-start | bytes 524288 | tf_op jit(solution)/shard_map/all_to_all | solution.py:429
  104.7 13.4 %collective-permute-start.2 = (bf16[4,2,4,2,16,128]{5,4,3,2,1,0:T(8,128)(2,1)}, bf16[4,2,4,2,16,128]{5,4,3,2,1,0:T(8,128)(2,1)}, u32[]{:S(2)}, u32[]{:S(2)}) collective-permute-start(bf16[4,2,4,2,16,128]{5,4,3,2,1,0:T(8,128)(2,1)} %copy-done.4), channel_id=1, source_target_pairs={{0,8},{4,12},{8,0},{12,4},{16,24},{20,28},{24,16},{28,20},{32,40},... | collective-permute-start | bytes 786440 | tf_op jit(solution)/shard_map/ppermute | solution.py:455
  105.5 12.7 %collective-permute-start.1 = (bf16[4,2,4,2,16,128]{5,4,3,2,1,0:T(8,128)(2,1)}, bf16[4,2,4,2,16,128]{5,4,3,2,1,0:T(8,128)(2,1)}, u32[]{:S(2)}, u32[]{:S(2)}) collective-permute-start(bf16[4,2,4,2,16,128]{5,4,3,2,1,0:T(8,128)(2,1)} %copy-done.5), channel_id=1, source_target_pairs={{0,8},{4,12},{8,0},{12,4},{16,24},{20,28},{24,16},{28,20},{32,40},... | collective-permute-start | bytes 786440 | tf_op jit(solution)/shard_map/ppermute | solution.py:455
  114.7 40.2 %all-to-all-start.3 = ((bf16[4,384,256]{2,1,0:T(8,128)(2,1)}), bf16[4,384,256]{2,1,0:T(8,128)(2,1)S(1)}, u32[]{:S(2)}, u32[]{:S(2)}) async-start(bf16[4,384,256]{2,1,0:T(8,128)(2,1)} %shard_map.94), calls=%async_computation.3 | async-start | bytes 1572864 | tf_op jit(solution)/shard_map/all_to_all | solution.py:429
  119.4 19.6 %collective-permute-start.3 = (bf16[2,2,4,4,16,128]{5,4,3,2,1,0:T(8,128)(2,1)S(1)}, bf16[2,2,4,4,16,128]{5,4,3,2,1,0:T(8,128)(2,1)S(1)}, u32[]{:S(2)}, u32[]{:S(2)}) collective-permute-start(bf16[2,2,4,4,16,128]{5,4,3,2,1,0:T(8,128)(2,1)S(1)} %get-tuple-element.43), channel_id=1, source_target_pairs={{0,32},{4,36},{8,40},{12,44},{16,48},{20,52},{24,56},{28,60},{32,0... | collective-permute-start | bytes 786440 | tf_op jit(solution)/shard_map/ppermute | solution.py:476
  139.1 6.6 %collective-permute-start.4 = (bf16[1,2,4,4,16,128]{5,4,3,2,1,0:T(8,128)(2,1)S(1)}, bf16[1,2,4,4,16,128]{5,4,3,2,1,0:T(8,128)(2,1)S(1)}, u32[]{:S(2)}, u32[]{:S(2)}) collective-permute-start(bf16[1,2,4,4,16,128]{5,4,3,2,1,0:T(8,128)(2,1)S(1)} %get-tuple-element.45), channel_id=1, source_target_pairs={{0,16},{4,20},{8,24},{12,28},{16,0},{20,4},{24,8},{28,12},{32,48},... | collective-permute-start | bytes 393224 | tf_op jit(solution)/shard_map/ppermute | solution.py:476
  146.2 4.0 %collective-permute-start.5 = (bf16[2,4,16,128]{3,2,1,0:T(8,128)(2,1)S(1)}, bf16[2,4,16,128]{3,2,1,0:T(8,128)(2,1)S(1)}, u32[]{:S(2)}, u32[]{:S(2)}) collective-permute-start(bf16[2,4,16,128]{3,2,1,0:T(8,128)(2,1)S(1)} %get-tuple-element.47), channel_id=1, source_target_pairs={{0,64},{64,128},{128,192},{192,0},{1,65},{65,129},{129,193},{193,1... | collective-permute-start | bytes 98312 | tf_op jit(solution)/shard_map/ppermute | solution.py:423
  146.9 5.4 %collective-permute-start.6 = (bf16[2,4,16,128]{3,2,1,0:T(8,128)(2,1)S(1)}, bf16[2,4,16,128]{3,2,1,0:T(8,128)(2,1)S(1)}, u32[]{:S(2)}, u32[]{:S(2)}) collective-permute-start(bf16[2,4,16,128]{3,2,1,0:T(8,128)(2,1)S(1)} %get-tuple-element.48), channel_id=1, source_target_pairs={{0,128},{64,192},{128,0},{192,64},{1,129},{65,193},{129,1},{193,65... | collective-permute-start | bytes 98312 | tf_op jit(solution)/shard_map/ppermute | solution.py:479
  148.2 5.1 %collective-permute-start.7 = (bf16[2,4,16,128]{3,2,1,0:T(8,128)(2,1)S(1)}, bf16[2,4,16,128]{3,2,1,0:T(8,128)(2,1)S(1)}, u32[]{:S(2)}, u32[]{:S(2)}) collective-permute-start(bf16[2,4,16,128]{3,2,1,0:T(8,128)(2,1)S(1)} %get-tuple-element.49), channel_id=1, source_target_pairs={{0,192},{64,0},{128,64},{192,128},{1,193},{65,1},{129,65},{193,129... | collective-permute-start | bytes 98312 | tf_op jit(solution)/shard_map/ppermute | solution.py:426
